TPU v7x, 32 devices: a whole 2x2x4 slice. The times are simulated.
32 devices in a mesh: dp: 4 (over z), head: 4 (over x, core), tensor: 2 (over y).
Axes of the slice: x: 2, y: 2, z: 4, core: 2. Of those that a mesh axis runs over, the one named last changes fastest.
Arguments:
- tokens: bfloat16 [8192, 768], P(('dp', 'head', 'tensor')), may hold values from -6 to 6
- seg_ids: int32 [4, 2048], P('dp'), may hold values from 0 to 2, never falling along the last dimension, each value on 1 to 1024 neighbouring positions
- norm1_gain: float32 [768], replicated, may hold values from 0.5 to 1.5
- norm1_bias: float32 [768], replicated, may hold values from -3 to 3
- norm2_gain: float32 [768], replicated, may hold values from 0.5 to 1.5
- norm2_bias: float32 [768], replicated, may hold values from -3 to 3
- q_weight: bfloat16 [768, 768], P('dp', ('head', 'tensor')), may hold values from -0.21875 to 0.21875
- k_weight: bfloat16 [768, 768], P('dp', ('head', 'tensor')), may hold values from -0.21875 to 0.21875
- v_weight: bfloat16 [768, 768], P('dp', ('head', 'tensor')), may hold values from -0.21875 to 0.21875
- out_weight: bfloat16 [768, 768], P('dp', ('head', 'tensor')), may hold values from -0.21875 to 0.21875
- up_weight: bfloat16 [768, 3072], P('dp', ('head', 'tensor')), may hold values from -0.21875 to 0.21875
- down_weight: bfloat16 [768, 3072], P('dp', ('head', 'tensor')), may hold values from -0.109375 to 0.109375
- shift_weight: float32 [4, 768], P(None, ('head', 'tensor')), may hold values from -3 to 3
- decay_rate: float32 [64, 768], P(None, ('head', 'tensor')), may hold values from 0.002 to 0.5
- in_coef: float32 [64, 768], P(None, ('head', 'tensor')), may hold values from -0.75 to 0.75
- out_coef: float32 [64, 768], P(None, ('head', 'tensor')), may hold values from -0.75 to 0.75
- skip_coef: float32 [768], P(('head', 'tensor')), may hold values from -4 to 4
- cotangent: bfloat16 [8192, 768], P(('dp', 'head', 'tensor')), may hold values from -6 to 6
Outputs:
- block_out: bfloat16 [8192, 768], P(('dp', 'head', 'tensor'))
- grad_tokens: float32 [8192, 768], P(('dp', 'head', 'tensor'))
- grad_norm1_gain: float32 [768], replicated
- grad_norm1_bias: float32 [768], replicated
- grad_norm2_gain: float32 [768], replicated
- grad_norm2_bias: float32 [768], replicated
- grad_q_weight: float32 [768, 768], P('dp', ('head', 'tensor'))
- grad_k_weight: float32 [768, 768], P('dp', ('head', 'tensor'))
- grad_v_weight: float32 [768, 768], P('dp', ('head', 'tensor'))
- grad_out_weight: float32 [768, 768], P('dp', ('head', 'tensor'))
- grad_up_weight: float32 [768, 3072], P('dp', ('head', 'tensor'))
- grad_down_weight: float32 [768, 3072], P('dp', ('head', 'tensor'))
- grad_shift_weight: float32 [4, 768], P(None, ('head', 'tensor'))
- grad_decay_rate: float32 [64, 768], P(None, ('head', 'tensor'))
- grad_in_coef: float32 [64, 768], P(None, ('head', 'tensor'))
- grad_out_coef: float32 [64, 768], P(None, ('head', 'tensor'))
- grad_skip_coef: float32 [768], P(('head', 'tensor'))
Inputs may be any that keep to these rules, and one draw needn't show every extreme that they name: `seg_ids`: along a row the sequence numbers never fall; each sequence has 1 to 1024 tokens and one has exactly 1024.
All inputs are finite; a program needn't handle non-finite values.
Results may differ from a plain program's by a relative error of at most 0.012.
The roundings to bfloat16 on the way count: a program that leaves them out, or rounds other values in their place, can miss the bound.
Values may be sent and summed in bfloat16 or wider, within the bound.
A program may use at most 128 MiB of HBM per device.

v0:
```python
import jax
import jax.numpy as jnp
from jax import lax
from jax.sharding import PartitionSpec as P

SHIFT = 4
BLOCK = 128


def layer_norm(values, gain, bias):
    centre = jnp.mean(values, axis=-1, keepdims=True)
    centred = values - centre
    spread = jnp.mean(centred * centred, axis=-1, keepdims=True)
    return centred * lax.rsqrt(spread + 1e-05) * gain + bias


def exact_gelu(values):
    return jax.nn.gelu(values, approximate=False)


def mixer_core(q_proj, k_proj, v_proj, shift_w, rate, in_b, out_c, skip, segment):
    length, chans = k_proj.shape
    shifted = shift_w[0] * k_proj
    for lag_step in range(1, SHIFT):
        same_seq = (segment[lag_step:] == segment[:-lag_step]).astype(k_proj.dtype)
        prior = k_proj[:-lag_step] * same_seq[:, None]
        prior = jnp.concatenate([jnp.zeros((lag_step, chans), k_proj.dtype), prior], axis=0)
        shifted = shifted + shift_w[lag_step] * prior
    drive = shifted * v_proj
    lag_pos = jnp.arange(BLOCK).astype(k_proj.dtype)
    powers = jnp.exp(-rate[None] * lag_pos[:, None, None])
    kernel = jnp.einsum("lnc,nc->lc", powers, in_b * out_c, precision=lax.Precision.HIGHEST)
    places = jnp.arange(BLOCK)
    offset = places[:, None] - places[None, :]
    toeplitz = kernel[jnp.clip(offset, 0, BLOCK - 1)]
    causal = offset >= 0
    ahead = powers * jnp.exp(-rate)[None]
    behind = powers[::-1]
    across = jnp.exp(-rate * BLOCK)
    blocks_in = drive.reshape(length // BLOCK, BLOCK, chans)
    blocks_seg = segment.reshape(length // BLOCK, BLOCK)

    def advance(carry, item):
        state, last_seg = carry
        part, seg_part = item
        same_mask = (causal & (seg_part[:, None] == seg_part[None, :])).astype(part.dtype)
        inner = jnp.einsum(
            "abc,ab,bc->ac", toeplitz, same_mask, part, precision=lax.Precision.HIGHEST
        )
        live = (seg_part == last_seg).astype(part.dtype)
        outer = (
            jnp.einsum("pnc,nc->pc", ahead, out_c * state, precision=lax.Precision.HIGHEST)
            * live[:, None]
        )
        end_seg = seg_part[BLOCK - 1]
        keep_mask = (seg_part == end_seg).astype(part.dtype)
        fresh = (
            jnp.einsum(
                "pnc,pc->nc", behind, part * keep_mask[:, None], precision=lax.Precision.HIGHEST
            )
            * in_b
        )
        carry_on = (end_seg == last_seg).astype(part.dtype)
        return ((fresh + across * state * carry_on, end_seg), inner + outer)

    start_state = (jnp.zeros_like(rate), jnp.array(-1, jnp.int32))
    _, outputs = lax.scan(jax.checkpoint(advance), start_state, (blocks_in, blocks_seg))
    return q_proj * (outputs.reshape(length, chans) + skip * drive)


def right_product(left, right):
    return lax.dot_general(
        left, right, (((1,), (1,)), ((), ())), preferred_element_type=jnp.float32
    )


def token_product(left, right):
    return lax.dot_general(
        left, right, (((0,), (0,)), ((), ())), preferred_element_type=jnp.float32
    )


def on_device(
    tokens,
    seg_ids,
    norm1_gain,
    norm1_bias,
    norm2_gain,
    norm2_bias,
    q_weight,
    k_weight,
    v_weight,
    out_weight,
    up_weight,
    down_weight,
    shift_weight,
    decay_rate,
    in_coef,
    out_coef,
    skip_coef,
    cotangent,
):
    w_query, w_keys, w_values, w_output, w_up, w_down = (
        lax.all_gather(q_weight, "dp", axis=0, tiled=True),
        lax.all_gather(k_weight, "dp", axis=0, tiled=True),
        lax.all_gather(v_weight, "dp", axis=0, tiled=True),
        lax.all_gather(out_weight, "dp", axis=0, tiled=True),
        lax.all_gather(up_weight, "dp", axis=0, tiled=True),
        lax.all_gather(down_weight, "dp", axis=0, tiled=True),
    )
    chans = w_query.shape[1]
    w_joint = jnp.concatenate([w_query, w_keys, w_values], axis=1)
    x_own = tokens.astype(jnp.float32)
    xn_one_f, norm1_back = jax.vjp(layer_norm, x_own, norm1_gain, norm1_bias)
    xn_one = lax.all_gather(xn_one_f.astype(jnp.bfloat16), ("head", "tensor"), axis=0, tiled=True)
    joint_proj = jnp.dot(xn_one, w_joint, preferred_element_type=jnp.float32)
    q_proj = joint_proj[:, :chans]
    k_proj = joint_proj[:, chans : 2 * chans]
    v_proj = joint_proj[:, 2 * chans :]
    segment = seg_ids[0]

    def mixer_local(q_in, k_in, v_in, shift_w, rate, in_b, out_c, skip):
        return mixer_core(q_in, k_in, v_in, shift_w, rate, in_b, out_c, skip, segment)

    mixed_f, mixer_back = jax.vjp(
        mixer_local, q_proj, k_proj, v_proj, shift_weight, decay_rate, in_coef, out_coef, skip_coef
    )
    mixed = mixed_f.astype(jnp.bfloat16)
    mix_own = lax.psum_scatter(
        right_product(mixed, w_output), ("head", "tensor"), scatter_dimension=0, tiled=True
    )
    hidden_own = x_own + mix_own
    xn_two_f, norm2_back = jax.vjp(layer_norm, hidden_own, norm2_gain, norm2_bias)
    xn_two_own = xn_two_f.astype(jnp.bfloat16)
    xn_two = lax.all_gather(xn_two_own, ("head", "tensor"), axis=0, tiled=True)
    pre_act = jnp.dot(xn_two, w_up, preferred_element_type=jnp.float32)
    act_f, gelu_back = jax.vjp(exact_gelu, pre_act)
    act_out = act_f.astype(jnp.bfloat16)
    mlp_own = lax.psum_scatter(
        right_product(act_out, w_down), ("head", "tensor"), scatter_dimension=0, tiled=True
    )
    result_own = hidden_own + mlp_own
    cot_all = lax.all_gather(cotangent, ("head", "tensor"), axis=0, tiled=True)
    grad_down = token_product(cot_all, act_out)
    grad_act = jnp.dot(cot_all, w_down, preferred_element_type=jnp.float32)
    grad_pre = gelu_back(grad_act)[0].astype(jnp.bfloat16)
    grad_up = token_product(xn_two, grad_pre)
    grad_xn_two = lax.psum_scatter(
        right_product(grad_pre, w_up), ("head", "tensor"), scatter_dimension=0, tiled=True
    )
    grad_hidden_norm, grad_gain_two, grad_bias_two = norm2_back(grad_xn_two)
    grad_hidden = cotangent.astype(jnp.float32) + grad_hidden_norm
    grad_mix = lax.all_gather(
        grad_hidden.astype(jnp.bfloat16), ("head", "tensor"), axis=0, tiled=True
    )
    grad_output_w = token_product(grad_mix, mixed)
    grad_mixed = jnp.dot(grad_mix, w_output, preferred_element_type=jnp.float32)
    grad_query, grad_keys, grad_values, grad_shift, grad_rate, grad_in_b, grad_out_c, grad_skip = (
        mixer_back(grad_mixed)
    )
    grad_joint = jnp.concatenate([grad_query, grad_keys, grad_values], axis=1).astype(jnp.bfloat16)
    grad_w_joint = token_product(xn_one, grad_joint)
    grad_xn_one = lax.psum_scatter(
        right_product(grad_joint, w_joint), ("head", "tensor"), scatter_dimension=0, tiled=True
    )
    grad_x_norm, grad_gain_one, grad_bias_one = norm1_back(grad_xn_one)
    grad_input = grad_hidden + grad_x_norm
    grad_wq = grad_w_joint[:, :chans]
    grad_wk = grad_w_joint[:, chans : 2 * chans]
    grad_wv = grad_w_joint[:, 2 * chans :]
    sum_wq, sum_wk, sum_wv, sum_wout, sum_wup, sum_wdown = (
        lax.psum_scatter(grad_wq, "dp", scatter_dimension=0, tiled=True),
        lax.psum_scatter(grad_wk, "dp", scatter_dimension=0, tiled=True),
        lax.psum_scatter(grad_wv, "dp", scatter_dimension=0, tiled=True),
        lax.psum_scatter(grad_output_w, "dp", scatter_dimension=0, tiled=True),
        lax.psum_scatter(grad_up, "dp", scatter_dimension=0, tiled=True),
        lax.psum_scatter(grad_down, "dp", scatter_dimension=0, tiled=True),
    )
    sum_shift, sum_rate, sum_in_b, sum_out_c, sum_skip = lax.psum(
        (grad_shift, grad_rate, grad_in_b, grad_out_c, grad_skip), "dp"
    )
    sum_gain_one, sum_bias_one, sum_gain_two, sum_bias_two = lax.psum(
        (grad_gain_one, grad_bias_one, grad_gain_two, grad_bias_two), ("dp", "head", "tensor")
    )
    return (
        result_own.astype(jnp.bfloat16),
        grad_input,
        sum_gain_one,
        sum_bias_one,
        sum_gain_two,
        sum_bias_two,
        sum_wq,
        sum_wk,
        sum_wv,
        sum_wout,
        sum_wup,
        sum_wdown,
        sum_shift,
        sum_rate,
        sum_in_b,
        sum_out_c,
        sum_skip,
    )


def solution(mesh):
    in_specs = (
        P(("dp", "head", "tensor"), None),
        P("dp", None),
        P(),
        P(),
        P(),
        P(),
        P("dp", ("head", "tensor")),
        P("dp", ("head", "tensor")),
        P("dp", ("head", "tensor")),
        P("dp", ("head", "tensor")),
        P("dp", ("head", "tensor")),
        P("dp", ("head", "tensor")),
        P(None, ("head", "tensor")),
        P(None, ("head", "tensor")),
        P(None, ("head", "tensor")),
        P(None, ("head", "tensor")),
        P(("head", "tensor")),
        P(("dp", "head", "tensor"), None),
    )
    out_specs = (
        P(("dp", "head", "tensor"), None),
        P(("dp", "head", "tensor"), None),
        P(),
        P(),
        P(),
        P(),
        P("dp", ("head", "tensor")),
        P("dp", ("head", "tensor")),
        P("dp", ("head", "tensor")),
        P("dp", ("head", "tensor")),
        P("dp", ("head", "tensor")),
        P("dp", ("head", "tensor")),
        P(None, ("head", "tensor")),
        P(None, ("head", "tensor")),
        P(None, ("head", "tensor")),
        P(None, ("head", "tensor")),
        P(("head", "tensor")),
    )
    return jax.shard_map(
        on_device, mesh=mesh, in_specs=in_specs, out_specs=out_specs, check_vma=False
    )
```

profile of v0, /device:TPU:0, one launch (start us, length us, event | category | flops | bytes accessed | tf_op | source)
XLA Modules:
  0.0 1561.6 jit_solution(3046614772982174814)
XLA Ops:
  22.2 54.5 %gather_fusion = f32[16384,96]{1,0:T(8,128)} fusion(f32[128,96]{1,0:T(8,128)S(1)} %bitcast.222, s32[16384]{0:T(1024)S(1)} %broadcast_clamp_fusion), kind=kCustom, calls=%fused_computation | custom fusion | bytes 12648448 | tf_op jit(solution)/shard_map/jvp()/gather | solution.py:35
  76.7 15.4 all_gather.31
  92.2 14.2 all_gather.32
  106.4 13.7 all_gather.33
  120.0 13.6 all_gather.34
  143.2 264.9 %while.48 = (s32[]{:T(128)}, f32[64,96]{1,0:T(8,128)S(1)}, s32[]{:T(128)}, f32[16,128,96]{2,1,0:T(8,128)}, f32[16,64,96]{2,1,0:T(8,128)}, /*index=5*/s32[16]{0:T...) while((s32[]{:T(128)}, f32[64,96]{1,0:T(8,128)S(1)}, ...), condition=%wide.region_3.4_spmd.clone, body=%wide.region_2.3_spmd.clone.sunk | while | flops 9568773 | bytes 10459934 | solution.py:67
  151.1 5.5 multiply_reduce_fusion.26
  167.7 5.5 multiply_reduce_fusion.26
  184.2 5.5 multiply_reduce_fusion.26
  200.8 5.5 multiply_reduce_fusion.26
  217.3 5.5 multiply_reduce_fusion.26
  233.9 5.5 multiply_reduce_fusion.26
  250.5 5.5 multiply_reduce_fusion.26
  267.0 5.5 multiply_reduce_fusion.26
  283.6 5.5 multiply_reduce_fusion.26
  300.1 5.5 multiply_reduce_fusion.26
  316.7 5.5 multiply_reduce_fusion.26
  416.5 63.3 %reduce-scatter.19.cloned.1.call-done = f32[256,768]{1,0:T(8,128)} async-done(((f32[2048,768]{1,0:T(8,128)}), f32[256,768]{1,0:T(8,128)}) %reduce-scatter.19.cloned.1.call-update) | async-done | bytes 786448 | tf_op jit(solution)/shard_map/reduce_scatter | solution.py:129
  483.7 18.3 %all_gather.36 = bf16[768,384]{1,0:T(8,128)(2,1)} all-gather(bf16[192,384]{1,0:T(8,128)(2,1)} %param.32), channel_id=1, replica_groups=mesh['dp'=4,'head'=4,'tensor'=2] {'dp'}, dimensions={0}, use_global_device_ids=true | all-gather | bytes 737280 | tf_op jit(solution)/shard_map/all_gather | solution.py:108
  502.0 17.0 %all_gather.37 = bf16[768,384]{1,0:T(8,128)(2,1)} all-gather(bf16[192,384]{1,0:T(8,128)(2,1)} %param.33), channel_id=1, replica_groups=mesh['dp'=4,'head'=4,'tensor'=2] {'dp'}, dimensions={0}, use_global_device_ids=true | all-gather | bytes 737280 | tf_op jit(solution)/shard_map/all_gather | solution.py:109
  524.4 25.4 %all-gather.9.cloned.1.call-done = bf16[2048,768]{1,0:T(8,128)(2,1)} async-done(((bf16[256,768]{1,0:T(8,128)(2,1)}), bf16[2048,768]{1,0:T(8,128)(2,1)}) %all-gather.9.cloned.1.call-update) | async-done | bytes 3145744 | tf_op jit(solution)/shard_map/all_gather | solution.py:143
  549.8 11.8 add_convert_fusion
  576.7 52.5 %reduce-scatter.23.cloned.1.call-done = f32[256,768]{1,0:T(8,128)} async-done(((f32[2048,768]{1,0:T(8,128)}), f32[256,768]{1,0:T(8,128)}) %reduce-scatter.23.cloned.1.call-update) | async-done | bytes 786448 | tf_op jit(solution)/shard_map/reduce_scatter | solution.py:148
  631.8 62.4 %reduce-scatter.21.cloned.1.call-done = f32[256,768]{1,0:T(8,128)} async-done(((f32[2048,768]{1,0:T(8,128)}), f32[256,768]{1,0:T(8,128)}) %reduce-scatter.21.cloned.1.call-update) | async-done | bytes 786448 | tf_op jit(solution)/shard_map/reduce_scatter | solution.py:139
  698.6 32.3 %all-gather.11.cloned.1.call-done = bf16[2048,768]{1,0:T(8,128)(2,1)} async-done(((bf16[256,768]{1,0:T(8,128)(2,1)}), bf16[2048,768]{1,0:T(8,128)(2,1)}) %all-gather.11.cloned.1.call-update) | async-done | bytes 3145744 | tf_op jit(solution)/shard_map/all_gather | solution.py:153
  738.3 547.5 %while.49 = (s32[]{:T(128)}, f32[128,128,96]{2,1,0:T(8,128)}, f32[64,96]{1,0:T(8,128)}, f32[128,64,96]{2,1,0:T(8,128)}, f32[128,64,96]{2,1,0:T(8,128)}, /*index=...) while((s32[]{:T(128)}, f32[128,128,96]{2,1,0:T(8,128)}, ...), condition=%wide.region_12.13_spmd.clone, body=%wide.region_11.12_spmd.clone.sunk | while | flops 22213124 | bytes 184844288 | solution.py:67
  1310.3 98.3 %scatter_custom_fusion = f32[128,96]{1,0:T(8,128)S(1)} fusion(s32[16384]{0:T(1024)S(1)} %fusion.43, f32[16384,96]{1,0:T(8,128)} %bitcast.224, f32[]{:T(128)} %constant.46.clone.1), kind=kCustom, calls=%fused_computation.140 | custom fusion | flops 1572864 | bytes 49664 | tf_op jit(solution)/shard_map/transpose(jvp())/scatter-add | solution.py:35
  1427.9 39.4 %all-reduce.10 = (f32[768]{0:T(1024)}, f32[768]{0:T(1024)}, f32[768]{0:T(1024)}, f32[768]{0:T(1024)}) all-reduce(f32[768]{0:T(1024)S(1)} %get-tuple-element.848, f32[768]{0:T(1024)S(1)} %get-tuple-element.855, f32[768]{0:T(1024)S(1)} %copy-done.86, ...), channel_id=1, replica_groups=mesh['dp'=4,'head'=4,'tensor'=2] {'dp','head','tensor'}, use_global_device_ids=true, to_apply=%region_17.18 | all-reduce | flops 3072 | bytes 24576 | tf_op jit(solution)/shard_map/psum | solution.py:182
  1469.8 13.2 reduce-scatter.27.cloned.1.call-done
  1483.1 21.7 %reduce-scatter.35.cloned.1.call-done = f32[192,96]{1,0:T(8,128)} async-done(((f32[768,96]{1,0:T(8,128)}), f32[192,96]{1,0:T(8,128)}) %reduce-scatter.35.cloned.1.call-update) | async-done | bytes 73744
  1504.8 21.7 %reduce-scatter.33.cloned.1.call-done = f32[192,96]{1,0:T(8,128)} async-done(((f32[768,96]{1,0:T(8,128)}), f32[192,96]{1,0:T(8,128)}) %reduce-scatter.33.cloned.1.call-update) | async-done | bytes 73744
  1526.5 21.6 %reduce-scatter.31.cloned.1.call-done = f32[192,96]{1,0:T(8,128)} async-done(((f32[768,96]{1,0:T(8,128)}), f32[192,96]{1,0:T(8,128)}) %reduce-scatter.31.cloned.1.call-update) | async-done | bytes 73744
  (1339 shorter events, 830.0 us)
Async XLA Ops:
  7.2 127.3 %all-gather.5.cloned.1.call-start = ((), (), s32[]{:S(2)}) async-start(), calls=%async_computation.10 | async-start | bytes 3538944 | tf_op jit(solution)/shard_map/all_gather | solution.py:115
  12.8 467.0 %reduce-scatter.19.cloned.1.call-start = ((), (), s32[]{:S(2)}) async-start(), calls=%async_computation.11 | async-start | bytes 7077888 | tf_op jit(solution)/shard_map/reduce_scatter | solution.py:129
  22.2 54.5 %copy-start.74 = (bf16[192,96]{1,0:T(8,128)(2,1)S(1)}, bf16[192,96]{1,0:T(8,128)(2,1)}, u32[]{:S(2)}) copy-start(bf16[192,96]{1,0:T(8,128)(2,1)} %param.28) | copy-start | bytes 110596
  22.2 70.0 %copy-start.75 = (bf16[192,96]{1,0:T(8,128)(2,1)S(1)}, bf16[192,96]{1,0:T(8,128)(2,1)}, u32[]{:S(2)}) copy-start(bf16[192,96]{1,0:T(8,128)(2,1)} %param.29) | copy-start | bytes 110596
  22.2 84.2 %copy-start.76 = (bf16[192,96]{1,0:T(8,128)(2,1)S(1)}, bf16[192,96]{1,0:T(8,128)(2,1)}, u32[]{:S(2)}) copy-start(bf16[192,96]{1,0:T(8,128)(2,1)} %param.30) | copy-start | bytes 110596
  22.2 97.8 %copy-start.77 = (bf16[192,96]{1,0:T(8,128)(2,1)S(1)}, bf16[192,96]{1,0:T(8,128)(2,1)}, u32[]{:S(2)}) copy-start(bf16[192,96]{1,0:T(8,128)(2,1)} %param.31) | copy-start | bytes 110596
  22.2 111.4 %copy-start.100 = (f32[4,96]{1,0:T(4,128)S(1)}, f32[4,96]{1,0:T(4,128)}, u32[]{:S(2)}) copy-start(f32[4,96]{1,0:T(4,128)} %param.34) | copy-start | bytes 4612
  22.2 112.0 %copy-start.62 = (s32[1,2048]{1,0:T(1,128)S(1)}, s32[1,2048]{1,0:T(1,128)}, u32[]{:S(2)}) copy-start(s32[1,2048]{1,0:T(1,128)} %param.23) | copy-start | bytes 24580
  92.1 45.5 %copy-start.42 = (bf16[768,96]{1,0:T(8,128)(2,1)}, bf16[768,96]{1,0:T(8,128)(2,1)S(1)}, u32[]{:S(2)}) copy-start(bf16[768,96]{1,0:T(8,128)(2,1)S(1)} %all_gather.31) | copy-start | bytes 442372
  133.6 278.3 %copy-start.41 = (bf16[768,96]{1,0:T(8,128)(2,1)}, bf16[768,96]{1,0:T(8,128)(2,1)S(1)}, u32[]{:S(2)}) copy-start(bf16[768,96]{1,0:T(8,128)(2,1)S(1)} %all_gather.34) | copy-start | bytes 442372
  140.8 269.8 %copy-start.11 = (f32[2048,96]{0,1:T(8,128)}, f32[2048,96]{0,1:T(8,128)S(1)}, u32[]{:S(2)}) copy-start(f32[2048,96]{0,1:T(8,128)S(1)} %get-tuple-element.953) | copy-start | bytes 2359300
  416.4 63.4 %copy-start.8 = (bf16[256,768]{1,0:T(8,128)(2,1)S(1)}, bf16[256,768]{1,0:T(8,128)(2,1)}, u32[]{:S(2)}) copy-start(bf16[256,768]{1,0:T(8,128)(2,1)} %param.22) | copy-start | bytes 1179652
  416.4 65.0 %copy-start.78 = (f32[768]{0:T(1024)S(1)}, f32[768]{0:T(1024)}, u32[]{:S(2)}) copy-start(f32[768]{0:T(1024)} %param.26) | copy-start | bytes 9220
  416.5 102.5 %all-gather.7.cloned.1.call-start = ((), (), s32[]{:S(2)}) async-start(), calls=%async_computation.12 | async-start | bytes 3538944 | tf_op jit(solution)/shard_map/all_gather | solution.py:135
  483.1 66.7 %all-gather.9.cloned.1.call-start = ((), (), s32[]{:S(2)}) async-start(), calls=%async_computation.14 | async-start | bytes 3538944 | tf_op jit(solution)/shard_map/all_gather | solution.py:143
  483.6 145.5 %reduce-scatter.23.cloned.1.call-start = ((), (), s32[]{:S(2)}) async-start(), calls=%async_computation.15 | async-start | bytes 7077888 | tf_op jit(solution)/shard_map/reduce_scatter | solution.py:148
  567.3 126.9 %reduce-scatter.21.cloned.1.call-start = ((), (), s32[]{:S(2)}) async-start(), calls=%async_computation.13 | async-start | bytes 7077888 | tf_op jit(solution)/shard_map/reduce_scatter | solution.py:139
  576.6 120.9 %copy-start.35 = (bf16[256,768]{1,0:T(8,128)(2,1)S(1)}, bf16[256,768]{1,0:T(8,128)(2,1)}, u32[]{:S(2)}) copy-start(bf16[256,768]{1,0:T(8,128)(2,1)} %param.39) | copy-start | bytes 1179652
  576.6 154.3 %all-gather.11.cloned.1.call-start = ((), (), s32[]{:S(2)}) async-start(), calls=%async_computation.16 | async-start | bytes 3538944 | tf_op jit(solution)/shard_map/all_gather | solution.py:153
  698.4 726.4 %reduce-scatter.25.cloned.1.call-start = ((), (), s32[]{:S(2)}) async-start(), calls=%async_computation.17 | async-start | bytes 7077888 | tf_op jit(solution)/shard_map/reduce_scatter | solution.py:163
  738.3 550.0 %copy-start.19 = (f32[2045,96]{0,1:T(8,128)S(1)}, f32[2045,96]{0,1:T(8,128)}, u32[]{:S(2)}) copy-start(f32[2045,96]{0,1:T(8,128)} %copy-done.18) | copy-start | bytes 2355844
  1298.2 171.6 %reduce-scatter.37.cloned.1.call-start = ((), (), s32[]{:S(2)}) async-start(), calls=%async_computation.23 | async-start | bytes 1474560
  1304.4 104.9 %copy-start.83 = (f32[128]{0:T(128)S(1)}, f32[128]{0:T(128)}, u32[]{:S(2)}) copy-start(f32[128]{0:T(128)} %get-tuple-element.1525) | copy-start | bytes 1540
  1304.4 165.4 %reduce-scatter.29.cloned.1.call-start = ((), (), s32[]{:S(2)}) async-start(), calls=%async_computation.19 | async-start | bytes 1474560 | tf_op jit(solution)/shard_map/reduce_scatter | solution.py:176
  1310.2 159.6 %all-reduce.14.cloned.1.call-start = ((), (), s32[]{:S(2)}) async-start(), calls=%async_computation.24 | async-start | bytes 201728 | tf_op jit(solution)/shard_map/psum | solution.py:179
  1416.4 66.7 %reduce-scatter.27.cloned.1.call-start = ((), (), s32[]{:S(2)}) async-start(), calls=%async_computation.18 | async-start | bytes 491520 | tf_op jit(solution)/shard_map/reduce_scatter | solution.py:175
  1418.3 86.5 %reduce-scatter.35.cloned.1.call-start = ((), (), s32[]{:S(2)}) async-start(), calls=%async_computation.22 | async-start | bytes 491520
  1421.9 45.5 %copy-start.17 = (f32[256,768]{1,0:T(8,128)S(1)}, f32[256,768]{1,0:T(8,128)}, u32[]{:S(2)}) copy-start(f32[256,768]{1,0:T(8,128)} %copy-done.16) | copy-start | bytes 2359300
  1421.9 45.5 %copy-start.36 = (bf16[256,768]{1,0:T(8,128)(2,1)S(1)}, bf16[256,768]{1,0:T(8,128)(2,1)}, u32[]{:S(2)}) copy-start(bf16[256,768]{1,0:T(8,128)(2,1)} %param.39) | copy-start | bytes 1179652
  1421.9 45.5 %copy-start.91 = (f32[256]{0:T(256)S(1)}, f32[256]{0:T(256)}, u32[]{:S(2)}) copy-start(f32[256]{0:T(256)} %copy-done.90) | copy-start | bytes 3076
  1422.9 103.6 %reduce-scatter.33.cloned.1.call-start = ((), (), s32[]{:S(2)}) async-start(), calls=%async_computation.21 | async-start | bytes 491520
  1423.9 124.2 %reduce-scatter.31.cloned.1.call-start = ((), (), s32[]{:S(2)}) async-start(), calls=%async_computation.20 | async-start | bytes 491520
  (326 other events, 1656.9 us)
Sparse Core Ops, SparseCore 0:
  13.0 34.9 all-gather.4
  416.6 63.2 reduce-scatter.18
  483.2 32.2 all-gather.6
  517.4 32.3 all-gather.8
  567.4 61.7 reduce-scatter.22
  632.4 61.7 reduce-scatter.20
  698.5 32.2 all-gather.10
  1298.4 61.7 reduce-scatter.24
  1363.1 29.1 reduce-scatter.36
  1395.0 27.8 reduce-scatter.28
  1426.2 33.2 all-reduce.13
  1462.3 20.7 reduce-scatter.26
  1485.9 18.8 reduce-scatter.34
  1507.6 18.8 reduce-scatter.32
  1529.2 18.8 reduce-scatter.30
where the time goes:
time: 1580 us; the launch traced here: 1560 us
  other arithmetic  703 us (44%)
  waiting for transfers between devices  315 us (20%)
  local copies, waits for them, and re-layouts  294 us (19%)
  blocking collectives  132 us (8%)
  matrix products  56.7 us (4%)
  loops' own time  45.2 us (3%)
    dot_general x32, other arithmetic, advance(): jnp.einsum('abc,ab,bc->ac', toeplitz, same_mask, part, precision=lax.Prec...  171 us
    while x528, local copies, waits for them, and re-layouts  105 us
    scatter-add x1, other arithmetic, mixer_core(): toeplitz = kernel[jnp.clip(offset, 0, BLOCK - 1)]  98.3 us
    add_any x32, other arithmetic, mixer_core(): lax.scan(jax.checkpoint(advance), start_state, (blocks_in, blocks_seg))  89 us
    dot_general x48, other arithmetic, advance(): jnp.einsum('pnc,pc->nc', behind, part * keep_mask[:, None], precision=lax...  67 us
    unnamed x19, waiting for transfers between devices  65.7 us
    reduce_scatter x1, waiting for transfers between devices, on_device(): lax.psum_scatter(right_product(mixed, w_output), ('head', 'tensor'), scat...  63.3 us
    reduce_scatter x1, waiting for transfers between devices, on_device(): lax.psum_scatter(right_product(act_out, w_down), ('head', 'tensor'), scat...  62.4 us
  transfers between devices with their start and end apart: 15, of which 9 were waited for; matrix products, arithmetic and copies ran while one was open for 13% of the time, Pallas kernels for 0%

commit v1 on v0

v1 whole, which is shorter than its diff:
```python
import functools
import jax, jax.numpy as jnp
from jax import lax
from jax.experimental import pallas as pl
from jax.experimental.pallas import tpu as pltpu

LANES = 128
SHIFT = 4
SEQS = 3
NT = (((1,), (1,)), ((), ()))
TN = (((0,), (0,)), ((), ()))
NN = (((1,), (0,)), ((), ()))


def mm(left, right, dims=NN):
    return lax.dot_general(left, right, dims, preferred_element_type=jnp.float32)


def iota(shape, axis):
    return lax.broadcasted_iota(jnp.int32, shape, axis)


def seg_masks(seg, nb):
    lane = iota((nb, LANES), 1)
    row = iota((nb, LANES), 0)
    masks = [(seg == k).astype(jnp.float32) for k in range(SEQS)]
    end = jnp.broadcast_to(seg[:, LANES - 1 :], (nb, LANES))
    last = jnp.where(row == 0, -1, pltpu.roll(end, 1, axis=0))
    live = (seg == last).astype(jnp.float32)
    keep = (seg == end).astype(jnp.float32)
    carry = (end == last).astype(jnp.float32)
    same = []
    for j in range(1, SHIFT):
        r = pltpu.roll(seg, j, axis=1)
        r2 = pltpu.roll(r, 1, axis=0)
        prior = jnp.where(lane < j, r2, r)
        ok = (prior == seg) & ((row > 0) | (lane >= j))
        same.append(ok.astype(jnp.float32))
    return masks, live, keep, carry, same


def priors(k, same):
    lane = iota(k.shape, 1)
    out = []
    for j in range(1, SHIFT):
        r = pltpu.roll(k, j, axis=1)
        r2 = pltpu.roll(r, 1, axis=0)
        out.append(jnp.where(lane < j, r2, r) * same[j - 1])
    return out


def flip_matrix():
    return (iota((LANES, LANES), 0) + iota((LANES, LANES), 1) == LANES - 1).astype(jnp.bfloat16)


def read_seg(seg_ref, nb):
    return jnp.concatenate([seg_ref[:, b * LANES : (b + 1) * LANES] for b in range(nb)], axis=0)


def transposed(scr, top, bottom):
    ns, chans = top.shape
    scr[...] = jnp.zeros_like(scr)
    scr[0:ns, 0:chans] = top
    if bottom is not None:
        scr[ns : 2 * ns, 0:chans] = bottom
    return scr[...].T


def stack_masked(x, masks):
    return jnp.concatenate([x * m for m in masks], axis=0).astype(jnp.bfloat16)


def merge_masked(y, masks):
    nb = masks[0].shape[0]
    return sum(y[i * nb : (i + 1) * nb] * m for i, m in enumerate(masks))


def toeplitz(krow):
    t = pltpu.roll(jnp.broadcast_to(krow, (LANES, LANES)), 0, axis=1, stride=1, stride_axis=0)
    return jnp.where(iota((LANES, LANES), 1) >= iota((LANES, LANES), 0), t, 0.0).astype(jnp.bfloat16)


def mixer_fwd_kernel(
    un, qkv_ref, seg_ref, sw_ref, skip_ref, rate_ref, inb_ref, outc_ref,
    mixed_ref, core_ref, s_ref, f_ref, urev_ref, pp_ref, kern_ref,
    tscr, a_scr, b_scr, c_scr, e_scr, u_scr, kscr,
):
    ns, chans = rate_ref.shape
    nb = qkv_ref.shape[1] // chans
    masks, live, keep, carry, same = seg_masks(read_seg(seg_ref, nb), nb)
    flip = flip_matrix()
    keep_rev = mm(keep.astype(jnp.bfloat16), flip)
    rate, in_b, out_c = rate_ref[...], inb_ref[...], outc_ref[...]
    decay = jnp.exp(-rate)
    a_scr[...] = transposed(tscr, rate, rate)
    b_scr[...] = transposed(tscr, in_b * decay, None)
    c_scr[...] = transposed(tscr, out_c, None)
    e_scr[...] = transposed(tscr, jnp.exp(-rate * LANES), None)

    def kern_step(i, e):
        for j in range(8):
            kscr[pl.ds(i * 8 + j, 1), 0:chans] = jnp.sum(e, axis=0, keepdims=True)
            e = e * decay
        return e

    kscr[...] = jnp.zeros_like(kscr)
    lax.fori_loop(0, LANES // 8, kern_step, in_b * out_c)
    kern_ref[...] = kscr[...].T[0:chans]

    def drive_step(i, _):
        for j in range(un):
            c = i * un + j
            rows = pl.ds(pl.multiple_of(c * nb, nb), nb)
            k = qkv_ref[1, rows]
            shifted = sw_ref[0, c] * k
            for lag, prior in enumerate(priors(k, same)):
                shifted = shifted + sw_ref[lag + 1, c] * prior
            u_scr[rows, :] = shifted * qkv_ref[2, rows]
        return 0

    lax.fori_loop(0, chans // un, drive_step, 0)
    step_rows = 16 * nb

    def rev_step(i, _):
        rows = pl.ds(pl.multiple_of(i * step_rows, step_rows), step_rows)
        urev_ref[rows, :] = mm(u_scr[rows, :].astype(jnp.bfloat16), flip).astype(jnp.bfloat16)
        return 0

    lax.fori_loop(0, chans // 16, rev_step, 0)
    pos = iota((LANES, LANES), 0).astype(jnp.float32)
    factor = jnp.where(iota((LANES, LANES), 1) < ns, 1.0, pos)
    i8 = iota((8, LANES), 0).astype(jnp.float32)
    i16 = iota((LANES // 8, LANES), 0).astype(jnp.float32) * 8.0

    def fresh_step(i, _):
        for j in range(un):
            c = i * un + j
            rows = pl.ds(pl.multiple_of(c * nb, nb), nb)
            a = a_scr[pl.ds(c, 1), :]
            base = jnp.exp(-a * i8)
            tall = jnp.exp(-a * i16)
            p = (tall[:, None, :] * base[None]).reshape(LANES, LANES)
            pp = (p * factor).astype(jnp.bfloat16)
            pp_ref[pl.ds(pl.multiple_of(c * LANES, LANES), LANES), :] = pp
            urk = (urev_ref[rows, :].astype(jnp.float32) * keep_rev).astype(jnp.bfloat16)
            f_ref[rows, :] = mm(urk, pp)
        return 0

    lax.fori_loop(0, chans // un, fresh_step, 0)
    across = e_scr[0:chans, :]
    b_ext = b_scr[0:chans, :]
    state = jnp.zeros((chans, LANES), jnp.float32)
    for b in range(nb):
        s_ref[pl.ds(b, chans, stride=nb), :] = state + pltpu.roll(state, ns, axis=1)
        fresh = f_ref[pl.ds(b, chans, stride=nb), :]
        state = across * carry[b : b + 1, :] * state + b_ext * fresh

    def out_step(i, _):
        for j in range(un):
            c = i * un + j
            rows = pl.ds(pl.multiple_of(c * nb, nb), nb)
            t = toeplitz(kern_ref[pl.ds(c, 1), :])
            u = u_scr[rows, :]
            y = merge_masked(mm(stack_masked(u, masks), t), masks)
            sc = (s_ref[rows, :] * c_scr[pl.ds(c, 1), :]).astype(jnp.bfloat16)
            pp = pp_ref[pl.ds(pl.multiple_of(c * LANES, LANES), LANES), :]
            core = y + live * mm(sc, pp, NT) + skip_ref[0, c] * u
            core_ref[rows, :] = core
            u_scr[rows, :] = qkv_ref[0, rows] * core
        return 0

    lax.fori_loop(0, chans // un, out_step, 0)
    for b in range(nb):
        half = b % 2
        mixed_ref[b // 2, :, half * LANES : (half + 1) * LANES] = u_scr[
            pl.ds(b, chans, stride=nb), :
        ].astype(jnp.bfloat16)


def mixer_fwd(qkv, seg, shift_w, skip, rate, in_b, out_c, un=4):
    ns, chans = rate.shape
    rows = qkv.shape[1]
    nb = rows // chans
    f32, bf16 = jnp.float32, jnp.bfloat16
    sds = jax.ShapeDtypeStruct
    vm = pl.BlockSpec(memory_space=pltpu.VMEM)
    sm = pl.BlockSpec(memory_space=pltpu.SMEM)
    sq = pltpu.VMEM((LANES, LANES), f32)
    return pl.pallas_call(
        functools.partial(mixer_fwd_kernel, un),
        out_shape=(
            sds((nb // 2, chans, 2 * LANES), bf16),
            sds((rows, LANES), f32),
            sds((rows, LANES), f32),
            sds((rows, LANES), f32),
            sds((rows, LANES), bf16),
            sds((chans * LANES, LANES), bf16),
            sds((chans, LANES), f32),
        ),
        in_specs=[vm, vm, sm, sm, vm, vm, vm],
        out_specs=(vm,) * 7,
        scratch_shapes=[sq, sq, sq, sq, sq, pltpu.VMEM((rows, LANES), f32), sq],
        compiler_params=pltpu.CompilerParams(vmem_limit_bytes=48 << 20),
        name="mixer_fwd",
    )(qkv, seg, shift_w, skip, rate, in_b, out_c)


def mixer_bwd_kernel(
    un, gm_ref, qkv_ref, core_ref, s_ref, f_ref, urev_ref, pp_ref, kern_ref, seg_ref,
    sw_ref, skip_ref, rate_ref, inb_ref, outc_ref,
    dqkv_ref, dsw_ref, drate_ref, dinb_ref, doutc_ref, dskip_ref,
    tscr, b_scr, c_scr, e_scr, g_scr, sh_scr, h_scr, x_scr, dur_scr, dui_scr, dq_scr, dk_scr, dv_scr, gr_scr, red_scr,
):
    ns, chans = rate_ref.shape
    nb = qkv_ref.shape[1] // chans
    masks, live, keep, carry, same = seg_masks(read_seg(seg_ref, nb), nb)
    flip = flip_matrix()
    keep_rev = mm(keep.astype(jnp.bfloat16), flip)
    masks_rev = [mm(m.astype(jnp.bfloat16), flip) for m in masks]
    rate, in_b, out_c = rate_ref[...], inb_ref[...], outc_ref[...]
    decay = jnp.exp(-rate)
    b_scr[...] = transposed(tscr, in_b * decay, None)
    c_scr[...] = transposed(tscr, out_c, None)
    e_scr[...] = transposed(tscr, jnp.exp(-rate * LANES), None)
    red_scr[...] = jnp.zeros_like(red_scr)
    gr_scr[...] = jnp.zeros_like(gr_scr)

    for b in range(nb):
        half = b % 2
        x_scr[pl.ds(b, chans, stride=nb), :] = gm_ref[
            b // 2, :, half * LANES : (half + 1) * LANES
        ].astype(jnp.float32)
    corner = iota((LANES, LANES), 0) + iota((LANES, LANES), 1) >= LANES - 1

    def grad_step(i, _):
        for j in range(un):
            c = i * un + j
            rows = pl.ds(pl.multiple_of(c * nb, nb), nb)
            gm = x_scr[rows, :]
            dq_scr[rows, :] = gm * core_ref[rows, :]
            g = gm * qkv_ref[0, rows]
            g_scr[rows, :] = g
            k = qkv_ref[1, rows]
            shifted = sw_ref[0, c] * k
            for lag, prior in enumerate(priors(k, same)):
                shifted = shifted + sw_ref[lag + 1, c] * prior
            sh_scr[rows, :] = shifted
            red_scr[SHIFT, pl.ds(c, 1), :] = jnp.sum(
                g * shifted * qkv_ref[2, rows], axis=0, keepdims=True
            )
            ur = stack_masked(urev_ref[rows, :].astype(jnp.float32), masks_rev)
            cross = mm(ur, stack_masked(g, masks), TN)
            skew = pltpu.roll(jnp.where(corner, cross, 0.0), 1, axis=1, stride=1, stride_axis=0)
            gr_scr[pl.ds(c, 1), :] = jnp.sum(skew, axis=0, keepdims=True)
            pp = pp_ref[pl.ds(pl.multiple_of(c * LANES, LANES), LANES), :]
            h_scr[rows, :] = mm((g * live).astype(jnp.bfloat16), pp)
        return 0

    lax.fori_loop(0, chans // un, grad_step, 0)
    across = e_scr[0:chans, :]
    b_ext = b_scr[0:chans, :]
    c_ext = c_scr[0:chans, :]
    zero = jnp.zeros((chans, LANES), jnp.float32)
    adj, acc_out, acc_in, acc_carry = zero, zero, zero, zero
    for b in range(nb - 1, -1, -1):
        here = pl.ds(b, chans, stride=nb)
        h = h_scr[here, :]
        s = s_ref[here, :]
        acc_out = acc_out + s * h
        acc_in = acc_in + (adj + pltpu.roll(adj, ns, axis=1)) * f_ref[here, :]
        acc_carry = acc_carry + carry[b : b + 1, :] * adj * s
        x_scr[here, :] = b_ext * adj
        adj = c_ext * h + across * carry[b : b + 1, :] * adj

    def back_step(i, _):
        for j in range(un):
            c = i * un + j
            rows = pl.ds(pl.multiple_of(c * nb, nb), nb)
            t = toeplitz(kern_ref[pl.ds(c, 1), :])
            g = g_scr[rows, :]
            inner = merge_masked(mm(stack_masked(g, masks), t, NT), masks)
            pp = pp_ref[pl.ds(pl.multiple_of(c * LANES, LANES), LANES), :]
            dur_scr[rows, :] = (mm(x_scr[rows, :].astype(jnp.bfloat16), pp, NT) * keep_rev).astype(jnp.bfloat16)
            g_scr[rows, :] = inner + skip_ref[0, c] * g
        return 0

    lax.fori_loop(0, chans // un, back_step, 0)
    step_rows = 16 * nb

    def rev_step(i, _):
        rows = pl.ds(pl.multiple_of(i * step_rows, step_rows), step_rows)
        dui_scr[rows, :] = mm(dur_scr[rows, :], flip)
        return 0

    lax.fori_loop(0, chans // 16, rev_step, 0)

    def last_step(i, _):
        for j in range(un):
            c = i * un + j
            rows = pl.ds(pl.multiple_of(c * nb, nb), nb)
            du = g_scr[rows, :] + dui_scr[rows, :]
            dv_scr[rows, :] = du * sh_scr[rows, :]
            ds = du * qkv_ref[2, rows]
            k = qkv_ref[1, rows]
            lane = iota(k.shape, 1)
            red_scr[0, pl.ds(c, 1), :] = jnp.sum(ds * k, axis=0, keepdims=True)
            dk = sw_ref[0, c] * ds
            for lag, prior in enumerate(priors(k, same)):
                red_scr[lag + 1, pl.ds(c, 1), :] = jnp.sum(ds * prior, axis=0, keepdims=True)
                d = ds * same[lag]
                r = pltpu.roll(d, LANES - (lag + 1), axis=1)
                r2 = pltpu.roll(r, nb - 1, axis=0)
                dk = dk + sw_ref[lag + 1, c] * jnp.where(lane < LANES - (lag + 1), r, r2)
            dk_scr[rows, :] = dk
        return 0

    lax.fori_loop(0, chans // un, last_step, 0)
    for b in range(nb):
        half = b % 2
        for i, scr in enumerate((dq_scr, dk_scr, dv_scr)):
            dqkv_ref[b // 2, i, :, half * LANES : (half + 1) * LANES] = scr[
                pl.ds(b, chans, stride=nb), :
            ].astype(jnp.bfloat16)
    for j in range(SHIFT):
        dsw_ref[j : j + 1, :] = jnp.sum(red_scr[j].T, axis=0, keepdims=True)[:, 0:chans]
    dskip_ref[...] = jnp.sum(red_scr[SHIFT].T, axis=0, keepdims=True)[:, 0:chans]
    tscr[...] = gr_scr[...].T

    def kern_back(i, carried):
        e, zeroth, first = carried
        block = tscr[pl.ds(pl.multiple_of(i * 8, 8), 8), 0:chans]
        for j in range(8):
            term = e * block[j : j + 1, :]
            zeroth = zeroth + term
            first = first + term * (i * 8 + j).astype(jnp.float32)
            e = e * decay
        return e, zeroth, first

    blank = jnp.zeros((ns, chans), jnp.float32)
    _, zeroth, first = lax.fori_loop(0, LANES // 8, kern_back, (blank + 1.0, blank, blank))

    def back(x):
        tscr[...] = jnp.zeros_like(tscr)
        tscr[0:chans, :] = x
        y = tscr[...].T
        return y[0:ns, 0:chans], y[ns : 2 * ns, 0:chans]

    d_out, s_h1 = back(acc_out)
    d_inp, ds_f1 = back(acc_in)
    d_carry, _ = back(acc_carry)
    dinb_ref[...] = decay * d_inp + out_c * zeroth
    doutc_ref[...] = d_out + in_b * zeroth
    drate_ref[...] = -(
        out_c * s_h1
        + in_b * decay * (ds_f1 + d_inp)
        + LANES * jnp.exp(-rate * LANES) * d_carry
        + in_b * out_c * first
    )


def mixer_bwd(gm, qkv, core, s, f, urev, pp, kern, seg, shift_w, skip, rate, in_b, out_c, un=4):
    ns, chans = rate.shape
    rows = qkv.shape[1]
    nb = rows // chans
    f32, bf16 = jnp.float32, jnp.bfloat16
    sds = jax.ShapeDtypeStruct
    vm = pl.BlockSpec(memory_space=pltpu.VMEM)
    sm = pl.BlockSpec(memory_space=pltpu.SMEM)
    sq = pltpu.VMEM((LANES, LANES), f32)
    full = pltpu.VMEM((rows, LANES), f32)
    half = pltpu.VMEM((rows, LANES), bf16)
    return pl.pallas_call(
        functools.partial(mixer_bwd_kernel, un),
        out_shape=(
            sds((nb // 2, 3, chans, 2 * LANES), bf16),
            sds((SHIFT, chans), f32),
            sds((ns, chans), f32),
            sds((ns, chans), f32),
            sds((ns, chans), f32),
            sds((1, chans), f32),
        ),
        in_specs=[vm] * 9 + [sm, sm, vm, vm, vm],
        out_specs=(vm,) * 6,
        scratch_shapes=[
            sq, sq, sq, sq, full, full, full, full, half, full, full, full, full, sq,
            pltpu.VMEM((SHIFT + 1, LANES, LANES), f32),
        ],
        compiler_params=pltpu.CompilerParams(vmem_limit_bytes=56 << 20),
        name="mixer_bwd",
    )(gm, qkv, core, s, f, urev, pp, kern, seg, shift_w, skip, rate, in_b, out_c)


from jax.sharding import PartitionSpec as P

GROUP = ("head", "tensor")


def norm_stats(x):
    centred = x - jnp.mean(x, axis=0, keepdims=True)
    spread = jnp.mean(centred * centred, axis=0, keepdims=True)
    inv = lax.rsqrt(spread + 1e-05)
    return centred * inv, inv


def norm_back(grad, gain, hat, inv):
    scaled = grad * gain
    return inv * (
        scaled
        - jnp.mean(scaled, axis=0, keepdims=True)
        - hat * jnp.mean(scaled * hat, axis=0, keepdims=True)
    )


def lanes_sum(x):
    return jnp.sum(x, axis=1)


def gelu_pair(pre):
    cdf = 0.5 * (1.0 + lax.erf(pre * 0.7071067811865476))
    return pre * cdf, cdf + pre * (0.3989422804014327 * jnp.exp(-0.5 * pre * pre))


def on_device(
    tokens, seg_ids, norm1_gain, norm1_bias, norm2_gain, norm2_bias, q_weight, k_weight, v_weight,
    out_weight, up_weight, down_weight, shift_weight, decay_rate, in_coef, out_coef, skip_coef, cotangent,
):
    bf16, f32 = jnp.bfloat16, jnp.float32
    chans = q_weight.shape[1]
    own = tokens.shape[0]
    feats = tokens.shape[1]
    gather = lambda w: lax.all_gather(w, "dp", axis=0, tiled=True)
    w_joint = gather(jnp.concatenate([q_weight, k_weight, v_weight], axis=1))
    w_out = lax.all_gather(gather(out_weight), GROUP, axis=1, tiled=True)
    w_up, w_down = gather(up_weight), gather(down_weight)
    group_gather = lambda x: lax.all_gather(x, GROUP, axis=0, tiled=False)
    scatter = lambda x: lax.psum_scatter(x, GROUP, scatter_dimension=0, tiled=False).astype(f32)
    swap = lambda x: lax.all_to_all(x, GROUP, split_axis=0, concat_axis=0, tiled=True)
    x = tokens.T.astype(f32)
    g = cotangent.T
    column = lambda v: v[:, None]
    hat1, inv1 = norm_stats(x)
    xn1 = group_gather((hat1 * column(norm1_gain) + column(norm1_bias)).astype(bf16))
    cot = group_gather(g)
    group = xn1.shape[0]
    qkv = jnp.einsum("gdt,dc->cgt", xn1, w_joint, preferred_element_type=f32)
    qkv = qkv.reshape(3, chans * group * own // LANES, LANES)
    mixed, *saved = mixer_fwd(
        qkv, seg_ids, shift_weight, skip_coef[None], decay_rate, in_coef, out_coef, un=16
    )
    mixed = swap(mixed).reshape(group * chans, own)
    hidden = x + jnp.dot(w_out, mixed, preferred_element_type=f32)
    hat2, inv2 = norm_stats(hidden)
    xn2 = group_gather((hat2 * column(norm2_gain) + column(norm2_bias)).astype(bf16))
    pre = jnp.einsum("gdt,df->gft", xn2, w_up, preferred_element_type=f32)
    act, slope = gelu_pair(pre)
    act = act.astype(bf16)
    grad_act = jnp.einsum("gdt,df->gft", cot, w_down, preferred_element_type=f32)
    grad_pre = (grad_act * slope).astype(bf16)
    mlp = scatter(jnp.einsum("gft,df->gdt", act, w_down, preferred_element_type=f32).astype(bf16))
    grad_xn2 = scatter(
        jnp.einsum("gft,df->gdt", grad_pre, w_up, preferred_element_type=f32).astype(bf16)
    )
    grad_down = jnp.einsum("gdt,gft->df", cot, act, preferred_element_type=f32)
    grad_up = jnp.einsum("gdt,gft->df", xn2, grad_pre, preferred_element_type=f32)
    result = (hidden + mlp).astype(bf16).T
    grad_hidden = g.astype(f32) + norm_back(grad_xn2, column(norm2_gain), hat2, inv2)
    gain2, bias2 = lanes_sum(grad_xn2 * hat2), lanes_sum(grad_xn2)
    grad_mix = grad_hidden.astype(bf16)
    grad_mixed = lax.dot_general(w_out, grad_mix, TN, preferred_element_type=f32).astype(bf16)
    grad_out = lax.dot_general(grad_mix, mixed, NT, preferred_element_type=f32)
    grad_out = lax.psum_scatter(grad_out.astype(bf16), GROUP, scatter_dimension=1, tiled=True)
    grad_mixed = swap(grad_mixed.reshape(group, chans, own))
    dqkv, dshift, drate, dinb, doutc, dskip = mixer_bwd(
        grad_mixed, qkv, *saved, seg_ids, shift_weight, skip_coef[None], decay_rate, in_coef, out_coef, un=16
    )
    dqkv = dqkv.reshape(group, 3 * chans, own)
    grad_w = jnp.einsum("gdt,gct->dc", xn1, dqkv, preferred_element_type=f32)
    grad_xn1 = scatter(
        jnp.einsum("gct,dc->gdt", dqkv, w_joint, preferred_element_type=f32).astype(bf16)
    )
    grad_x = (grad_hidden + norm_back(grad_xn1, column(norm1_gain), hat1, inv1)).T
    gain1, bias1 = lanes_sum(grad_xn1 * hat1), lanes_sum(grad_xn1)
    reduce = lambda v: lax.psum_scatter(v, "dp", scatter_dimension=0, tiled=True)
    grad_w = reduce(grad_w)
    sums = lax.psum((dshift, drate, dinb, doutc, dskip[0]), "dp")
    norms = lax.psum((gain1, bias1, gain2, bias2), ("dp", "head", "tensor"))
    return (
        result, grad_x, *norms, grad_w[:, :chans], grad_w[:, chans : 2 * chans], grad_w[:, 2 * chans :],
        reduce(grad_out.astype(f32)), reduce(grad_up), reduce(grad_down), *sums,
    )


def solution(mesh):
    rows = P(("dp", "head", "tensor"), None)
    weight = P("dp", GROUP)
    chan = P(None, GROUP)
    in_specs = (rows, P("dp", None)) + (P(),) * 4 + (weight,) * 6 + (chan,) * 4 + (P(GROUP), rows)
    out_specs = (rows, rows) + (P(),) * 4 + (weight,) * 6 + (chan,) * 4 + (P(GROUP),)
    return jax.shard_map(on_device, mesh=mesh, in_specs=in_specs, out_specs=out_specs, check_vma=False)
```

time: 1580 us -> 512 us (0.32); the launches traced: 1560 us -> 511 us
  other arithmetic: 703 us -> 16 us
  local copies, waits for them, and re-layouts: 294 us -> 35.7 us
  waiting for transfers between devices: 315 us -> 252 us
  loops' own time: 45.2 us -> 0 us
  Pallas kernels: 0 us -> 32.3 us
  matrix products: 56.7 us -> 37.1 us
    dot_general x114 -> x0, other arithmetic: 302 us -> none  [the longest x32 171 us: advance(): jnp.einsum('abc,ab,bc->ac', toeplitz, same_mask, part, precision=lax.Prec...]
    while x528 -> x0, local copies, waits for them, and re-layouts: 105 us -> none
    add_any x51 -> x0, other arithmetic: 101 us -> none  [the longest x32 89 us: mixer_core(): lax.scan(jax.checkpoint(advance), start_state, (blocks_in, blocks_seg))]
    scatter-add x1 -> x0, other arithmetic: 98.3 us -> none  [mixer_core(): toeplitz = kernel[jnp.clip(offset, 0, BLOCK - 1)]]
    mul x39 -> x0, other arithmetic: 55.9 us -> none  [the longest x16 51.8 us: mixer_core(): ahead = powers * jnp.exp(-rate)[None]]
    gather x1 -> x0, local copies, waits for them, and re-layouts: 54.5 us -> none  [mixer_core(): toeplitz = kernel[jnp.clip(offset, 0, BLOCK - 1)]]
    convert_element_type x57 -> x2, other arithmetic: 56.1 us -> 3.65 us  [the longest x1 2.02 us: on_device(): (hat1 * column(norm1_gain) + column(norm1_bias)).astype(bf16)]
    squeeze x64 -> x0, local copies, waits for them, and re-layouts: 50.3 us -> none  [mixer_core(): lax.scan(jax.checkpoint(advance), start_state, (blocks_in, blocks_seg))]
  transfers between devices with their start and end apart: 15 -> 14, of which waited for: 9 -> 10; matrix products, arithmetic and copies ran while one was open for 13% -> 11% of each run, Pallas kernels for 0% -> 6%
where the time goes in v1:
time: 512 us; the launch traced here: 511 us
  waiting for transfers between devices  252 us (49%)
  blocking collectives  119 us (23%)
  matrix products  37.1 us (7%)
  local copies, waits for them, and re-layouts  35.7 us (7%)
  Pallas kernels  32.3 us (6%)
  other arithmetic  16 us (3%)
  between operations  14.4 us (3%)
    reduce_scatter x3, waiting for transfers between devices, on_device(): lax.psum_scatter(x, GROUP, scatter_dimension=0, tiled=False).astype(f32)  136 us
    all_gather x4, blocking collectives, on_device(): gather = lambda w: lax.all_gather(w, 'dp', axis=0, tiled=True)  66.6 us
    unnamed x15, waiting for transfers between devices  42.5 us
    psum x1, blocking collectives, on_device(): norms = lax.psum((gain1, bias1, gain2, bias2), ('dp', 'head', 'tensor'))  41.6 us
    psum x1, waiting for transfers between devices, on_device(): sums = lax.psum((dshift, drate, dinb, doutc, dskip[0]), 'dp')  37 us
    pallas_call x1, Pallas kernels, mixer_bwd(): pl.pallas_call(functools.partial(mixer_bwd_kernel, un), out_shape=(sds((n...  20.1 us
    unnamed x72, local copies, waits for them, and re-layouts  19.8 us
    reduce_scatter x2, waiting for transfers between devices, on_device(): lax.psum_scatter(v, 'dp', scatter_dimension=0, tiled=True)  15.1 us
  transfers between devices with their start and end apart: 14, of which 10 were waited for; matrix products, arithmetic and copies ran while one was open for 11% of the time, Pallas kernels for 6%

profile of v1, /device:TPU:0, one launch (start us, length us, event | category | flops | bytes accessed | tf_op | source)
XLA Modules:
  0.0 510.8 jit_solution(10405596615110839730)
XLA Ops:
  11.7 15.7 %all_gather.36 = bf16[768,96]{1,0:T(8,128)(2,1)S(1)} all-gather(bf16[192,96]{1,0:T(8,128)(2,1)} %param.27), channel_id=1, replica_groups=mesh['dp'=4,'head'=4,'tensor'=2] {'dp'}, dimensions={0}, use_global_device_ids=true | all-gather | bytes 184320 | tf_op jit(solution)/shard_map/all_gather | solution.py:431
  29.1 17.0 %all_gather.33 = bf16[768,288]{1,0:T(8,128)(2,1)} all-gather(bf16[192,288]{1,0:T(8,128)(2,1)S(1)} %pad_maximum_fusion), channel_id=1, replica_groups=mesh['dp'=4,'head'=4,'tensor'=2] {'dp'}, dimensions={0}, use_global_device_ids=true | all-gather | bytes 552960 | tf_op jit(solution)/shard_map/all_gather | solution.py:431
  46.8 3.2 copy.67
  50.0 2.6 fusion.55
  52.6 2.8 copy.69
  58.0 12.2 %mixer_fwd.1 = (bf16[8,96,256]{2,1,0:T(8,128)(2,1)}, f32[1536,128]{1,0:T(8,128)S(1)}, f32[1536,128]{1,0:T(8,128)S(1)}, f32[1536,128]{1,0:T(8,128)S(1)}, bf16[153...) custom-call(f32[3,1536,128]{2,1,0:T(8,128)S(1)} %reshape.94.qkv_ref, ...), custom_call_target="tpu_custom_call" | custom-call | tf_op jit(solution)/shard_map/mixer_fwd/pallas_call | solution.py:189
  74.2 4.1 all-to-all-start
  78.4 7.4 %all-to-all-done = bf16[8,96,256]{2,1,0:T(8,128)(2,1)} async-done(((bf16[8,96,256]{2,1,0:T(8,128)(2,1)}), bf16[8,96,256]{2,1,0:T(8,128)(2,1)}, u32[]{:S(2)}, u32[]{:S(2)}) %all-to-all-start) | async-done | bytes 393248 | tf_op jit(solution)/shard_map/all_to_all | solution.py:437
  90.3 17.1 %all_gather.40 = bf16[768,384]{1,0:T(8,128)(2,1)S(1)} all-gather(bf16[192,384]{1,0:T(8,128)(2,1)} %param.28), channel_id=1, replica_groups=mesh['dp'=4,'head'=4,'tensor'=2] {'dp'}, dimensions={0}, use_global_device_ids=true | all-gather | bytes 737280 | tf_op jit(solution)/shard_map/all_gather | solution.py:431
  107.5 16.7 %all_gather.41 = bf16[768,384]{1,0:T(8,128)(2,1)S(1)} all-gather(bf16[192,384]{1,0:T(8,128)(2,1)} %param.29), channel_id=1, replica_groups=mesh['dp'=4,'head'=4,'tensor'=2] {'dp'}, dimensions={0}, use_global_device_ids=true | all-gather | bytes 737280 | tf_op jit(solution)/shard_map/all_gather | solution.py:431
  124.2 4.6 copy.90
  128.8 13.4 %all-gather.12.cloned.1.call-done = bf16[6144,256]{0,1:T(8,128)(2,1)} async-done(((bf16[768,256]{0,1:T(8,128)(2,1)}), bf16[6144,256]{0,1:T(8,128)(2,1)}) %all-gather.12.cloned.1.call-update) | async-done | bytes 3145744 | tf_op jit(solution)/shard_map/all_gather | solution.py:435
  142.2 5.2 %fusion.12 = (bf16[8,384,256]{1,2,0:T(8,128)(2,1)}, f32[8,256,384]{2,1,0:T(8,128)S(1)}) fusion(bf16[768,384]{1,0:T(8,128)(2,1)S(1)} %all_gather.40, bf16[32,8,8,768]{3,2,1,0:T(8,128)(2,1)} %bitcast.183), kind=kOutput, calls=%fused_computation.15 | convolution fusion | flops 1211891712 | bytes 8454144 | tf_op jit(solution)/shard_map/gdt,df->gft/dot_general | solution.py:454
  147.5 2.8 fusion.5
  151.4 3.5 convert_bitcast_fusion.1
  156.3 3.5 convert_bitcast_fusion.2
  159.9 41.5 %reduce-scatter.15.cloned.1.call-done = bf16[1,768,256]{1,2,0:T(8,128)(2,1)} async-done(((bf16[8,768,256]{1,2,0:T(8,128)(2,1)}), bf16[1,768,256]{1,2,0:T(8,128)(2,1)}) %reduce-scatter.15.cloned.1.call-update) | async-done | bytes 393232 | tf_op jit(solution)/shard_map/reduce_scatter | solution.py:436
  203.9 47.3 %reduce-scatter.13.cloned.1.call-done = bf16[1,768,256]{1,2,0:T(8,128)(2,1)} async-done(((bf16[8,768,256]{1,2,0:T(8,128)(2,1)}), bf16[1,768,256]{1,2,0:T(8,128)(2,1)}) %reduce-scatter.13.cloned.1.call-update) | async-done | bytes 393232 | tf_op jit(solution)/shard_map/reduce_scatter | solution.py:436
  253.5 2.6 convolution_convert_fusion
  256.8 10.8 %all_to_all.10.gm_ref = bf16[8,96,256]{2,1,0:T(8,128)(2,1)} all-to-all(bf16[8,96,256]{2,1,0:T(8,128)(2,1)S(1)} %bitcast.187), channel_id=1, replica_groups=mesh['dp'=4,'head'=4,'tensor'=2] {'head','tensor'}, dimensions={0} | all-to-all | bytes 786432 | tf_op jit(solution)/shard_map/all_to_all | solution.py:437
  267.7 20.1 %mixer_bwd.1 = (bf16[8,3,96,256]{3,2,1,0:T(8,128)(2,1)}, f32[4,96]{1,0:T(4,128)}, f32[64,96]{1,0:T(8,128)}, f32[64,96]{1,0:T(8,128)}, f32[64,96]{1,0:T(8,128)}, /*index=5*/f32[1,96]{1,0:T(1,128)}) custom-call(bf16[8,96,256]{2,1,0:T(8,128)(2,1)} %all_to_all.10.gm_ref, f32[3,1536,128]{2,1,0:T(8,128)} %copy-done, f32[1536,128]{1,0:T(8,128)} %copy-done.1, ...), custom_call_target="tpu_custom_call" | custom-call | tf_op jit(solution)/shard_map/mixer_bwd/pallas_call | solution.py:372
  287.8 4.2 convolution_bitcast_fusion.1
  292.1 3.5 convert_bitcast_fusion
  295.8 2.9 copy.92
  298.7 2.9 fusion.15
  301.6 3.8 convolution_bitcast_fusion
  309.5 15.1 %reduce-scatter.19.cloned.1.call-done = f32[192,288]{1,0:T(8,128)} async-done(((f32[768,288]{1,0:T(8,128)}), f32[192,288]{1,0:T(8,128)}) %reduce-scatter.19.cloned.1.call-update) | async-done | bytes 221200 | tf_op jit(solution)/shard_map/reduce_scatter | solution.py:483
  326.5 46.9 %reduce-scatter.17.cloned.1.call-done = bf16[1,768,256]{1,2,0:T(8,128)(2,1)} async-done(((bf16[8,768,256]{1,2,0:T(8,128)(2,1)}), bf16[1,768,256]{1,2,0:T(8,128)(2,1)}) %reduce-scatter.17.cloned.1.call-update) | async-done | bytes 393232 | tf_op jit(solution)/shard_map/reduce_scatter | solution.py:436
  375.9 41.6 %all-reduce = (f32[768]{0:T(1024)}, f32[768]{0:T(1024)}, f32[768]{0:T(1024)}, f32[768]{0:T(1024)}) all-reduce(f32[768]{0:T(1024)S(1)} %get-tuple-element.96, f32[768]{0:T(1024)S(1)} %convert_reduce_fusion.1, f32[768]{0:T(1024)S(1)} %copy-done.27, ...), channel_id=1, replica_groups=mesh['dp'=4,'head'=4,'tensor'=2] {'dp','head','tensor'}, use_global_device_ids=true, to_apply=%region_12.0 | all-reduce | flops 3072 | bytes 24576 | tf_op jit(solution)/shard_map/psum | solution.py:486
  419.7 17.4 %reduce-scatter.27.cloned.1.call-done = f32[192,384]{1,0:T(8,128)} async-done(((f32[768,384]{1,0:T(8,128)}), f32[192,384]{1,0:T(8,128)}) %reduce-scatter.27.cloned.1.call-update) | async-done | bytes 294928
  437.1 37.0 %all-reduce.4.cloned.1.call-done = (f32[4,96]{1,0:T(4,128)}, f32[64,96]{1,0:T(8,128)}, f32[64,96]{1,0:T(8,128)}, f32[64,96]{1,0:T(8,128)}, f32[96]{0:T(128)}) async-done(((f32[4,96]{1,0:T(4,128)}, f32[64,96]{1,0:T(8,128)}, f32[64,96]{1,0:T(8,128)}, f32[64,96]{1,0:T(8,128)}, f32[96]{0:T(128)}), (f32[4,96]{1,0:T(4,128)}, f32[64,96]{1,0:T(8,128)}, f32[64,96]{1,0:T(8,128)}, f32[64,96]{1,0:T(8,128)}, ...) | async-done | bytes 75664 | tf_op jit(solution)/shard_map/psum | solution.py:485
  474.1 23.7 %reduce-scatter.25.cloned.1.call-done = f32[192,96]{1,0:T(8,128)} async-done(((f32[768,96]{1,0:T(8,128)}), f32[192,96]{1,0:T(8,128)}) %reduce-scatter.25.cloned.1.call-update) | async-done | bytes 73744
  (127 shorter events, 43.3 us)
Async XLA Ops:
  7.2 21.8 %copy-start.22 = (bf16[192,96]{1,0:T(8,128)(2,1)S(1)}, bf16[192,96]{1,0:T(8,128)(2,1)}, u32[]{:S(2)}) copy-start(bf16[192,96]{1,0:T(8,128)(2,1)} %param.24) | copy-start | bytes 110596
  7.2 21.8 %copy-start.21 = (bf16[192,96]{1,0:T(8,128)(2,1)S(1)}, bf16[192,96]{1,0:T(8,128)(2,1)}, u32[]{:S(2)}) copy-start(bf16[192,96]{1,0:T(8,128)(2,1)} %param.25) | copy-start | bytes 110596
  7.2 21.8 %copy-start.20 = (bf16[192,96]{1,0:T(8,128)(2,1)S(1)}, bf16[192,96]{1,0:T(8,128)(2,1)}, u32[]{:S(2)}) copy-start(bf16[192,96]{1,0:T(8,128)(2,1)} %param.26) | copy-start | bytes 110596
  7.2 39.6 %all-gather.10.cloned.1.call-start = ((), (), s32[]{:S(2)}) async-start(), calls=%async_computation.17 | async-start | bytes 3538944 | tf_op jit(solution)/shard_map/all_gather | solution.py:435
  11.7 66.7 %all-gather.8.cloned.1.call-start = ((), (), s32[]{:S(2)}) async-start(), calls=%async_computation.10 | async-start | bytes 1327104 | tf_op jit(solution)/shard_map/all_gather | solution.py:433
  28.2 96.0 %all-gather.14.cloned.1.call-start = ((), (), s32[]{:S(2)}) async-start(), calls=%async_computation.19 | async-start | bytes 3538944 | tf_op jit(solution)/shard_map/all_gather | solution.py:435
  50.0 2.6 copy-start.12
  55.4 2.6 copy-start.10
  55.4 30.4 %copy-start.14 = (bf16[256,768]{1,0:T(8,128)(2,1)S(1)}, bf16[256,768]{1,0:T(8,128)(2,1)}, u32[]{:S(2)}) copy-start(bf16[256,768]{1,0:T(8,128)(2,1)} %param.18) | copy-start | bytes 1179652
  57.9 30.1 %copy-start = (f32[3,1536,128]{2,1,0:T(8,128)}, f32[3,1536,128]{2,1,0:T(8,128)S(1)}, u32[]{:S(2)}) copy-start(f32[3,1536,128]{2,1,0:T(8,128)S(1)} %reshape.94.qkv_ref) | copy-start | bytes 7077892
  58.0 30.7 %copy-start.23 = (f32[768]{0:T(1024)S(1)}, f32[768]{0:T(1024)}, u32[]{:S(2)}) copy-start(f32[768]{0:T(1024)} %param.22) | copy-start | bytes 9220
  74.2 11.6 %all-to-all-start = ((bf16[8,96,256]{2,1,0:T(8,128)(2,1)}), bf16[8,96,256]{2,1,0:T(8,128)(2,1)}, u32[]{:S(2)}, u32[]{:S(2)}) async-start(bf16[8,96,256]{2,1,0:T(8,128)(2,1)} %get-tuple-element.30), calls=%async_computation | async-start | bytes 786432 | tf_op jit(solution)/shard_map/all_to_all | solution.py:437
  78.3 63.9 %all-gather.12.cloned.1.call-start = ((), (), s32[]{:S(2)}) async-start(), calls=%async_computation.18 | async-start | bytes 3538944 | tf_op jit(solution)/shard_map/all_gather | solution.py:435
  90.3 111.0 %reduce-scatter.15.cloned.1.call-start = ((), (), s32[]{:S(2)}) async-start(), calls=%async_computation.12 | async-start | bytes 3538944 | tf_op jit(solution)/shard_map/reduce_scatter | solution.py:436
  142.2 5.2 %copy-start.17 = (bf16[6144,256]{1,0:T(8,128)(2,1)S(1)}, bf16[6144,256]{1,0:T(8,128)(2,1)}, u32[]{:S(2)}) copy-start(bf16[6144,256]{1,0:T(8,128)(2,1)} %copy.90) | copy-start | bytes 9437188
  154.9 96.3 %reduce-scatter.13.cloned.1.call-start = ((), (), s32[]{:S(2)}) async-start(), calls=%async_computation.11 | async-start | bytes 3538944 | tf_op jit(solution)/shard_map/reduce_scatter | solution.py:436
  156.3 45.0 %copy-start.26 = (f32[256]{0:T(256)S(1)}, f32[256]{0:T(256)}, u32[]{:S(2)}) copy-start(f32[256]{0:T(256)} %copy-done.25) | copy-start | bytes 3076
  159.8 91.4 %copy-start.19 = (bf16[256,768]{1,0:T(8,128)(2,1)S(1)}, bf16[256,768]{1,0:T(8,128)(2,1)}, u32[]{:S(2)}) copy-start(bf16[256,768]{1,0:T(8,128)(2,1)} %param.35) | copy-start | bytes 1179652
  159.8 147.8 %reduce-scatter.21.cloned.1.call-start = ((), (), s32[]{:S(2)}) async-start(), calls=%async_computation.15 | async-start | bytes 1327104 | tf_op jit(solution)/shard_map/reduce_scatter | solution.py:471
  251.2 4.9 copy-start.15
  256.1 68.5 %reduce-scatter.19.cloned.1.call-start = ((), (), s32[]{:S(2)}) async-start(), calls=%async_computation.14 | async-start | bytes 1474560 | tf_op jit(solution)/shard_map/reduce_scatter | solution.py:483
  267.7 20.1 %copy-start.13 = (bf16[6144,256]{1,0:T(8,128)(2,1)S(1)}, bf16[6144,256]{1,0:T(8,128)(2,1)}, u32[]{:S(2)}) copy-start(bf16[6144,256]{1,0:T(8,128)(2,1)} %copy-done.12) | copy-start | bytes 9437188
  287.8 4.3 copy-start.18
  287.8 4.3 copy-start.28
  292.1 81.3 %reduce-scatter.17.cloned.1.call-start = ((), (), s32[]{:S(2)}) async-start(), calls=%async_computation.13 | async-start | bytes 3538944 | tf_op jit(solution)/shard_map/reduce_scatter | solution.py:436
  295.7 124.0 %reduce-scatter.23.cloned.1.call-start = ((), (), s32[]{:S(2)}) async-start(), calls=%async_computation.16 | async-start | bytes 1474560 | tf_op jit(solution)/shard_map/reduce_scatter | solution.py:483
  295.7 2.9 copy-start.31
  301.6 135.5 %reduce-scatter.27.cloned.1.call-start = ((), (), s32[]{:S(2)}) async-start(), calls=%async_computation.21 | async-start | bytes 1474560
  305.5 67.9 %copy-start.24 = (f32[768]{0:T(1024)S(1)}, f32[768]{0:T(1024)}, u32[]{:S(2)}) copy-start(f32[768]{0:T(1024)} %param.20) | copy-start | bytes 9220
  305.5 70.5 %copy-start.27 = (f32[768]{0:T(1024)S(1)}, f32[768]{0:T(1024)}, u32[]{:S(2)}) copy-start(f32[768]{0:T(1024)} %get-tuple-element.94) | copy-start | bytes 9220
  306.9 167.2 %all-reduce.4.cloned.1.call-start = ((), (), s32[]{:S(2)}) async-start(), calls=%async_computation.22 | async-start | bytes 201728 | tf_op jit(solution)/shard_map/psum | solution.py:485
  307.5 190.3 %reduce-scatter.25.cloned.1.call-start = ((), (), s32[]{:S(2)}) async-start(), calls=%async_computation.20 | async-start | bytes 491520
  (14 other events, 22.0 us)
Sparse Core Ops, SparseCore 0:
  11.8 34.9 all-gather.9
  49.3 24.1 all-gather.7
  75.3 32.2 all-gather.13
  110.0 32.2 all-gather.11
  155.0 46.2 reduce-scatter.14
  204.9 46.2 reduce-scatter.12
  256.2 36.7 reduce-scatter.20
  295.4 29.1 reduce-scatter.18
  328.4 44.9 reduce-scatter.16
  376.1 29.8 reduce-scatter.22
  408.9 28.1 reduce-scatter.26
  440.8 33.2 all-reduce.3
  477.1 20.7 reduce-scatter.24

commit v2 on v1

--- a/solution.py
+++ b/solution.py
@@ -390,6 +390,231 @@
     )(gm, qkv, core, s, f, urev, pp, kern, seg, shift_w, skip, rate, in_b, out_c)
 
 
+MESH = pl.DeviceIdType.MESH
+
+
+class Place:
+    def __init__(self, n_dp, n_head, n_tensor):
+        self.n_dp, self.n_head, self.n_tensor = n_dp, n_head, n_tensor
+        self.dp = lax.axis_index("dp")
+        h, t = lax.axis_index("head"), lax.axis_index("tensor")
+        self.size = n_head * n_tensor
+        ph, xh, yt = h + 1 - 2 * (h % 2), (h + 2) % n_head, 1 - t
+        pxh = (ph + 2) % n_head
+        slot = lambda a, b: a * n_tensor + b
+        self.me, self.p, self.x, self.y, self.d = (
+            slot(h, t), slot(ph, t), slot(xh, t), slot(h, yt), slot(xh, yt),
+        )
+        self.px, self.py, self.pd = slot(pxh, t), slot(ph, yt), slot(pxh, yt)
+        self.to_p, self.to_x, self.to_y = {"head": ph}, {"head": xh}, {"tensor": yt}
+
+    def dp_peer(self, step):
+        return (self.dp + step) % self.n_dp
+
+    def barrier(self, over_dp):
+        sem = pltpu.get_barrier_semaphore()
+        for where in (self.to_p, self.to_x, self.to_y):
+            pl.semaphore_signal(sem, inc=1, device_id=where, device_id_type=MESH)
+        count = 3
+        if over_dp:
+            def greet(step, _):
+                pl.semaphore_signal(
+                    sem, inc=1, device_id={"dp": self.dp_peer(step)}, device_id_type=MESH
+                )
+                return 0
+
+            lax.fori_loop(1, self.n_dp, greet, 0)
+            count += self.n_dp - 1
+        pl.semaphore_wait(sem, count)
+
+
+def remote(src, dst, ssem, rsem, where):
+    return pltpu.make_async_remote_copy(
+        src_ref=src, dst_ref=dst, send_sem=ssem, recv_sem=rsem, device_id=where, device_id_type=MESH
+    )
+
+
+class GroupGather:
+    COPIES = 9
+
+    def __init__(self, place, ref, ssem, rsem):
+        self.ssem, self.rsem = ssem, rsem
+        half = ref.shape[1] // 2
+        top, low = pl.ds(0, half), pl.ds(half, half)
+        pc = place
+        full = lambda s: ref.at[s]
+        part = lambda s, rows: ref.at[s, rows]
+        self.out = [
+            (full(pc.me), pc.to_p), (full(pc.me), pc.to_x), (full(pc.me), pc.to_y),
+            (part(pc.x, top), pc.to_y), (part(pc.y, low), pc.to_x),
+            (full(pc.x), pc.to_p), (full(pc.y), pc.to_p),
+            (part(pc.d, top), pc.to_p), (part(pc.d, low), pc.to_p),
+        ]
+        self.into = [
+            full(pc.p), full(pc.x), full(pc.y), part(pc.d, top), part(pc.d, low),
+            full(pc.px), full(pc.py), part(pc.pd, top), part(pc.pd, low),
+        ]
+
+    def send(self, *which):
+        for i in which:
+            src, where = self.out[i]
+            remote(src, src, self.ssem.at[i], self.rsem.at[i], where).start()
+
+    def arrive(self, *which):
+        for i in which:
+            dst = self.into[i]
+            remote(dst, dst, self.ssem.at[i], self.rsem.at[i], self.out[i][1]).wait_recv()
+
+    def start(self):
+        self.send(1, 2, 0)
+
+    def middle(self):
+        self.arrive(1, 2)
+        self.send(3, 4, 5, 6)
+
+    def late(self):
+        self.arrive(3, 4)
+        self.send(7, 8)
+
+    def finish(self):
+        self.arrive(0, 5, 6, 7, 8)
+
+    def drain(self):
+        for i in range(self.COPIES):
+            src, where = self.out[i]
+            remote(src, src, self.ssem.at[i], self.rsem.at[i], where).wait_send()
+
+
+class DepthGather:
+    def __init__(self, place, ref, ssem, rsem):
+        self.place, self.ref, self.ssem, self.rsem = place, ref, ssem, rsem
+
+    def _copy(self, step, slot, peer):
+        return remote(
+            self.ref.at[slot], self.ref.at[slot], self.ssem.at[step], self.rsem.at[step], {"dp": peer}
+        )
+
+    def _loop(self, body):
+        def step(i, _):
+            body(i)
+            return 0
+
+        lax.fori_loop(1, self.place.n_dp, step, 0)
+
+    def start(self):
+        pc = self.place
+        self._loop(lambda i: self._copy(i, pc.dp, pc.dp_peer(i)).start())
+
+    def finish(self):
+        pc = self.place
+        source = lambda i: (pc.dp + pc.n_dp - i) % pc.n_dp
+        self._loop(lambda i: self._copy(i, source(i), pc.dp_peer(i)).wait_recv())
+
+    def drain(self):
+        pc = self.place
+        self._loop(lambda i: self._copy(i, pc.dp, pc.dp_peer(i)).wait_send())
+
+
+def joined(ref):
+    n, rows, columns = ref.shape
+    if rows % 16 == 0:
+        return ref[...].reshape(n * rows, columns)
+    parts = [ref[j].astype(jnp.float32) for j in range(n)]
+    return jnp.concatenate(parts, axis=0).astype(ref.dtype)
+
+
+def row_norm(x):
+    centred = x - jnp.mean(x, axis=1, keepdims=True)
+    inv = lax.rsqrt(jnp.mean(centred * centred, axis=1, keepdims=True) + 1e-05)
+    return centred * inv, inv
+
+
+def first_kernel(
+    axes, tok_ref, cot_ref, gain_ref, bias_ref, qkvo_ref, up_ref,
+    xn_all, cot_all, qkv_ref, wqkvo_all, wup_all, wupt_ref, wout_all,
+    wt_scr, gs, gr, cs, cr, os, orr, zs, zr, lsem,
+):
+    pc = Place(*axes)
+    pc.barrier(True)
+    chans = wout_all.shape[1]
+    own = tok_ref.shape[0]
+    keep_qkvo = pltpu.make_async_copy(qkvo_ref, wqkvo_all.at[pc.dp], lsem.at[0])
+    keep_up = pltpu.make_async_copy(up_ref, wup_all.at[pc.dp], lsem.at[1])
+    keep_qkvo.start()
+    keep_up.start()
+    z_qkvo = DepthGather(pc, wqkvo_all, zs.at[0], zr.at[0])
+    z_up = DepthGather(pc, wup_all, zs.at[1], zr.at[1])
+    xn_g = GroupGather(pc, xn_all, gs, gr)
+    cot_g = GroupGather(pc, cot_all, cs, cr)
+    out_g = GroupGather(pc, wout_all, os, orr)
+    keep_qkvo.wait()
+    z_qkvo.start()
+    keep_up.wait()
+    z_up.start()
+    hat, _ = row_norm(tok_ref[...].astype(jnp.float32))
+    xn_all[pc.me] = (hat * gain_ref[...] + bias_ref[...]).astype(jnp.bfloat16).T
+    xn_g.start()
+    cot_all[pc.me] = cot_ref[...].T
+    cot_g.start()
+    z_qkvo.finish()
+    wt_scr[...] = joined(wqkvo_all).T
+    wout_all[pc.me] = wt_scr[3 * chans :, :]
+    xn_g.middle()
+    xn_g.late()
+    out_g.start()
+    cot_g.middle()
+    xn_g.finish()
+    for s in range(pc.size):
+        y = mm(wt_scr[0 : 3 * chans, :], xn_all[s])
+        for h in range(own // LANES):
+            qkv_ref[pl.ds(s * (own // LANES) + h, 3 * chans, stride=pc.size * (own // LANES)), :] = y[
+                :, h * LANES : (h + 1) * LANES
+            ]
+    z_up.finish()
+    wupt_ref[...] = joined(wup_all).T
+    cot_g.late()
+    out_g.middle()
+    out_g.late()
+    cot_g.finish()
+    out_g.finish()
+    for work in (xn_g, cot_g, out_g, z_qkvo, z_up):
+        work.drain()
+
+
+def first_stage(axes, tokens, cot, gain, bias, qkvo, up):
+    n_dp, n_head, n_tensor = axes
+    group = n_head * n_tensor
+    own, feats = tokens.shape
+    chans = qkvo.shape[1] // 4
+    f32, bf16 = jnp.float32, jnp.bfloat16
+    sds = jax.ShapeDtypeStruct
+    vm = pl.BlockSpec(memory_space=pltpu.VMEM)
+    dma = pltpu.SemaphoreType.DMA
+    return pl.pallas_call(
+        functools.partial(first_kernel, axes),
+        out_shape=(
+            sds((group, feats, own), bf16),
+            sds((group, feats, own), bf16),
+            sds((3 * chans * group * own // LANES, LANES), f32),
+            sds((n_dp,) + qkvo.shape, bf16),
+            sds((n_dp,) + up.shape, bf16),
+            sds((up.shape[1], feats), bf16),
+            sds((group, chans, feats), bf16),
+        ),
+        in_specs=[vm] * 6,
+        out_specs=(vm,) * 7,
+        scratch_shapes=[
+            pltpu.VMEM((4 * chans, feats), bf16),
+            dma((9,)), dma((9,)), dma((9,)), dma((9,)), dma((9,)), dma((9,)),
+            dma((2, n_dp)), dma((2, n_dp)), dma((2,)),
+        ],
+        compiler_params=pltpu.CompilerParams(
+            collective_id=1, has_side_effects=True, vmem_limit_bytes=56 << 20
+        ),
+        name="first_stage",
+    )(tokens, cot, gain, bias, qkvo, up)
+
+
 from jax.sharding import PartitionSpec as P
 
 GROUP = ("head", "tensor")
@@ -426,12 +651,18 @@
 ):
     bf16, f32 = jnp.bfloat16, jnp.float32
     chans = q_weight.shape[1]
+    axes = (lax.axis_size("dp"), lax.axis_size("head"), lax.axis_size("tensor"))
     own = tokens.shape[0]
     feats = tokens.shape[1]
     gather = lambda w: lax.all_gather(w, "dp", axis=0, tiled=True)
-    w_joint = gather(jnp.concatenate([q_weight, k_weight, v_weight], axis=1))
-    w_out = lax.all_gather(gather(out_weight), GROUP, axis=1, tiled=True)
-    w_up, w_down = gather(up_weight), gather(down_weight)
+    packed = jnp.concatenate([q_weight, k_weight, v_weight, out_weight], axis=1)
+    xn1, cot, qkv, w_packed, w_up, w_up_t, w_out_t = first_stage(
+        axes, tokens, cotangent, norm1_gain[None], norm1_bias[None], packed, up_weight
+    )
+    w_joint = w_packed.reshape(feats, 4 * chans)[:, : 3 * chans]
+    w_up = w_up.reshape(feats, -1)
+    w_out = w_out_t.reshape(feats, feats).T
+    w_down = gather(down_weight)
     group_gather = lambda x: lax.all_gather(x, GROUP, axis=0, tiled=False)
     scatter = lambda x: lax.psum_scatter(x, GROUP, scatter_dimension=0, tiled=False).astype(f32)
     swap = lambda x: lax.all_to_all(x, GROUP, split_axis=0, concat_axis=0, tiled=True)
@@ -439,10 +670,7 @@
     g = cotangent.T
     column = lambda v: v[:, None]
     hat1, inv1 = norm_stats(x)
-    xn1 = group_gather((hat1 * column(norm1_gain) + column(norm1_bias)).astype(bf16))
-    cot = group_gather(g)
     group = xn1.shape[0]
-    qkv = jnp.einsum("gdt,dc->cgt", xn1, w_joint, preferred_element_type=f32)
     qkv = qkv.reshape(3, chans * group * own // LANES, LANES)
     mixed, *saved = mixer_fwd(
         qkv, seg_ids, shift_weight, skip_coef[None], decay_rate, in_coef, out_coef, un=16

time: 512 us -> 498 us (0.973)
  Pallas kernels: 32.3 us -> 79.8 us
  blocking collectives: 119 us -> 71.6 us
  local copies, waits for them, and re-layouts: 35.7 us -> 27.3 us
  other arithmetic: 16 us -> 9.09 us
    pallas_call x0 -> x1, Pallas kernels: none -> 47.6 us  [first_stage(): pl.pallas_call(functools.partial(first_kernel, axes), out_shape=(sds((gro...]
    all_gather x4 -> x1, blocking collectives: 66.6 us -> 19.7 us  [on_device(): gather = lambda w: lax.all_gather(w, 'dp', axis=0, tiled=True)]
    unnamed x15 -> x11, waiting for transfers between devices: 42.5 us -> 23.7 us
    reduce_scatter x2 -> x3, waiting for transfers between devices: 15.1 us -> 32.6 us  [on_device(): lax.psum_scatter(v, 'dp', scatter_dimension=0, tiled=True)]
    all_gather x3 -> x0, local copies, waits for them, and re-layouts: 8.61 us -> none  [the longest x2 7.81 us: on_device(): group_gather = lambda x: lax.all_gather(x, GROUP, axis=0, tiled=False)]
    unnamed x72 -> x64, local copies, waits for them, and re-layouts: 19.8 us -> 22.8 us
    all_gather x3 -> x1, waiting for transfers between devices: 14 us -> 15.3 us  [on_device(): group_gather = lambda x: lax.all_gather(x, GROUP, axis=0, tiled=False)]
  transfers between devices with their start and end apart: 14 -> 11, of which waited for: 10 -> 9; matrix products, arithmetic and copies ran while one was open for 11% -> 7% of each run, Pallas kernels for 6% -> 4%
where the time goes in v2:
time: 498 us; the launch traced here: 497 us
  waiting for transfers between devices  252 us (51%)
  Pallas kernels  79.8 us (16%)
  blocking collectives  71.6 us (14%)
  matrix products  38.7 us (8%)
  local copies, waits for them, and re-layouts  27.3 us (5%)
  between operations  14.5 us (3%)
  other arithmetic  9.09 us (2%)
    reduce_scatter x3, waiting for transfers between devices, on_device(): lax.psum_scatter(x, GROUP, scatter_dimension=0, tiled=False).astype(f32)  136 us
    pallas_call x1, Pallas kernels, first_stage(): pl.pallas_call(functools.partial(first_kernel, axes), out_shape=(sds((gro...  47.6 us
    psum x1, blocking collectives, on_device(): norms = lax.psum((gain1, bias1, gain2, bias2), ('dp', 'head', 'tensor'))  41.1 us
    psum x1, waiting for transfers between devices, on_device(): sums = lax.psum((dshift, drate, dinb, doutc, dskip[0]), 'dp')  37.2 us
    reduce_scatter x3, waiting for transfers between devices, on_device(): lax.psum_scatter(v, 'dp', scatter_dimension=0, tiled=True)  32.6 us
    unnamed x11, waiting for transfers between devices  23.7 us
    unnamed x64, local copies, waits for them, and re-layouts  22.8 us
    pallas_call x1, Pallas kernels, mixer_bwd(): pl.pallas_call(functools.partial(mixer_bwd_kernel, un), out_shape=(sds((n...  20.1 us
  transfers between devices with their start and end apart: 11, of which 9 were waited for; matrix products, arithmetic and copies ran while one was open for 7% of the time, Pallas kernels for 4%

profile of v2, /device:TPU:0, one launch (start us, length us, event | category | flops | bytes accessed | tf_op | source)
XLA Modules:
  0.0 496.9 jit_solution(2470943636658216522)
XLA Ops:
  9.8 1.7 pad_maximum_fusion.qkvo_ref
  11.5 47.6 %first_stage.1 = (bf16[8,768,256]{2,1,0:T(8,128)(2,1)}, bf16[8,768,256]{2,1,0:T(8,128)(2,1)}, f32[4608,128]{1,0:T(8,128)}, bf16[4,192,384]{2,1,0:T(8,128)(2,1)},...) custom-call(bf16[256,768]{1,0:T(8,128)(2,1)} %tok_ref.1, ...), custom_call_target="tpu_custom_call" | custom-call | tf_op jit(solution)/shard_map/first_stage/pallas_call | solution.py:593
  59.0 1.7 copy-done
  65.0 12.2 %mixer_fwd.1 = (bf16[8,96,256]{2,1,0:T(8,128)(2,1)}, f32[1536,128]{1,0:T(8,128)S(1)}, f32[1536,128]{1,0:T(8,128)S(1)}, f32[1536,128]{1,0:T(8,128)S(1)}, bf16[153...) custom-call(f32[3,1536,128]{2,1,0:T(8,128)S(1)} %bitcast.154, s32[1,2048]{1,0:T(1,128)S(1)} %copy-done.9, ...), custom_call_target="tpu_custom_call" | custom-call | tf_op jit(solution)/shard_map/mixer_fwd/pallas_call | solution.py:189
  81.3 3.6 all-to-all-start
  85.1 7.1 %all-to-all-done = bf16[8,96,256]{2,1,0:T(8,128)(2,1)S(1)} async-done(((bf16[8,96,256]{2,1,0:T(8,128)(2,1)}), bf16[8,96,256]{2,1,0:T(8,128)(2,1)S(1)}, u32[]{:S(2)}, u32[]{:S(2)}) %all-to-all-start) | async-done | bytes 393248 | tf_op jit(solution)/shard_map/all_to_all | solution.py:668
  92.2 1.8 fusion.44
  95.3 19.7 %all_gather.11 = bf16[768,384]{1,0:T(8,128)(2,1)S(1)} all-gather(bf16[192,384]{1,0:T(8,128)(2,1)S(1)} %copy-done.17), channel_id=1, replica_groups=mesh['dp'=4,'head'=4,'tensor'=2] {'dp'}, dimensions={0}, use_global_device_ids=true | all-gather | bytes 737280 | tf_op jit(solution)/shard_map/all_gather | solution.py:657
  115.0 15.3 %all-gather.3.cloned.1.call-done = bf16[6144,256]{1,0:T(8,128)(2,1)} async-done(((bf16[768,256]{1,0:T(8,128)(2,1)}), bf16[6144,256]{1,0:T(8,128)(2,1)}) %all-gather.3.cloned.1.call-update) | async-done | bytes 3145744 | tf_op jit(solution)/shard_map/all_gather | solution.py:666
  130.3 5.2 %fusion.9 = (bf16[8,384,256]{2,1,0:T(8,128)(2,1)}, f32[384,8,256]{2,0,1:T(8,128)S(1)}) fusion(bf16[768,384,1]{1,0,2:T(8,128)(2,1)} %bitcast.166, bf16[8,768,256]{2,1,0:T(8,128)(2,1)} %bitcast.161), kind=kOutput, calls=%fused_computation.12 | convolution fusion | flops 1211891712 | bytes 8454144 | tf_op jit(solution)/shard_map/gdt,df->gft/dot_general | solution.py:682
  135.5 2.5 fusion.5
  139.2 3.4 convert_bitcast_fusion.1
  142.7 4.9 convert_bitcast_fusion.2
  148.8 40.3 %reduce-scatter.13.cloned.1.call-done = bf16[1,768,256]{2,1,0:T(8,128)(2,1)} async-done(((bf16[8,768,256]{2,1,0:T(8,128)(2,1)}), bf16[1,768,256]{2,1,0:T(8,128)(2,1)}) %reduce-scatter.13.cloned.1.call-update) | async-done | bytes 393232 | tf_op jit(solution)/shard_map/reduce_scatter | solution.py:667
  190.4 48.6 %reduce-scatter.11.cloned.1.call-done = bf16[1,768,256]{2,1,0:T(8,128)(2,1)} async-done(((bf16[8,768,256]{2,1,0:T(8,128)(2,1)}), bf16[1,768,256]{2,1,0:T(8,128)(2,1)}) %reduce-scatter.11.cloned.1.call-update) | async-done | bytes 393232 | tf_op jit(solution)/shard_map/reduce_scatter | solution.py:667
  239.1 1.5 fusion.32
  240.5 1.6 convolution_convert_fusion
  242.7 10.8 %all_to_all.10.gm_ref = bf16[8,96,256]{2,1,0:T(8,128)(2,1)} all-to-all(bf16[8,96,256]{2,1,0:T(8,128)(2,1)S(1)} %bitcast.158), channel_id=1, replica_groups=mesh['dp'=4,'head'=4,'tensor'=2] {'head','tensor'}, dimensions={0} | all-to-all | bytes 786432 | tf_op jit(solution)/shard_map/all_to_all | solution.py:668
  253.6 20.1 %mixer_bwd.1 = (bf16[8,3,96,256]{3,2,1,0:T(8,128)(2,1)}, f32[4,96]{1,0:T(4,128)}, f32[64,96]{1,0:T(8,128)}, f32[64,96]{1,0:T(8,128)}, f32[64,96]{1,0:T(8,128)}, /*index=5*/f32[1,96]{1,0:T(1,128)}) custom-call(bf16[8,96,256]{2,1,0:T(8,128)(2,1)} %all_to_all.10.gm_ref, f32[3,1536,128]{2,1,0:T(8,128)} %bitcast.153, f32[1536,128]{1,0:T(8,128)} %copy-done.1, ...), custom_call_target="tpu_custom_call" | custom-call | tf_op jit(solution)/shard_map/mixer_bwd/pallas_call | solution.py:372
  273.7 4.2 convolution_bitcast_fusion.2
  278.0 4.6 convert_bitcast_fusion
  282.6 5.3 %convolution_bitcast_fusion.1 = f32[768,384]{1,0:T(8,128)} fusion(bf16[8,768,256]{2,1,0:T(8,128)(2,1)} %bitcast.162, bf16[8,384,256]{2,1,0:T(8,128)(2,1)} %copy-done.26), kind=kOutput, calls=%fused_computation.18 | convolution fusion | flops 1207959552 | bytes 5898240 | tf_op jit(solution)/shard_map/gdt,gft->df/dot_general | solution.py:692
  288.0 4.7 convolution_bitcast_fusion
  294.6 1.8 copy.63
  296.4 14.3 %reduce-scatter.17.cloned.1.call-done = f32[192,288]{1,0:T(8,128)} async-done(((f32[768,288]{1,0:T(8,128)}), f32[192,288]{1,0:T(8,128)}) %reduce-scatter.17.cloned.1.call-update) | async-done | bytes 221200 | tf_op jit(solution)/shard_map/reduce_scatter | solution.py:711
  310.7 1.9 fusion.43
  312.5 46.7 %reduce-scatter.15.cloned.1.call-done = bf16[1,768,256]{2,1,0:T(8,128)(2,1)} async-done(((bf16[8,768,256]{2,1,0:T(8,128)(2,1)}), bf16[1,768,256]{2,1,0:T(8,128)(2,1)}) %reduce-scatter.15.cloned.1.call-update) | async-done | bytes 393232 | tf_op jit(solution)/shard_map/reduce_scatter | solution.py:667
  359.3 1.5 fusion.36
  363.4 41.1 %all-reduce = (f32[768]{0:T(1024)}, f32[768]{0:T(1024)}, f32[768]{0:T(1024)}, f32[768]{0:T(1024)}) all-reduce(f32[768]{0:T(1024)S(1)} %get-tuple-element.91, f32[768]{0:T(1024)S(1)} %convert_reduce_fusion, f32[768]{0:T(1024)S(1)} %get-tuple-element.89, ...), channel_id=1, replica_groups=mesh['dp'=4,'head'=4,'tensor'=2] {'dp','head','tensor'}, use_global_device_ids=true, to_apply=%region_12.0 | all-reduce | flops 3072 | bytes 24576 | tf_op jit(solution)/shard_map/psum | solution.py:714
  404.5 18.4 %reduce-scatter.23.cloned.1.call-done = f32[192,384]{1,0:T(8,128)} async-done(((f32[768,384]{1,0:T(8,128)}), f32[192,384]{1,0:T(8,128)}) %reduce-scatter.23.cloned.1.call-update) | async-done | bytes 294928 | tf_op jit(solution)/shard_map/reduce_scatter | solution.py:711
  422.8 37.2 %all-reduce.4.cloned.1.call-done = (f32[4,96]{1,0:T(4,128)}, f32[64,96]{1,0:T(8,128)}, f32[64,96]{1,0:T(8,128)}, f32[64,96]{1,0:T(8,128)}, f32[96]{0:T(128)}) async-done(((f32[4,96]{1,0:T(4,128)}, f32[64,96]{1,0:T(8,128)}, f32[64,96]{1,0:T(8,128)}, f32[64,96]{1,0:T(8,128)}, f32[96]{0:T(128)}), (f32[4,96]{1,0:T(4,128)}, f32[64,96]{1,0:T(8,128)}, f32[64,96]{1,0:T(8,128)}, f32[64,96]{1,0:T(8,128)}, ...) | async-done | bytes 75664 | tf_op jit(solution)/shard_map/psum | solution.py:713
  460.0 23.6 %reduce-scatter.25.cloned.1.call-done = f32[192,96]{1,0:T(8,128)} async-done(((f32[768,96]{1,0:T(8,128)}), f32[192,96]{1,0:T(8,128)}) %reduce-scatter.25.cloned.1.call-update) | async-done | bytes 73744
  (102 shorter events, 27.9 us)
Async XLA Ops:
  7.2 77.8 %copy-start.14 = (bf16[256,768]{1,0:T(8,128)(2,1)S(1)}, bf16[256,768]{1,0:T(8,128)(2,1)}, u32[]{:S(2)}) copy-start(bf16[256,768]{1,0:T(8,128)(2,1)} %tok_ref.1) | copy-start | bytes 1179652
  59.0 1.7 copy-start
  60.7 0.8 copy-start.5
  61.4 0.8 copy-start.6
  77.2 0.9 copy-start.1
  78.0 1.0 copy-start.2
  79.0 0.9 copy-start.3
  81.3 12.9 %copy-start.18 = (f32[768]{0:T(1024)S(1)}, f32[768]{0:T(1024)}, u32[]{:S(2)}) copy-start(f32[768]{0:T(1024)} %param.22) | copy-start | bytes 9220
  81.3 12.9 %copy-start.20 = (f32[768]{0:T(1024)S(1)}, f32[768]{0:T(1024)}, u32[]{:S(2)}) copy-start(f32[768]{0:T(1024)} %param.23) | copy-start | bytes 9220
  81.3 11.0 %all-to-all-start = ((bf16[8,96,256]{2,1,0:T(8,128)(2,1)}), bf16[8,96,256]{2,1,0:T(8,128)(2,1)S(1)}, u32[]{:S(2)}, u32[]{:S(2)}) async-start(bf16[8,96,256]{2,1,0:T(8,128)(2,1)} %get-tuple-element.38), calls=%async_computation | async-start | bytes 786432 | tf_op jit(solution)/shard_map/all_to_all | solution.py:668
  84.9 10.4 %copy-start.17 = (bf16[192,384]{1,0:T(8,128)(2,1)S(1)}, bf16[192,384]{1,0:T(8,128)(2,1)}, u32[]{:S(2)}) copy-start(bf16[192,384]{1,0:T(8,128)(2,1)} %param.29) | copy-start | bytes 442372
  84.9 45.4 %all-gather.3.cloned.1.call-start = ((), (), s32[]{:S(2)}) async-start(), calls=%async_computation.17 | async-start | bytes 3538944 | tf_op jit(solution)/shard_map/all_gather | solution.py:666
  95.3 93.8 %reduce-scatter.13.cloned.1.call-start = ((), (), s32[]{:S(2)}) async-start(), calls=%async_computation.11 | async-start | bytes 3538944 | tf_op jit(solution)/shard_map/reduce_scatter | solution.py:667
  130.3 5.2 %copy-start.21 = (bf16[8,768,256]{2,1,0:T(8,128)(2,1)S(1)}, bf16[8,768,256]{2,1,0:T(8,128)(2,1)}, u32[]{:S(2)}) copy-start(bf16[8,768,256]{2,1,0:T(8,128)(2,1)} %get-tuple-element.40) | copy-start | bytes 9437188
  135.5 3.7 copy-start.24
  138.0 1.2 copy-start.26
  142.7 96.4 %reduce-scatter.11.cloned.1.call-start = ((), (), s32[]{:S(2)}) async-start(), calls=%async_computation.10 | async-start | bytes 3538944 | tf_op jit(solution)/shard_map/reduce_scatter | solution.py:667
  147.6 1.0 copy-start.15
  147.6 146.9 %reduce-scatter.19.cloned.1.call-start = ((), (), s32[]{:S(2)}) async-start(), calls=%async_computation.14 | async-start | bytes 1327104 | tf_op jit(solution)/shard_map/reduce_scatter | solution.py:699
  240.5 1.7 copy-start.16
  242.2 68.5 %reduce-scatter.17.cloned.1.call-start = ((), (), s32[]{:S(2)}) async-start(), calls=%async_computation.13 | async-start | bytes 1474560 | tf_op jit(solution)/shard_map/reduce_scatter | solution.py:711
  253.6 20.1 %copy-start.22 = (bf16[8,768,256]{2,1,0:T(8,128)(2,1)S(1)}, bf16[8,768,256]{2,1,0:T(8,128)(2,1)}, u32[]{:S(2)}) copy-start(bf16[8,768,256]{2,1,0:T(8,128)(2,1)} %get-tuple-element.49) | copy-start | bytes 9437188
  273.7 4.3 copy-start.23
  277.9 81.3 %reduce-scatter.15.cloned.1.call-start = ((), (), s32[]{:S(2)}) async-start(), calls=%async_computation.12 | async-start | bytes 3538944 | tf_op jit(solution)/shard_map/reduce_scatter | solution.py:667
  282.6 5.4 %copy-start.25 = (bf16[8,384,256]{2,1,0:T(8,128)(2,1)S(1)}, bf16[8,384,256]{2,1,0:T(8,128)(2,1)}, u32[]{:S(2)}) copy-start(bf16[8,384,256]{2,1,0:T(8,128)(2,1)} %get-tuple-element.111) | copy-start | bytes 4718596
  282.6 121.9 %reduce-scatter.21.cloned.1.call-start = ((), (), s32[]{:S(2)}) async-start(), calls=%async_computation.15 | async-start | bytes 1474560 | tf_op jit(solution)/shard_map/reduce_scatter | solution.py:711
  288.0 134.9 %reduce-scatter.23.cloned.1.call-start = ((), (), s32[]{:S(2)}) async-start(), calls=%async_computation.16 | async-start | bytes 1474560 | tf_op jit(solution)/shard_map/reduce_scatter | solution.py:711
  292.7 1.6 copy-start.13
  292.7 66.5 %copy-start.19 = (f32[768]{0:T(1024)S(1)}, f32[768]{0:T(1024)}, u32[]{:S(2)}) copy-start(f32[768]{0:T(1024)} %param.20) | copy-start | bytes 9220
  292.8 167.3 %all-reduce.4.cloned.1.call-start = ((), (), s32[]{:S(2)}) async-start(), calls=%async_computation.19 | async-start | bytes 201728 | tf_op jit(solution)/shard_map/psum | solution.py:713
  294.1 189.5 %reduce-scatter.25.cloned.1.call-start = ((), (), s32[]{:S(2)}) async-start(), calls=%async_computation.18 | async-start | bytes 491520
  359.3 3.9 copy-start.12
  (6 other events, 4.1 us)
Sparse Core Ops, SparseCore 0:
  95.4 34.8 all-gather.2
  142.8 46.2 reduce-scatter.12
  192.8 46.2 reduce-scatter.10
  242.3 36.8 reduce-scatter.18
  281.4 29.1 reduce-scatter.16
  314.3 44.9 reduce-scatter.14
  362.1 29.8 reduce-scatter.20
  394.9 27.8 reduce-scatter.22
  426.7 33.3 all-reduce.3
  462.8 20.7 reduce-scatter.24

commit v3 on v2

--- a/solution.py
+++ b/solution.py
@@ -411,19 +411,27 @@
     def dp_peer(self, step):
         return (self.dp + step) % self.n_dp
 
-    def barrier(self, over_dp):
+    def barrier(self, whole_group, over_dp):
         sem = pltpu.get_barrier_semaphore()
-        for where in (self.to_p, self.to_x, self.to_y):
+
+        def greet(where):
             pl.semaphore_signal(sem, inc=1, device_id=where, device_id_type=MESH)
-        count = 3
+
+        if whole_group:
+            for i in range(1, self.size):
+                peer = (self.me + i) % self.size
+                greet({"head": peer // self.n_tensor, "tensor": peer % self.n_tensor})
+            count = self.size - 1
+        else:
+            for where in (self.to_p, self.to_x, self.to_y):
+                greet(where)
+            count = 3
         if over_dp:
-            def greet(step, _):
-                pl.semaphore_signal(
-                    sem, inc=1, device_id={"dp": self.dp_peer(step)}, device_id_type=MESH
-                )
+            def step(i, _):
+                greet({"dp": self.dp_peer(i)})
                 return 0
 
-            lax.fori_loop(1, self.n_dp, greet, 0)
+            lax.fori_loop(1, self.n_dp, step, 0)
             count += self.n_dp - 1
         pl.semaphore_wait(sem, count)
 
@@ -535,7 +543,7 @@
     wt_scr, gs, gr, cs, cr, os, orr, zs, zr, lsem,
 ):
     pc = Place(*axes)
-    pc.barrier(True)
+    pc.barrier(False, True)
     chans = wout_all.shape[1]
     own = tok_ref.shape[0]
     keep_qkvo = pltpu.make_async_copy(qkvo_ref, wqkvo_all.at[pc.dp], lsem.at[0])
@@ -615,106 +623,514 @@
     )(tokens, cot, gain, bias, qkvo, up)
 
 
-from jax.sharding import PartitionSpec as P
-
-GROUP = ("head", "tensor")
-
-
-def norm_stats(x):
-    centred = x - jnp.mean(x, axis=0, keepdims=True)
-    spread = jnp.mean(centred * centred, axis=0, keepdims=True)
-    inv = lax.rsqrt(spread + 1e-05)
-    return centred * inv, inv
-
-
-def norm_back(grad, gain, hat, inv):
+class GroupReduce:
+    def __init__(self, place, part, land, half_land, last_land, ssem, rsem):
+        pc = place
+        self.part, self.land, self.half_land, self.last_land = part, land, half_land, last_land
+        self.ssem, self.rsem = ssem, rsem
+        half = part.shape[1] // 2
+        self.top, self.low = pl.ds(0, half), pl.ds(half, half)
+        self.mine = [pc.d, pc.x, pc.y, pc.me]
+        theirs = [pc.pd, pc.px, pc.py, pc.p]
+        self.copies = [(part.at[theirs[i]], land.at[i], pc.to_p) for i in range(4)] + [
+            (part.at[pc.d, self.top], half_land.at[0], pc.to_x),
+            (part.at[pc.d, self.low], half_land.at[1], pc.to_y),
+            (part.at[pc.x], last_land.at[0], pc.to_x),
+            (part.at[pc.y], last_land.at[1], pc.to_y),
+        ]
+        self.pc = pc
+
+    COPIES = 8
+
+    def _copy(self, i):
+        src, dst, where = self.copies[i]
+        return remote(src, dst, self.ssem.at[i], self.rsem.at[i], where)
+
+    def give(self, i):
+        self._copy(i).start()
+
+    def pair(self, i):
+        self._copy(i).wait_recv()
+        s = self.mine[i]
+        self.part[s] = (self.part[s].astype(jnp.float32) + self.land[i].astype(jnp.float32)).astype(
+            self.part.dtype
+        )
+
+    def far(self):
+        self._copy(4).start()
+        self._copy(5).start()
+
+    def near(self):
+        for i, s, rows in ((4, self.pc.y, self.top), (5, self.pc.x, self.low)):
+            self._copy(i).wait_recv()
+            self.part[s, rows] = (
+                self.part[s, rows].astype(jnp.float32) + self.half_land[i - 4].astype(jnp.float32)
+            ).astype(self.part.dtype)
+            self._copy(7 if i == 4 else 6).start()
+
+    def total(self):
+        self._copy(6).wait_recv()
+        self._copy(7).wait_recv()
+        return (
+            self.part[self.pc.me].astype(jnp.float32)
+            + self.last_land[0].astype(jnp.float32)
+            + self.last_land[1].astype(jnp.float32)
+        )
+
+    def drain(self):
+        for i in range(self.COPIES):
+            self._copy(i).wait_send()
+
+    @staticmethod
+    def scratch(group, rows, columns):
+        bf16 = jnp.bfloat16
+        return [
+            pltpu.VMEM((group, rows, columns), bf16),
+            pltpu.VMEM((4, rows, columns), bf16),
+            pltpu.VMEM((2, rows // 2, columns), bf16),
+            pltpu.VMEM((2, rows, columns), bf16),
+            pltpu.SemaphoreType.DMA((8,)),
+            pltpu.SemaphoreType.DMA((8,)),
+        ]
+
+
+class GroupSwap:
+    def __init__(self, place, src, dst, ssem, rsem, lsem):
+        self.pc, self.src, self.dst, self.ssem, self.rsem, self.lsem = place, src, dst, ssem, rsem, lsem
+
+    def _peer(self, i):
+        return (self.pc.me + i) % self.pc.size
+
+    def _copy(self, i, slot):
+        peer = self._peer(i)
+        where = {"head": peer // self.pc.n_tensor, "tensor": peer % self.pc.n_tensor}
+        return remote(self.src.at[peer], self.dst.at[slot], self.ssem.at[i], self.rsem.at[i], where)
+
+    def _own(self):
+        return pltpu.make_async_copy(self.src.at[self.pc.me], self.dst.at[self.pc.me], self.lsem)
+
+    def start(self):
+        for i in range(1, self.pc.size):
+            self._copy(i, self.pc.me).start()
+        self._own().start()
+
+    def finish(self):
+        for i in range(1, self.pc.size):
+            self._copy(i, (self.pc.me + self.pc.size - i) % self.pc.size).wait_recv()
+        self._own().wait()
+
+    def drain(self):
+        for i in range(1, self.pc.size):
+            self._copy(i, self.pc.me).wait_send()
+
+
+class DepthReduce:
+    def __init__(self, place, src, land, ssem, rsem):
+        self.place, self.src, self.land, self.ssem, self.rsem = place, src, land, ssem, rsem
+
+    def _copy(self, step, mine, slot, peer):
+        return remote(
+            self.src.at[mine], self.land.at[slot], self.ssem.at[step], self.rsem.at[step], {"dp": peer}
+        )
+
+    def _loop(self, body, start):
+        return lax.fori_loop(1, self.place.n_dp, body, start)
+
+    def start(self):
+        pc = self.place
+
+        def step(i, _):
+            self._copy(i, pc.dp_peer(i), pc.dp, pc.dp_peer(i)).start()
+            return 0
+
+        self._loop(step, 0)
+
+    def total(self):
+        pc = self.place
+
+        def step(i, acc):
+            source = (pc.dp + pc.n_dp - i) % pc.n_dp
+            self._copy(i, source, source, pc.dp_peer(i)).wait_recv()
+            return acc + self.land[source].astype(jnp.float32)
+
+        return self._loop(step, self.src[pc.dp].astype(jnp.float32))
+
+    def drain(self):
+        pc = self.place
+
+        def step(i, _):
+            self._copy(i, pc.dp_peer(i), pc.dp, pc.dp_peer(i)).wait_send()
+            return 0
+
+        self._loop(step, 0)
+
+
+def split_rows(ref, value):
+    n, rows, columns = ref.shape
+    if rows % 16 == 0:
+        ref[...] = value.astype(ref.dtype).reshape(n, rows, columns)
+    else:
+        for j in range(n):
+            ref[j] = value[j * rows : (j + 1) * rows].astype(ref.dtype)
+
+
+def row_norm_back(grad, gain, hat, inv):
     scaled = grad * gain
     return inv * (
         scaled
-        - jnp.mean(scaled, axis=0, keepdims=True)
-        - hat * jnp.mean(scaled * hat, axis=0, keepdims=True)
+        - jnp.mean(scaled, axis=1, keepdims=True)
+        - hat * jnp.mean(scaled * hat, axis=1, keepdims=True)
     )
-
-
-def lanes_sum(x):
-    return jnp.sum(x, axis=1)
 
 
 def gelu_pair(pre):
     cdf = 0.5 * (1.0 + lax.erf(pre * 0.7071067811865476))
     return pre * cdf, cdf + pre * (0.3989422804014327 * jnp.exp(-0.5 * pre * pre))
+
+
+def middle_kernel(
+    axes, mixed_ref, tok_ref, cot_ref, cot_all, woutt_ref, wup_ref, wupt_ref, down_ref, gain_ref, bias_ref,
+    hid_ref, ghid_ref, gmix_all, mlp_part, down_part, up_ref, out_part, norm_ref,
+    mixed_in, xn_all, wdown_all, wdownt, hat_scr, act_all, gpre_all, gm_scr, up_part, up_land,
+    part, land, half_land, last_land, rs, rr, gs, gr, ms, mr, bs, br, zs, zr, us, ur, lsem,
+):
+    pc = Place(*axes)
+    pc.barrier(True, True)
+    f32, bf16 = jnp.float32, jnp.bfloat16
+    group, chans, own = mixed_in.shape
+    feats = group * chans
+    own_down = pltpu.make_async_copy(down_ref, wdown_all.at[pc.dp], lsem.at[0])
+    own_down.start()
+    swap_in = GroupSwap(pc, mixed_ref, mixed_in, ms, mr, lsem.at[1])
+    swap_in.start()
+    own_down.wait()
+    z_down = DepthGather(pc, wdown_all, zs, zr)
+    z_down.start()
+    xn_g = GroupGather(pc, xn_all, gs, gr)
+    red = GroupReduce(pc, part, land, half_land, last_land, rs, rr)
+    x = tok_ref[...].astype(f32)
+    swap_in.finish()
+    mixed_t = mixed_in[...].reshape(feats, own)
+    wout_t = woutt_ref[...].reshape(feats, feats)
+    hidden = x + mm(mixed_t, wout_t, TN)
+    hid_ref[...] = hidden
+    hat, inv = row_norm(hidden)
+    xn_all[pc.me] = (hat * gain_ref[...] + bias_ref[...]).astype(bf16).T
+    xn_g.start()
+    hat_scr[...] = hat
+    z_down.finish()
+    w_down = joined(wdown_all)
+    wdownt[...] = w_down.T
+    w_up = joined(wup_ref)
+
+    def chunk(s):
+        act, slope = gelu_pair(mm(wupt_ref[...], xn_all[s]))
+        act_all[s] = act.astype(bf16)
+        grad_act = mm(wdownt[...], cot_all[s])
+        grad_pre = (grad_act * slope).astype(bf16)
+        gpre_all[s] = grad_pre
+        part[s] = mm(w_up, grad_pre).astype(bf16)
+
+    chunk(pc.me)
+    xn_g.arrive(0)
+    chunk(pc.p)
+    red.give(3)
+    xn_g.middle()
+    chunk(pc.x)
+    xn_g.late()
+    chunk(pc.y)
+    xn_g.arrive(5)
+    chunk(pc.px)
+    red.give(1)
+    xn_g.arrive(6)
+    chunk(pc.py)
+    red.give(2)
+    chunk(pc.d)
+    xn_g.arrive(7, 8)
+    chunk(pc.pd)
+    red.give(0)
+    red.pair(1)
+    red.pair(2)
+    red.pair(0)
+    red.far()
+    red.pair(3)
+    grad_up = jnp.zeros((feats, wupt_ref.shape[0]), f32)
+    for s in range(group):
+        grad_up = grad_up + mm(xn_all[s], gpre_all[s], NT)
+    split_rows(up_part, grad_up)
+    z_up = DepthReduce(pc, up_part, up_land, us, ur)
+    z_up.start()
+    red.near()
+    for s in range(group):
+        mlp_part[s] = mm(w_down, act_all[s]).astype(bf16)
+    grad_down = jnp.zeros((feats, wupt_ref.shape[0]), f32)
+    for s in range(group):
+        grad_down = grad_down + mm(cot_all[s], act_all[s], NT)
+    split_rows(down_part, grad_down)
+    grad_xn = red.total().T
+    norm_ref[0:1, :] = jnp.sum(grad_xn * hat_scr[...], axis=0, keepdims=True)
+    norm_ref[1:2, :] = jnp.sum(grad_xn, axis=0, keepdims=True)
+    grad_hidden = cot_ref[...].astype(f32) + row_norm_back(grad_xn, gain_ref[...], hat_scr[...], inv)
+    ghid_ref[...] = grad_hidden
+    grad_mix = grad_hidden.astype(bf16)
+    gm_scr[...] = mm(wout_t, grad_mix, NT).astype(bf16).reshape(group, chans, own)
+    swap_out = GroupSwap(pc, gm_scr, gmix_all, bs, br, lsem.at[2])
+    swap_out.start()
+    out_part[...] = mm(mixed_t, grad_mix).astype(bf16).reshape(group, chans, feats)
+    swap_out.finish()
+    up_ref[...] = z_up.total()
+    for work in (swap_in, z_down, xn_g, red, z_up, swap_out):
+        work.drain()
+
+
+def middle_stage(axes, mixed, tokens, cot_own, cot_all, wout_t, wup, wup_t, down, gain, bias):
+    n_dp, n_head, n_tensor = axes
+    group = n_head * n_tensor
+    own, feats = tokens.shape
+    _, chans, _ = mixed.shape
+    rows, units = down.shape
+    f32, bf16 = jnp.float32, jnp.bfloat16
+    sds = jax.ShapeDtypeStruct
+    vm = pl.BlockSpec(memory_space=pltpu.VMEM)
+    dma = pltpu.SemaphoreType.DMA
+    return pl.pallas_call(
+        functools.partial(middle_kernel, axes),
+        out_shape=(
+            sds((own, feats), f32),
+            sds((own, feats), f32),
+            sds((group, chans, own), bf16),
+            sds((group, feats, own), bf16),
+            sds((n_dp, rows, units), bf16),
+            sds((rows, units), f32),
+            sds((group, chans, feats), bf16),
+            sds((2, feats), f32),
+        ),
+        in_specs=[vm] * 10,
+        out_specs=(vm,) * 8,
+        scratch_shapes=[
+            pltpu.VMEM((group, chans, own), bf16),
+            pltpu.VMEM((group, feats, own), bf16),
+            pltpu.VMEM((n_dp, rows, units), bf16),
+            pltpu.VMEM((units, feats), bf16),
+            pltpu.VMEM((own, feats), f32),
+            pltpu.VMEM((group, units, own), bf16),
+            pltpu.VMEM((group, units, own), bf16),
+            pltpu.VMEM((group, chans, own), bf16),
+            pltpu.VMEM((n_dp, rows, units), bf16),
+            pltpu.VMEM((n_dp, rows, units), bf16),
+            *GroupReduce.scratch(group, feats, own),
+            dma((9,)), dma((9,)), dma((8,)), dma((8,)), dma((8,)), dma((8,)),
+            dma((n_dp,)), dma((n_dp,)), dma((n_dp,)), dma((n_dp,)), dma((3,)),
+        ],
+        compiler_params=pltpu.CompilerParams(
+            collective_id=2, has_side_effects=True, vmem_limit_bytes=60 << 20
+        ),
+        name="middle_stage",
+    )(mixed, tokens, cot_own, cot_all, wout_t, wup, wup_t, down, gain, bias)
+
+
+class GroupSpread:
+    def __init__(self, place, ref, ssem, rsem):
+        self.pc, self.ref, self.ssem, self.rsem = place, ref, ssem, rsem
+
+    def _copy(self, i, slot):
+        peer = (self.pc.me + i) % self.pc.size
+        where = {"head": peer // self.pc.n_tensor, "tensor": peer % self.pc.n_tensor}
+        return remote(self.ref.at[slot], self.ref.at[slot], self.ssem.at[i], self.rsem.at[i], where)
+
+    def start(self):
+        for i in range(1, self.pc.size):
+            self._copy(i, self.pc.me).start()
+
+    def finish(self):
+        for i in range(1, self.pc.size):
+            self._copy(i, (self.pc.me + self.pc.size - i) % self.pc.size).wait_recv()
+
+    def drain(self):
+        for i in range(1, self.pc.size):
+            self._copy(i, self.pc.me).wait_send()
+
+
+RATE, INB, OUTC, TAPS, SKIP, PARAM_ROWS = 0, 64, 128, 192, 208, 224
+
+
+def last_kernel(
+    axes, dqkv_ref, xn_all, wqkvo_ref, mlp_hbm, out_hbm, down_ref, hid_ref, ghid_ref, tok_ref, gain_ref, norm2_ref,
+    dsw_ref, drate_ref, dinb_ref, doutc_ref, dskip_ref,
+    res_ref, gx_ref, g1_ref, b1_ref, g2_ref, b2_ref, wq_ref, wk_ref, wv_ref, wo_ref, wd_ref,
+    sw_ref, rate_ref, inb_ref, outc_ref, skip_ref,
+    w_part, w_land, d_land, p_all, n_all, m_all,
+    xp, xl, xh, xe, xs, xr, op, ol, oh, oe, os, orr, mp, ml, mh, me, ms, mr,
+    ds, dr, ws, wr, ps, pr, ns, nr, qs, qr, lsem,
+):
+    pc = Place(*axes)
+    f32, bf16 = jnp.float32, jnp.bfloat16
+    load_out = pltpu.make_async_copy(out_hbm, op, lsem.at[0])
+    load_mlp = pltpu.make_async_copy(mlp_hbm, mp, lsem.at[1])
+    load_out.start()
+    load_mlp.start()
+    group, chans, feats = out_hbm.shape
+    own = tok_ref.shape[0]
+    pc.barrier(True, True)
+    z_down = DepthReduce(pc, down_ref, d_land, ds, dr)
+    z_down.start()
+    p_all[pc.dp] = jnp.zeros(p_all.shape[1:], bf16)
+    for at, ref in ((RATE, drate_ref), (INB, dinb_ref), (OUTC, doutc_ref), (TAPS, dsw_ref), (SKIP, dskip_ref)):
+        p_all[pc.dp, at : at + ref.shape[0], 0:chans] = ref[...].astype(bf16)
+    z_par = DepthGather(pc, p_all, ps, pr)
+    z_par.start()
+    red_o = GroupReduce(pc, op, ol, oh, oe, os, orr)
+    red_x = GroupReduce(pc, xp, xl, xh, xe, xs, xr)
+    red_m = GroupReduce(pc, mp, ml, mh, me, ms, mr)
+    load_out.wait()
+    for i in range(4):
+        red_o.give(i)
+    w_joint = joined(wqkvo_ref)
+
+    def grads(s):
+        return dqkv_ref[s].reshape(3 * chans, own)
+
+    def chunk(s):
+        padded = jnp.concatenate([grads(s), jnp.zeros((chans, own), bf16)], axis=0)
+        xp[s] = mm(w_joint, padded).astype(bf16)
+
+    for i, s in enumerate((pc.pd, pc.px, pc.py, pc.p)):
+        chunk(s)
+        red_x.give(i)
+    red_o.pair(0)
+    red_o.far()
+    load_mlp.wait()
+    for i in range(4):
+        red_m.give(i)
+    chunk(pc.d)
+    red_x.pair(0)
+    red_x.far()
+    for i in (1, 2):
+        red_o.pair(i)
+    chunk(pc.x)
+    chunk(pc.y)
+    red_o.near()
+    red_o.pair(3)
+    red_x.pair(1)
+    red_x.pair(2)
+    red_x.near()
+    chunk(pc.me)
+    red_x.pair(3)
+    grad_w = jnp.zeros((feats, 3 * chans), f32)
+    for s in range(group):
+        grad_w = grad_w + mm(xn_all[s], grads(s), NT)
+    split_rows(w_part, jnp.concatenate([grad_w, red_o.total().T], axis=1))
+    z_w = DepthReduce(pc, w_part, w_land, ws, wr)
+    z_w.start()
+    red_m.pair(0)
+    red_m.far()
+    for i in (1, 2, 3):
+        red_m.pair(i)
+    hat, inv = row_norm(tok_ref[...].astype(f32))
+    grad_xn = red_x.total().T
+    n_all[pc.me, 0:1, :] = jnp.sum(grad_xn * hat, axis=0, keepdims=True)
+    n_all[pc.me, 1:2, :] = jnp.sum(grad_xn, axis=0, keepdims=True)
+    n_all[pc.me, 2:4, :] = norm2_ref[...]
+    n_all[pc.me, 4:8, :] = jnp.zeros((4, feats), f32)
+    spread = GroupSpread(pc, n_all, ns, nr)
+    spread.start()
+    red_m.near()
+    gx_ref[...] = ghid_ref[...] + row_norm_back(grad_xn, gain_ref[...], hat, inv)
+    spread.finish()
+    m_all[pc.dp] = jnp.sum(n_all[...], axis=0)
+    z_norm = DepthGather(pc, m_all, qs, qr)
+    z_norm.start()
+    z_par.finish()
+    params = jnp.sum(p_all[...].astype(f32), axis=0)
+    for at, ref in ((RATE, rate_ref), (INB, inb_ref), (OUTC, outc_ref), (TAPS, sw_ref), (SKIP, skip_ref)):
+        ref[...] = params[at : at + ref.shape[0], 0:chans]
+    wd_ref[...] = z_down.total()
+    res_ref[...] = (hid_ref[...] + red_m.total().T).astype(bf16)
+    z_norm.finish()
+    norms = jnp.sum(m_all[...], axis=0)
+    for i, ref in enumerate((g1_ref, b1_ref, g2_ref, b2_ref)):
+        ref[...] = norms[i : i + 1, :]
+    w_sum = z_w.total()
+    for i, ref in enumerate((wq_ref, wk_ref, wv_ref, wo_ref)):
+        ref[...] = w_sum[:, i * chans : (i + 1) * chans]
+    for work in (z_down, z_par, red_o, red_x, red_m, z_w, spread, z_norm):
+        work.drain()
+
+
+def last_stage(axes, dqkv, xn_all, wqkvo, mlp, out, down, hidden, ghid, tokens, gain, norm2, dsw, drate, dinb, doutc, dskip):
+    n_dp, n_head, n_tensor = axes
+    group = n_head * n_tensor
+    own, feats = tokens.shape
+    chans = out.shape[1]
+    _, rows, units = down.shape
+    f32, bf16 = jnp.float32, jnp.bfloat16
+    sds = jax.ShapeDtypeStruct
+    vm = pl.BlockSpec(memory_space=pltpu.VMEM)
+    hbm = pl.BlockSpec(memory_space=pl.ANY)
+    dma = pltpu.SemaphoreType.DMA
+    wide, thin = GroupReduce.scratch(group, feats, own), GroupReduce.scratch(group, chans, feats)
+    return pl.pallas_call(
+        functools.partial(last_kernel, axes),
+        out_shape=(
+            sds((own, feats), bf16),
+            sds((own, feats), f32),
+            *(sds((1, feats), f32),) * 4,
+            *(sds((rows, chans), f32),) * 4,
+            sds((rows, units), f32),
+            *(sds(a.shape, f32) for a in (dsw, drate, dinb, doutc, dskip)),
+        ),
+        in_specs=[vm, vm, vm, hbm, hbm] + [vm] * 11,
+        out_specs=(vm,) * 16,
+        scratch_shapes=[
+            pltpu.VMEM(wqkvo.shape, bf16),
+            pltpu.VMEM(wqkvo.shape, bf16),
+            pltpu.VMEM((n_dp, rows, units), bf16),
+            pltpu.VMEM((n_dp, PARAM_ROWS, LANES), bf16),
+            pltpu.VMEM((group, 8, feats), f32),
+            pltpu.VMEM((n_dp, 8, feats), f32),
+            *wide, *thin, *wide,
+            *(dma((n_dp,)),) * 6,
+            dma((8,)), dma((8,)), dma((n_dp,)), dma((n_dp,)), dma((2,)),
+        ],
+        compiler_params=pltpu.CompilerParams(
+            collective_id=3, has_side_effects=True, vmem_limit_bytes=62 << 20
+        ),
+        name="last_stage",
+    )(dqkv, xn_all, wqkvo, mlp, out, down, hidden, ghid, tokens, gain, norm2, dsw, drate, dinb, doutc, dskip)
+
+
+from jax.sharding import PartitionSpec as P
+
+GROUP = ("head", "tensor")
 
 
 def on_device(
     tokens, seg_ids, norm1_gain, norm1_bias, norm2_gain, norm2_bias, q_weight, k_weight, v_weight,
     out_weight, up_weight, down_weight, shift_weight, decay_rate, in_coef, out_coef, skip_coef, cotangent,
 ):
-    bf16, f32 = jnp.bfloat16, jnp.float32
     chans = q_weight.shape[1]
     axes = (lax.axis_size("dp"), lax.axis_size("head"), lax.axis_size("tensor"))
-    own = tokens.shape[0]
-    feats = tokens.shape[1]
-    gather = lambda w: lax.all_gather(w, "dp", axis=0, tiled=True)
     packed = jnp.concatenate([q_weight, k_weight, v_weight, out_weight], axis=1)
     xn1, cot, qkv, w_packed, w_up, w_up_t, w_out_t = first_stage(
         axes, tokens, cotangent, norm1_gain[None], norm1_bias[None], packed, up_weight
     )
-    w_joint = w_packed.reshape(feats, 4 * chans)[:, : 3 * chans]
-    w_up = w_up.reshape(feats, -1)
-    w_out = w_out_t.reshape(feats, feats).T
-    w_down = gather(down_weight)
-    group_gather = lambda x: lax.all_gather(x, GROUP, axis=0, tiled=False)
-    scatter = lambda x: lax.psum_scatter(x, GROUP, scatter_dimension=0, tiled=False).astype(f32)
-    swap = lambda x: lax.all_to_all(x, GROUP, split_axis=0, concat_axis=0, tiled=True)
-    x = tokens.T.astype(f32)
-    g = cotangent.T
-    column = lambda v: v[:, None]
-    hat1, inv1 = norm_stats(x)
-    group = xn1.shape[0]
-    qkv = qkv.reshape(3, chans * group * own // LANES, LANES)
-    mixed, *saved = mixer_fwd(
-        qkv, seg_ids, shift_weight, skip_coef[None], decay_rate, in_coef, out_coef, un=16
+    qkv = qkv.reshape(3, qkv.shape[0] // 3, LANES)
+    mixer = (seg_ids, shift_weight, skip_coef[None], decay_rate, in_coef, out_coef)
+    mixed, *saved = mixer_fwd(qkv, *mixer, un=16)
+    hidden, grad_hidden, grad_mixed, mlp_part, down_part, sum_up, out_part, norms2 = middle_stage(
+        axes, mixed, tokens, cotangent, cot, w_out_t, w_up, w_up_t, down_weight, norm2_gain[None], norm2_bias[None]
     )
-    mixed = swap(mixed).reshape(group * chans, own)
-    hidden = x + jnp.dot(w_out, mixed, preferred_element_type=f32)
-    hat2, inv2 = norm_stats(hidden)
-    xn2 = group_gather((hat2 * column(norm2_gain) + column(norm2_bias)).astype(bf16))
-    pre = jnp.einsum("gdt,df->gft", xn2, w_up, preferred_element_type=f32)
-    act, slope = gelu_pair(pre)
-    act = act.astype(bf16)
-    grad_act = jnp.einsum("gdt,df->gft", cot, w_down, preferred_element_type=f32)
-    grad_pre = (grad_act * slope).astype(bf16)
-    mlp = scatter(jnp.einsum("gft,df->gdt", act, w_down, preferred_element_type=f32).astype(bf16))
-    grad_xn2 = scatter(
-        jnp.einsum("gft,df->gdt", grad_pre, w_up, preferred_element_type=f32).astype(bf16)
+    dqkv, *mixer_grads = mixer_bwd(grad_mixed, qkv, *saved, *mixer, un=16)
+    (
+        result, grad_x, gain1, bias1, gain2, bias2, sum_q, sum_k, sum_v, sum_o, sum_down,
+        sum_shift, sum_rate, sum_in, sum_out, sum_skip,
+    ) = last_stage(
+        axes, dqkv, xn1, w_packed, mlp_part, out_part, down_part, hidden, grad_hidden, tokens,
+        norm1_gain[None], norms2, *mixer_grads
     )
-    grad_down = jnp.einsum("gdt,gft->df", cot, act, preferred_element_type=f32)
-    grad_up = jnp.einsum("gdt,gft->df", xn2, grad_pre, preferred_element_type=f32)
-    result = (hidden + mlp).astype(bf16).T
-    grad_hidden = g.astype(f32) + norm_back(grad_xn2, column(norm2_gain), hat2, inv2)
-    gain2, bias2 = lanes_sum(grad_xn2 * hat2), lanes_sum(grad_xn2)
-    grad_mix = grad_hidden.astype(bf16)
-    grad_mixed = lax.dot_general(w_out, grad_mix, TN, preferred_element_type=f32).astype(bf16)
-    grad_out = lax.dot_general(grad_mix, mixed, NT, preferred_element_type=f32)
-    grad_out = lax.psum_scatter(grad_out.astype(bf16), GROUP, scatter_dimension=1, tiled=True)
-    grad_mixed = swap(grad_mixed.reshape(group, chans, own))
-    dqkv, dshift, drate, dinb, doutc, dskip = mixer_bwd(
-        grad_mixed, qkv, *saved, seg_ids, shift_weight, skip_coef[None], decay_rate, in_coef, out_coef, un=16
-    )
-    dqkv = dqkv.reshape(group, 3 * chans, own)
-    grad_w = jnp.einsum("gdt,gct->dc", xn1, dqkv, preferred_element_type=f32)
-    grad_xn1 = scatter(
-        jnp.einsum("gct,dc->gdt", dqkv, w_joint, preferred_element_type=f32).astype(bf16)
-    )
-    grad_x = (grad_hidden + norm_back(grad_xn1, column(norm1_gain), hat1, inv1)).T
-    gain1, bias1 = lanes_sum(grad_xn1 * hat1), lanes_sum(grad_xn1)
-    reduce = lambda v: lax.psum_scatter(v, "dp", scatter_dimension=0, tiled=True)
-    grad_w = reduce(grad_w)
-    sums = lax.psum((dshift, drate, dinb, doutc, dskip[0]), "dp")
-    norms = lax.psum((gain1, bias1, gain2, bias2), ("dp", "head", "tensor"))
     return (
-        result, grad_x, *norms, grad_w[:, :chans], grad_w[:, chans : 2 * chans], grad_w[:, 2 * chans :],
-        reduce(grad_out.astype(f32)), reduce(grad_up), reduce(grad_down), *sums,
+        result, grad_x, gain1[0], bias1[0], gain2[0], bias2[0], sum_q, sum_k, sum_v, sum_o, sum_up, sum_down,
+        sum_shift, sum_rate, sum_in, sum_out, sum_skip[0],
     )
 
 

time: 498 us -> 229 us (0.46)
  waiting for transfers between devices: 252 us -> 0 us
  Pallas kernels: 79.8 us -> 190 us
  blocking collectives: 71.6 us -> 0 us
  matrix products: 38.7 us -> 0 us
  between operations: 14.5 us -> 0.77 us
    reduce_scatter x7 -> x0, waiting for transfers between devices: 168 us -> none  [the longest x3 136 us: on_device(): lax.psum_scatter(x, GROUP, scatter_dimension=0, tiled=False).astype(f32)]
    pallas_call x0 -> x2, Pallas kernels: none -> 111 us  [the longest x1 66.1 us: middle_stage(): pl.pallas_call(functools.partial(middle_kernel, axes), out_shape=(sds((ow...]
    psum x1 -> x0, blocking collectives: 41.1 us -> none  [on_device(): norms = lax.psum((gain1, bias1, gain2, bias2), ('dp', 'head', 'tensor'))]
    dot_general x11 -> x0, matrix products: 38.7 us -> none  [the longest x1 5.29 us: on_device(): jnp.einsum('gdt,gft->df', xn2, grad_pre, preferred_element_type=f32)]
    psum x1 -> x0, waiting for transfers between devices: 37.2 us -> none  [on_device(): sums = lax.psum((dshift, drate, dinb, doutc, dskip[0]), 'dp')]
    unnamed x11 -> x0, waiting for transfers between devices: 23.7 us -> none
    all_gather x1 -> x0, blocking collectives: 19.7 us -> none  [on_device(): gather = lambda w: lax.all_gather(w, 'dp', axis=0, tiled=True)]
    all_gather x1 -> x0, waiting for transfers between devices: 15.3 us -> none  [on_device(): group_gather = lambda x: lax.all_gather(x, GROUP, axis=0, tiled=False)]
  transfers between devices with their start and end apart: 11 -> 0, of which waited for: 9 -> 0; matrix products, arithmetic and copies ran while one was open for 7% -> 0% of each run, Pallas kernels for 4% -> 0%
where the time goes in v3:
time: 229 us; the launch traced here: 228 us
  Pallas kernels  190 us (83%)
  local copies, waits for them, and re-layouts  30.2 us (13%)
  other arithmetic  6.83 us (3%)
    pallas_call x1, Pallas kernels, middle_stage(): pl.pallas_call(functools.partial(middle_kernel, axes), out_shape=(sds((ow...  66.1 us
    pallas_call x1, Pallas kernels, first_stage(): pl.pallas_call(functools.partial(first_kernel, axes), out_shape=(sds((gro...  47.5 us
    pallas_call x1, Pallas kernels, last_stage(): pl.pallas_call(functools.partial(last_kernel, axes), out_shape=(sds((own,...  44.4 us
    unnamed x53, local copies, waits for them, and re-layouts  25.1 us
    pallas_call x1, Pallas kernels, mixer_bwd(): pl.pallas_call(functools.partial(mixer_bwd_kernel, un), out_shape=(sds((n...  20.1 us
    pallas_call x1, Pallas kernels, mixer_fwd(): pl.pallas_call(functools.partial(mixer_fwd_kernel, un), out_shape=(sds((n...  11.9 us
    pallas_call x4, other arithmetic, last_stage(): pl.pallas_call(functools.partial(last_kernel, axes), out_shape=(sds((own,...  5.17 us

profile of v3, /device:TPU:0, one launch (start us, length us, event | category | flops | bytes accessed | tf_op | source)
XLA Modules:
  0.0 227.9 jit_solution(39856585380894923)
XLA Ops:
  0.7 1.3 broadcast_in_dim.16.gain_ref
  1.9 1.3 broadcast_in_dim.17.bias_ref
  3.2 1.3 broadcast_in_dim.19.gain_ref
  4.5 1.3 broadcast_in_dim.20.bias_ref
  5.7 1.7 pad_maximum_fusion.qkvo_ref
  7.4 47.5 %first_stage.1 = (bf16[8,768,256]{2,1,0:T(8,128)(2,1)}, bf16[8,768,256]{2,1,0:T(8,128)(2,1)}, f32[4608,128]{1,0:T(8,128)}, bf16[4,192,384]{2,1,0:T(8,128)(2,1)},...) custom-call(bf16[256,768]{1,0:T(8,128)(2,1)} %tok_ref.5, ...), custom_call_target="tpu_custom_call" | custom-call | tf_op jit(solution)/shard_map/first_stage/pallas_call | solution.py:601
  54.9 1.7 copy-done
  56.6 0.8 copy-done.6
  57.4 0.8 copy-done.7
  58.1 0.8 copy-done.8
  58.9 0.7 copy-done.10
  60.9 11.9 %mixer_fwd.1 = (bf16[8,96,256]{2,1,0:T(8,128)(2,1)S(1)}, f32[1536,128]{1,0:T(8,128)S(1)}, f32[1536,128]{1,0:T(8,128)S(1)}, f32[1536,128]{1,0:T(8,128)S(1)}, bf16...) custom-call(f32[3,1536,128]{2,1,0:T(8,128)S(1)} %bitcast.4, ...), custom_call_target="tpu_custom_call" | custom-call | tf_op jit(solution)/shard_map/mixer_fwd/pallas_call | solution.py:189
  72.8 0.9 copy-done.1
  73.7 0.9 copy-done.2
  74.6 0.9 copy-done.3
  75.5 0.7 copy-done.4
  76.2 0.7 copy-done.5
  77.6 66.1 %middle_stage.1 = (f32[256,768]{1,0:T(8,128)}, f32[256,768]{1,0:T(8,128)}, bf16[8,96,256]{2,1,0:T(8,128)(2,1)}, bf16[8,768,256]{2,1,0:T(8,128)(2,1)}, bf16[4,192...) custom-call(bf16[8,96,256]{2,1,0:T(8,128)(2,1)} %copy-done.5, ...), custom_call_target="tpu_custom_call" | custom-call | tf_op jit(solution)/shard_map/middle_stage/pallas_call | solution.py:896
  143.7 20.1 %mixer_bwd.1 = (bf16[8,3,96,256]{3,2,1,0:T(8,128)(2,1)}, f32[4,96]{1,0:T(4,128)}, f32[64,96]{1,0:T(8,128)}, f32[64,96]{1,0:T(8,128)}, f32[64,96]{1,0:T(8,128)}, /*index=5*/f32[1,96]{1,0:T(1,128)}) custom-call(bf16[8,96,256]{2,1,0:T(8,128)(2,1)} %get-tuple-element.67.gm_ref, f32[3,1536,128]{2,1,0:T(8,128)} %bitcast.3, f32[1536,128]{1,0:T(8,128)} %copy-done.1, ...), custom_call_target="tpu_custom_call" | custom-call | tf_op jit(solution)/shard_map/mixer_bwd/pallas_call | solution.py:372
  163.9 44.4 %last_stage.1 = (bf16[256,768]{1,0:T(8,128)(2,1)}, f32[256,768]{1,0:T(8,128)}, f32[1,768]{1,0:T(1,128)}, f32[1,768]{1,0:T(1,128)}, f32[1,768]{1,0:T(1,128)}, /*i...) custom-call(bf16[8,3,96,256]{3,2,1,0:T(8,128)(2,1)} %get-tuple-eleme, ...), custom_call_target="tpu_custom_call" | custom-call | tf_op jit(solution)/shard_map/last_stage/pallas_call | solution.py:1072
  208.4 1.3 reduce
  209.7 1.3 reduce.1
  211.0 1.3 reduce.2
  212.2 1.3 reduce.3
  213.5 1.8 copy.48
  215.3 2.1 copy.49
  217.4 1.5 copy.50
  218.9 1.5 copy.51
  220.4 1.5 copy.52
  222.0 1.5 copy.53
  223.5 0.7 copy.54
  224.2 0.7 copy.55
  (35 shorter events, 4.9 us)
Async XLA Ops:
  54.9 1.7 copy-start
  56.6 0.8 copy-start.6
  57.4 0.8 copy-start.7
  58.1 0.8 copy-start.8
  58.9 0.7 copy-start.10
  59.6 0.7 copy-start.11
  60.2 0.7 copy-start.12
  72.8 0.9 copy-start.1
  73.7 0.9 copy-start.2
  74.6 0.9 copy-start.3
  75.5 0.7 copy-start.4
  76.2 0.7 copy-start.5
  77.0 0.6 copy-start.9
  208.3 15.2 %copy-start.13 = (f32[192,384]{1,0:T(8,128)S(1)}, f32[192,384]{1,0:T(8,128)}, u32[]{:S(2)}) copy-start(f32[192,384]{1,0:T(8,128)} %get-tuple-element.132) | copy-start | bytes 884740
  208.3 15.9 %copy-start.14 = (f32[192,384]{1,0:T(8,128)S(1)}, f32[192,384]{1,0:T(8,128)}, u32[]{:S(2)}) copy-start(f32[192,384]{1,0:T(8,128)} %get-tuple-element.133) | copy-start | bytes 884740
  208.3 16.6 %copy-start.18 = (f32[4,96]{1,0:T(4,128)S(1)}, f32[4,96]{1,0:T(4,128)}, u32[]{:S(2)}) copy-start(f32[4,96]{1,0:T(4,128)} %get-tuple-element.134) | copy-start | bytes 4612
  208.3 17.2 %copy-start.17 = (f32[64,96]{1,0:T(8,128)S(1)}, f32[64,96]{1,0:T(8,128)}, u32[]{:S(2)}) copy-start(f32[64,96]{1,0:T(8,128)} %get-tuple-element.135) | copy-start | bytes 73732
  208.3 17.8 %copy-start.16 = (f32[64,96]{1,0:T(8,128)S(1)}, f32[64,96]{1,0:T(8,128)}, u32[]{:S(2)}) copy-start(f32[64,96]{1,0:T(8,128)} %get-tuple-element.136) | copy-start | bytes 73732
  208.3 18.4 %copy-start.15 = (f32[64,96]{1,0:T(8,128)S(1)}, f32[64,96]{1,0:T(8,128)}, u32[]{:S(2)}) copy-start(f32[64,96]{1,0:T(8,128)} %get-tuple-element.137) | copy-start | bytes 73732
  208.3 19.0 %copy-start.19 = (f32[1,96]{1,0:T(1,128)S(1)}, f32[1,96]{1,0:T(1,128)}, u32[]{:S(2)}) copy-start(f32[1,96]{1,0:T(1,128)} %get-tuple-element.104) | copy-start | bytes 1156

commit v4 on v1

--- a/solution.py
+++ b/solution.py
@@ -80,7 +80,7 @@
     return jnp.where(iota((LANES, LANES), 1) >= iota((LANES, LANES), 0), t, 0.0).astype(jnp.bfloat16)
 
 
-def mixer_fwd_kernel(
+def mixer_forward(
     un, qkv_ref, seg_ref, sw_ref, skip_ref, rate_ref, inb_ref, outc_ref,
     mixed_ref, core_ref, s_ref, f_ref, urev_ref, pp_ref, kern_ref,
     tscr, a_scr, b_scr, c_scr, e_scr, u_scr, kscr,
@@ -119,6 +119,7 @@
         return 0
 
     lax.fori_loop(0, chans // un, drive_step, 0)
+    yield
     step_rows = 16 * nb
 
     def rev_step(i, _):
@@ -147,6 +148,7 @@
         return 0
 
     lax.fori_loop(0, chans // un, fresh_step, 0)
+    yield
     across = e_scr[0:chans, :]
     b_ext = b_scr[0:chans, :]
     state = jnp.zeros((chans, LANES), jnp.float32)
@@ -154,6 +156,8 @@
         s_ref[pl.ds(b, chans, stride=nb), :] = state + pltpu.roll(state, ns, axis=1)
         fresh = f_ref[pl.ds(b, chans, stride=nb), :]
         state = across * carry[b : b + 1, :] * state + b_ext * fresh
+
+    yield
 
     def out_step(i, _):
         for j in range(un):
@@ -170,6 +174,7 @@
         return 0
 
     lax.fori_loop(0, chans // un, out_step, 0)
+    yield
     for b in range(nb):
         half = b % 2
         mixed_ref[b // 2, :, half * LANES : (half + 1) * LANES] = u_scr[
@@ -177,35 +182,7 @@
         ].astype(jnp.bfloat16)
 
 
-def mixer_fwd(qkv, seg, shift_w, skip, rate, in_b, out_c, un=4):
-    ns, chans = rate.shape
-    rows = qkv.shape[1]
-    nb = rows // chans
-    f32, bf16 = jnp.float32, jnp.bfloat16
-    sds = jax.ShapeDtypeStruct
-    vm = pl.BlockSpec(memory_space=pltpu.VMEM)
-    sm = pl.BlockSpec(memory_space=pltpu.SMEM)
-    sq = pltpu.VMEM((LANES, LANES), f32)
-    return pl.pallas_call(
-        functools.partial(mixer_fwd_kernel, un),
-        out_shape=(
-            sds((nb // 2, chans, 2 * LANES), bf16),
-            sds((rows, LANES), f32),
-            sds((rows, LANES), f32),
-            sds((rows, LANES), f32),
-            sds((rows, LANES), bf16),
-            sds((chans * LANES, LANES), bf16),
-            sds((chans, LANES), f32),
-        ),
-        in_specs=[vm, vm, sm, sm, vm, vm, vm],
-        out_specs=(vm,) * 7,
-        scratch_shapes=[sq, sq, sq, sq, sq, pltpu.VMEM((rows, LANES), f32), sq],
-        compiler_params=pltpu.CompilerParams(vmem_limit_bytes=48 << 20),
-        name="mixer_fwd",
-    )(qkv, seg, shift_w, skip, rate, in_b, out_c)
-
-
-def mixer_bwd_kernel(
+def mixer_backward(
     un, gm_ref, qkv_ref, core_ref, s_ref, f_ref, urev_ref, pp_ref, kern_ref, seg_ref,
     sw_ref, skip_ref, rate_ref, inb_ref, outc_ref,
     dqkv_ref, dsw_ref, drate_ref, dinb_ref, doutc_ref, dskip_ref,
@@ -257,6 +234,7 @@
         return 0
 
     lax.fori_loop(0, chans // un, grad_step, 0)
+    yield
     across = e_scr[0:chans, :]
     b_ext = b_scr[0:chans, :]
     c_ext = c_scr[0:chans, :]
@@ -272,6 +250,8 @@
         x_scr[here, :] = b_ext * adj
         adj = c_ext * h + across * carry[b : b + 1, :] * adj
 
+    yield
+
     def back_step(i, _):
         for j in range(un):
             c = i * un + j
@@ -285,6 +265,7 @@
         return 0
 
     lax.fori_loop(0, chans // un, back_step, 0)
+    yield
     step_rows = 16 * nb
 
     def rev_step(i, _):
@@ -315,12 +296,14 @@
         return 0
 
     lax.fori_loop(0, chans // un, last_step, 0)
+    yield
     for b in range(nb):
         half = b % 2
         for i, scr in enumerate((dq_scr, dk_scr, dv_scr)):
             dqkv_ref[b // 2, i, :, half * LANES : (half + 1) * LANES] = scr[
                 pl.ds(b, chans, stride=nb), :
             ].astype(jnp.bfloat16)
+    yield
     for j in range(SHIFT):
         dsw_ref[j : j + 1, :] = jnp.sum(red_scr[j].T, axis=0, keepdims=True)[:, 0:chans]
     dskip_ref[...] = jnp.sum(red_scr[SHIFT].T, axis=0, keepdims=True)[:, 0:chans]
@@ -358,36 +341,752 @@
     )
 
 
-def mixer_bwd(gm, qkv, core, s, f, urev, pp, kern, seg, shift_w, skip, rate, in_b, out_c, un=4):
-    ns, chans = rate.shape
-    rows = qkv.shape[1]
-    nb = rows // chans
+MESH = pl.DeviceIdType.MESH
+
+
+class Place:
+    def __init__(self, n_dp, n_head, n_tensor):
+        self.n_dp, self.n_head, self.n_tensor = n_dp, n_head, n_tensor
+        self.dp = lax.axis_index("dp")
+        h, t = lax.axis_index("head"), lax.axis_index("tensor")
+        self.size = n_head * n_tensor
+        ph, xh, yt = h + 1 - 2 * (h % 2), (h + 2) % n_head, 1 - t
+        pxh = (ph + 2) % n_head
+        slot = lambda a, b: a * n_tensor + b
+        self.me, self.p, self.x, self.y, self.d = (
+            slot(h, t), slot(ph, t), slot(xh, t), slot(h, yt), slot(xh, yt),
+        )
+        self.px, self.py, self.pd = slot(pxh, t), slot(ph, yt), slot(pxh, yt)
+        self.to_p, self.to_x, self.to_y = {"head": ph}, {"head": xh}, {"tensor": yt}
+
+    def dp_peer(self, step):
+        return (self.dp + step) % self.n_dp
+
+    def barrier(self, whole_group, over_dp):
+        sem = pltpu.get_barrier_semaphore()
+
+        def greet(where):
+            pl.semaphore_signal(sem, inc=1, device_id=where, device_id_type=MESH)
+
+        if whole_group:
+            for i in range(1, self.size):
+                peer = (self.me + i) % self.size
+                greet({"head": peer // self.n_tensor, "tensor": peer % self.n_tensor})
+            count = self.size - 1
+        else:
+            for where in (self.to_p, self.to_x, self.to_y):
+                greet(where)
+            count = 3
+        if over_dp:
+            def step(i, _):
+                greet({"dp": self.dp_peer(i)})
+                return 0
+
+            lax.fori_loop(1, self.n_dp, step, 0)
+            count += self.n_dp - 1
+        pl.semaphore_wait(sem, count)
+
+
+def remote(src, dst, ssem, rsem, where):
+    return pltpu.make_async_remote_copy(
+        src_ref=src, dst_ref=dst, send_sem=ssem, recv_sem=rsem, device_id=where, device_id_type=MESH
+    )
+
+
+class GroupGather:
+    COPIES = 11
+
+    def __init__(self, place, ref, ssem, rsem):
+        self.ssem, self.rsem = ssem, rsem
+        half = ref.shape[1] // 2
+        top, low = pl.ds(0, half), pl.ds(half, half)
+        pc = place
+        full = lambda s: ref.at[s]
+        part = lambda s, rows: ref.at[s, rows]
+        self.out = [
+            (full(pc.me), pc.to_p),
+            (part(pc.me, top), pc.to_x), (part(pc.me, low), pc.to_x),
+            (part(pc.me, low), pc.to_y), (part(pc.me, top), pc.to_y),
+            (part(pc.x, top), pc.to_y), (part(pc.y, low), pc.to_x),
+            (full(pc.x), pc.to_p), (full(pc.y), pc.to_p),
+            (part(pc.d, top), pc.to_p), (part(pc.d, low), pc.to_p),
+        ]
+        self.into = [
+            full(pc.p), part(pc.x, top), part(pc.x, low), part(pc.y, low), part(pc.y, top),
+            part(pc.d, top), part(pc.d, low), full(pc.px), full(pc.py), part(pc.pd, top), part(pc.pd, low),
+        ]
+
+    def send(self, *which):
+        for i in which:
+            src, where = self.out[i]
+            remote(src, src, self.ssem.at[i], self.rsem.at[i], where).start()
+
+    def arrive(self, *which):
+        for i in which:
+            dst = self.into[i]
+            remote(dst, dst, self.ssem.at[i], self.rsem.at[i], self.out[i][1]).wait_recv()
+
+    def start(self):
+        self.send(1, 3, 2, 4, 0)
+
+    def first(self):
+        self.arrive(1)
+        self.send(5)
+        self.arrive(3)
+        self.send(6)
+
+    def second(self):
+        self.arrive(2)
+        self.send(7)
+        self.arrive(4)
+        self.send(8)
+
+    def third(self):
+        self.arrive(5)
+        self.send(9)
+        self.arrive(6)
+        self.send(10)
+
+    def finish(self):
+        self.arrive(0, 7, 8, 9, 10)
+
+    def drain(self):
+        for i in range(self.COPIES):
+            src, where = self.out[i]
+            remote(src, src, self.ssem.at[i], self.rsem.at[i], where).wait_send()
+
+
+class DepthGather:
+    def __init__(self, place, ref, ssem, rsem):
+        self.place, self.ref, self.ssem, self.rsem = place, ref, ssem, rsem
+
+    def _copy(self, step, slot, peer):
+        return remote(
+            self.ref.at[slot], self.ref.at[slot], self.ssem.at[step], self.rsem.at[step], {"dp": peer}
+        )
+
+    def _loop(self, body):
+        def step(i, _):
+            body(i)
+            return 0
+
+        lax.fori_loop(1, self.place.n_dp, step, 0)
+
+    def start(self):
+        pc = self.place
+        self._loop(lambda i: self._copy(i, pc.dp, pc.dp_peer(i)).start())
+
+    def finish(self):
+        pc = self.place
+        source = lambda i: (pc.dp + pc.n_dp - i) % pc.n_dp
+        self._loop(lambda i: self._copy(i, source(i), pc.dp_peer(i)).wait_recv())
+
+    def drain(self):
+        pc = self.place
+        self._loop(lambda i: self._copy(i, pc.dp, pc.dp_peer(i)).wait_send())
+
+
+def joined(ref):
+    n, rows, columns = ref.shape
+    if rows % 16 == 0:
+        return ref[...].reshape(n * rows, columns)
+    parts = [ref[j].astype(jnp.float32) for j in range(n)]
+    return jnp.concatenate(parts, axis=0).astype(ref.dtype)
+
+
+def row_norm(x):
+    centred = x - jnp.mean(x, axis=1, keepdims=True)
+    inv = lax.rsqrt(jnp.mean(centred * centred, axis=1, keepdims=True) + 1e-05)
+    return centred * inv, inv
+
+
+class GroupReduce:
+    COPIES = 10
+
+    def __init__(self, place, part, land, half_land, last_land, ssem, rsem):
+        pc = place
+        self.pc = pc
+        self.part, self.land, self.half_land, self.last_land = part, land, half_land, last_land
+        self.ssem, self.rsem = ssem, rsem
+        half = part.shape[1] // 2
+        top, low = pl.ds(0, half), pl.ds(half, half)
+        self.top, self.low = top, low
+        self.mine = [pc.d, pc.x, pc.y, pc.me]
+        self.theirs = [pc.pd, pc.px, pc.py, pc.p]
+        self.copies = [(part.at[self.theirs[i]], land.at[i], pc.to_p) for i in range(4)] + [
+            (part.at[pc.d, top], half_land.at[0], pc.to_x),
+            (part.at[pc.d, low], half_land.at[1], pc.to_y),
+            (part.at[pc.x, top], last_land.at[0, top], pc.to_x),
+            (part.at[pc.y, low], last_land.at[1, low], pc.to_y),
+            (part.at[pc.x, low], last_land.at[0, low], pc.to_x),
+            (part.at[pc.y, top], last_land.at[1, top], pc.to_y),
+        ]
+
+    def _copy(self, i):
+        src, dst, where = self.copies[i]
+        return remote(src, dst, self.ssem.at[i], self.rsem.at[i], where)
+
+    def give(self, *which):
+        for i in which:
+            self._copy(i).start()
+
+    def pair(self, i):
+        self._copy(i).wait_recv()
+        s = self.mine[i]
+        self.part[s] = (self.part[s].astype(jnp.float32) + self.land[i].astype(jnp.float32)).astype(
+            self.part.dtype
+        )
+
+    def far(self):
+        self.pair(0)
+        self.give(4, 5)
+        self.pair(1)
+        self.give(6)
+        self.pair(2)
+        self.give(7)
+
+    def near(self):
+        for i, s, rows in ((4, self.pc.y, self.top), (5, self.pc.x, self.low)):
+            self._copy(i).wait_recv()
+            self.part[s, rows] = (
+                self.part[s, rows].astype(jnp.float32) + self.half_land[i - 4].astype(jnp.float32)
+            ).astype(self.part.dtype)
+            self.give(9 if i == 4 else 8)
+
+    def total(self):
+        for i in (6, 7, 8, 9):
+            self._copy(i).wait_recv()
+        return (
+            self.part[self.pc.me].astype(jnp.float32)
+            + self.last_land[0].astype(jnp.float32)
+            + self.last_land[1].astype(jnp.float32)
+        )
+
+    def drain(self):
+        for i in range(self.COPIES):
+            self._copy(i).wait_send()
+
+    @staticmethod
+    def scratch(group, rows, columns):
+        bf16 = jnp.bfloat16
+        return [
+            pltpu.VMEM((group, rows, columns), bf16),
+            pltpu.VMEM((4, rows, columns), bf16),
+            pltpu.VMEM((2, rows // 2, columns), bf16),
+            pltpu.VMEM((2, rows, columns), bf16),
+        ]
+
+
+class GroupSwap:
+    def __init__(self, place, src, dst, lsem, ssem, rsem):
+        self.pc, self.src, self.dst, self.ssem, self.rsem, self.lsem = place, src, dst, ssem, rsem, lsem
+
+    def _peer(self, i):
+        return (self.pc.me + i) % self.pc.size
+
+    def _copy(self, i, slot):
+        peer = self._peer(i)
+        where = {"head": peer // self.pc.n_tensor, "tensor": peer % self.pc.n_tensor}
+        return remote(self.src.at[peer], self.dst.at[slot], self.ssem.at[i], self.rsem.at[i], where)
+
+    def _own(self):
+        return pltpu.make_async_copy(self.src.at[self.pc.me], self.dst.at[self.pc.me], self.lsem)
+
+    def start(self):
+        for i in range(1, self.pc.size):
+            self._copy(i, self.pc.me).start()
+        self._own().start()
+
+    def finish(self):
+        for i in range(1, self.pc.size):
+            self._copy(i, (self.pc.me + self.pc.size - i) % self.pc.size).wait_recv()
+        self._own().wait()
+
+    def drain(self):
+        for i in range(1, self.pc.size):
+            self._copy(i, self.pc.me).wait_send()
+
+
+class DepthReduce:
+    def __init__(self, place, src, land, ssem, rsem):
+        self.place, self.src, self.land, self.ssem, self.rsem = place, src, land, ssem, rsem
+
+    def _copy(self, step, mine, slot, peer):
+        return remote(
+            self.src.at[mine], self.land.at[slot], self.ssem.at[step], self.rsem.at[step], {"dp": peer}
+        )
+
+    def _loop(self, body, start):
+        return lax.fori_loop(1, self.place.n_dp, body, start)
+
+    def start(self):
+        pc = self.place
+
+        def step(i, _):
+            self._copy(i, pc.dp_peer(i), pc.dp, pc.dp_peer(i)).start()
+            return 0
+
+        self._loop(step, 0)
+
+    def total(self):
+        pc = self.place
+
+        def step(i, acc):
+            source = (pc.dp + pc.n_dp - i) % pc.n_dp
+            self._copy(i, source, source, pc.dp_peer(i)).wait_recv()
+            return acc + self.land[source].astype(jnp.float32)
+
+        return self._loop(step, self.src[pc.dp].astype(jnp.float32))
+
+    def drain(self):
+        pc = self.place
+
+        def step(i, _):
+            self._copy(i, pc.dp_peer(i), pc.dp, pc.dp_peer(i)).wait_send()
+            return 0
+
+        self._loop(step, 0)
+
+
+def split_rows(ref, value):
+    n, rows, columns = ref.shape
+    if rows % 16 == 0:
+        ref[...] = value.astype(ref.dtype).reshape(n, rows, columns)
+    else:
+        for j in range(n):
+            ref[j] = value[j * rows : (j + 1) * rows].astype(ref.dtype)
+
+
+def row_norm_back(grad, gain, hat, inv):
+    scaled = grad * gain
+    return inv * (
+        scaled
+        - jnp.mean(scaled, axis=1, keepdims=True)
+        - hat * jnp.mean(scaled * hat, axis=1, keepdims=True)
+    )
+
+
+def gelu_pair(pre):
+    cdf = 0.5 * (1.0 + lax.erf(pre * 0.7071067811865476))
+    return pre * cdf, cdf + pre * (0.3989422804014327 * jnp.exp(-0.5 * pre * pre))
+
+
+class GroupSpread:
+    def __init__(self, place, ref, ssem, rsem):
+        self.pc, self.ref, self.ssem, self.rsem = place, ref, ssem, rsem
+
+    def _copy(self, i, slot):
+        peer = (self.pc.me + i) % self.pc.size
+        where = {"head": peer // self.pc.n_tensor, "tensor": peer % self.pc.n_tensor}
+        return remote(self.ref.at[slot], self.ref.at[slot], self.ssem.at[i], self.rsem.at[i], where)
+
+    def start(self):
+        for i in range(1, self.pc.size):
+            self._copy(i, self.pc.me).start()
+
+    def finish(self):
+        for i in range(1, self.pc.size):
+            self._copy(i, (self.pc.me + self.pc.size - i) % self.pc.size).wait_recv()
+
+    def drain(self):
+        for i in range(1, self.pc.size):
+            self._copy(i, self.pc.me).wait_send()
+
+
+TAPS_AT, SKIP_AT, PARAM_ROWS = 192, 208, 224
+UNROLL = 16
+
+
+class Names:
+    def __init__(self, names, refs):
+        assert len(names) == len(refs)
+        for name, ref in zip(names, refs):
+            setattr(self, name, ref)
+
+
+def layout(axes, own, feats, rows, chans, units, ns):
+    n_dp, n_head, n_tensor = axes
+    group = n_head * n_tensor
+    f32, bf16 = jnp.float32, jnp.bfloat16
+    v = pltpu.VMEM
+    dma = lambda *shape: pltpu.SemaphoreType.DMA(shape)
+    blocks = group * own // LANES
+    conv = chans * blocks
+    sq = v((LANES, LANES), f32)
+    full = v((conv, LANES), f32)
+    out = dict(
+        tok=v((own, feats), bf16), cot=v((own, feats), bf16), four=v((4, rows, chans), bf16),
+        wqkvo=v((n_dp, rows, 4 * chans), bf16), wup=v((n_dp, rows, units), bf16), wdown=v((n_dp, rows, units), bf16),
+        wt=v((4 * chans, feats), bf16), wupt=v((units, feats), bf16), wdownt=v((units, feats), bf16),
+        wout=v((group, chans, feats), bf16),
+        xn1=v((group, feats, own), bf16), cots=v((group, feats, own), bf16), xn2=v((group, feats, own), bf16),
+        act=v((group, units, own), bf16), gpre=v((group, units, own), bf16),
+        qkv=v((3, conv, LANES), f32), core=full, s=full, f=full, urev=v((conv, LANES), bf16),
+        pp=v((chans * LANES, LANES), bf16), kern=v((chans, LANES), f32),
+        mixed=v((group, chans, own), bf16), mixed_in=v((group, chans, own), bf16),
+        gmix=v((group, chans, own), bf16), gmix_in=v((group, chans, own), bf16),
+        dqkv=v((group, 3, chans, own), bf16),
+        t0=sq, t1=sq, t2=sq, t3=sq, t4=sq, t5=sq, gr=sq, red=v((SHIFT + 1, LANES, LANES), f32),
+        w0=full, w1=full, w2=full, w3=full, w4=full, w5=full, w6=full, dur=v((conv, LANES), bf16),
+        dsw=v((SHIFT, chans), f32), drate=v((ns, chans), f32), dinb=v((ns, chans), f32), doutc=v((ns, chans), f32),
+        dskip=v((1, chans), f32),
+        hat=v((own, feats), f32), hid=v((own, feats), f32), ghid=v((own, feats), f32),
+        up_part=v((n_dp, rows, units), bf16), up_land=v((n_dp, rows, units), bf16),
+        dn_part=v((n_dp, rows, units), bf16), dn_land=v((n_dp, rows, units), bf16),
+        w_part=v((n_dp, rows, 4 * chans), bf16), w_land=v((n_dp, rows, 4 * chans), bf16),
+        params=v((n_dp, PARAM_ROWS, LANES), bf16),
+        n1=v((group, 2, feats), f32), n2=v((group, 2, feats), f32), m1=v((n_dp, 2, feats), f32), m2=v((n_dp, 2, feats), f32),
+    )
+    for name, height, width in (("x", feats, own), ("m", feats, own), ("o", chans, feats)):
+        for part, alloc in zip(("part", "land", "half", "last"), GroupReduce.scratch(group, height, width)):
+            out[f"{name}_{part}"] = alloc
+    for name, count in (
+        ("xn1", 11), ("cots", 11), ("wout", 11), ("xn2", 11), ("x2", 10), ("m", 10), ("o", 10), ("x1", 10),
+        ("in", group), ("back", group), ("sp1", group), ("sp2", group),
+        ("zq", n_dp), ("zu", n_dp), ("zd", n_dp), ("gu", n_dp), ("gd", n_dp), ("gw", n_dp), ("zp", n_dp),
+        ("zn1", n_dp), ("zn2", n_dp),
+    ):
+        out[f"send_{name}"] = dma(count)
+        out[f"recv_{name}"] = dma(count)
+    out["local"] = dma(12)
+    return out
+
+
+INPUTS = (
+    "tok_hbm", "cot_hbm", "q_hbm", "k_hbm", "v_hbm", "o_hbm", "up_hbm", "down_hbm",
+    "seg", "gain1", "bias1", "gain2", "bias2", "taps", "rate", "inb", "outc", "skip",
+)
+OUTPUTS = (
+    "res", "gx", "g1", "b1", "g2", "b2", "dq", "dk", "dv", "do", "dup", "ddown",
+    "out_taps", "out_rate", "out_inb", "out_outc", "out_skip",
+)
+
+
+def run_beside(body, tasks):
+    tasks = list(tasks)
+    for _ in body:
+        if tasks:
+            tasks.pop(0)()
+    for task in tasks:
+        task()
+
+
+def block_kernel(axes, names, *refs):
+    r = Names(names, refs)
+    pc = Place(*axes)
+    f32, bf16 = jnp.float32, jnp.bfloat16
+    group, chans, feats = r.wout.shape
+    own = r.tok.shape[0]
+    blocks = own // LANES
+    work = []
+
+    def sems(name):
+        return getattr(r, f"send_{name}"), getattr(r, f"recv_{name}")
+
+    def make(kind, name, *args):
+        made = kind(pc, *args, *sems(name))
+        work.append(made)
+        return made
+
+    def local(i, src, dst):
+        copy = pltpu.make_async_copy(src, dst, r.local.at[i])
+        copy.start()
+        return copy
+
+    four = [local(i, src, r.four.at[i]) for i, src in enumerate((r.q_hbm, r.k_hbm, r.v_hbm, r.o_hbm))]
+    load_tok = local(4, r.tok_hbm, r.tok)
+    load_cot = local(5, r.cot_hbm, r.cot)
+    load_up = local(6, r.up_hbm, r.wup.at[pc.dp])
+    load_down = local(7, r.down_hbm, r.wdown.at[pc.dp])
+    pc.barrier(True, True)
+    for copy in four:
+        copy.wait()
+    r.wqkvo[pc.dp] = jnp.concatenate([r.four[i] for i in range(4)], axis=1)
+    z_qkvo = make(DepthGather, "zq", r.wqkvo)
+    z_up = make(DepthGather, "zu", r.wup)
+    z_down = make(DepthGather, "zd", r.wdown)
+    xn1_g = make(GroupGather, "xn1", r.xn1)
+    cot_g = make(GroupGather, "cots", r.cots)
+    out_g = make(GroupGather, "wout", r.wout)
+    xn2_g = make(GroupGather, "xn2", r.xn2)
+    z_qkvo.start()
+    load_tok.wait()
+    x = r.tok[...].astype(f32)
+    gain1, gain2 = r.gain1[...].reshape(1, feats), r.gain2[...].reshape(1, feats)
+    bias1, bias2 = r.bias1[...].reshape(1, feats), r.bias2[...].reshape(1, feats)
+    hat1, _ = row_norm(x)
+    r.xn1[pc.me] = (hat1 * gain1 + bias1).astype(bf16).T
+    xn1_g.start()
+    load_up.wait()
+    z_up.start()
+    load_down.wait()
+    z_down.start()
+    load_cot.wait()
+    r.cots[pc.me] = r.cot[...].T
+    xn1_g.first()
+    cot_g.start()
+    xn1_g.second()
+    z_qkvo.finish()
+    r.wt[...] = joined(r.wqkvo).T
+    r.wout[pc.me] = r.wt[3 * chans :, :]
+    out_g.start()
+
+    def project(s):
+        y = mm(r.wt[0 : 3 * chans, :], r.xn1[s])
+        for i in range(3):
+            for h in range(blocks):
+                r.qkv[i, pl.ds(s * blocks + h, chans, stride=group * blocks), :] = y[
+                    i * chans : (i + 1) * chans, h * LANES : (h + 1) * LANES
+                ]
+
+    xn1_g.third()
+    xn1_g.finish()
+    for s in range(group):
+        project(s)
+
+    def cot_first():
+        cot_g.first()
+
+    def cot_second():
+        cot_g.second()
+        out_g.first()
+
+    def late_weights():
+        z_up.finish()
+        r.wupt[...] = joined(r.wup).T
+        out_g.second()
+
+    def cot_third():
+        cot_g.third()
+        out_g.third()
+
+    mixer = (r.seg, r.taps, r.skip, r.rate, r.inb, r.outc)
+    run_beside(
+        mixer_forward(
+            UNROLL, r.qkv, *mixer, r.mixed, r.core, r.s, r.f, r.urev, r.pp, r.kern,
+            r.t0, r.t1, r.t2, r.t3, r.t4, r.w0, r.t5,
+        ),
+        (cot_first, cot_second, late_weights, cot_third),
+    )
+    swap_in = make(GroupSwap, "in", r.mixed, r.mixed_in, r.local.at[8])
+    swap_in.start()
+    out_g.finish()
+    cot_g.finish()
+    z_down.finish()
+    w_down = joined(r.wdown)
+    r.wdownt[...] = w_down.T
+    w_up = joined(r.wup)
+    swap_in.finish()
+    mixed_t = r.mixed_in[...].reshape(feats, own)
+    wout_t = r.wout[...].reshape(feats, feats)
+    hidden = r.tok[...].astype(f32) + mm(mixed_t, wout_t, TN)
+    r.hid[...] = hidden
+    hat2, inv2 = row_norm(hidden)
+    r.xn2[pc.me] = (hat2 * gain2 + bias2).astype(bf16).T
+    xn2_g.start()
+    r.hat[...] = hat2
+    red_x2 = make(GroupReduce, "x2", r.x_part, r.x_land, r.x_half, r.x_last)
+    red_m = make(GroupReduce, "m", r.m_part, r.m_land, r.m_half, r.m_last)
+    red_o = make(GroupReduce, "o", r.o_part, r.o_land, r.o_half, r.o_last)
+
+    def chunk(s):
+        act, slope = gelu_pair(mm(r.wupt[...], r.xn2[s]))
+        r.act[s] = act.astype(bf16)
+        grad_pre = (mm(r.wdownt[...], r.cots[s]) * slope).astype(bf16)
+        r.gpre[s] = grad_pre
+        r.x_part[s] = mm(w_up, grad_pre).astype(bf16)
+
+    chunk(pc.me)
+    xn2_g.arrive(0)
+    chunk(pc.p)
+    red_x2.give(3)
+    xn2_g.first()
+    xn2_g.second()
+    chunk(pc.x)
+    chunk(pc.y)
+    xn2_g.arrive(7)
+    chunk(pc.px)
+    red_x2.give(1)
+    xn2_g.arrive(8)
+    chunk(pc.py)
+    red_x2.give(2)
+    xn2_g.third()
+    chunk(pc.d)
+    xn2_g.arrive(9, 10)
+    chunk(pc.pd)
+    red_x2.give(0)
+    red_x2.far()
+    units = r.act.shape[1]
+    grad_up = jnp.zeros((feats, units), f32)
+    for s in range(group):
+        grad_up = grad_up + mm(r.xn2[s], r.gpre[s], NT)
+    split_rows(r.up_part, grad_up)
+    sum_up = make(DepthReduce, "gu", r.up_part, r.up_land)
+    sum_up.start()
+    red_x2.near()
+    red_x2.pair(3)
+    for i, s in enumerate(red_m.theirs):
+        r.m_part[s] = mm(w_down, r.act[s]).astype(bf16)
+        red_m.give(i)
+    for s in red_m.mine:
+        r.m_part[s] = mm(w_down, r.act[s]).astype(bf16)
+    grad_down = jnp.zeros((feats, units), f32)
+    for s in range(group):
+        grad_down = grad_down + mm(r.cots[s], r.act[s], NT)
+    split_rows(r.dn_part, grad_down)
+    sum_down = make(DepthReduce, "gd", r.dn_part, r.dn_land)
+    sum_down.start()
+    grad_xn = red_x2.total().T
+    hat2 = r.hat[...]
+    grad_hidden = r.cot[...].astype(f32) + row_norm_back(grad_xn, gain2, hat2, inv2)
+    r.ghid[...] = grad_hidden
+    grad_mix = grad_hidden.astype(bf16)
+    r.gmix[...] = mm(wout_t, grad_mix, NT).astype(bf16).reshape(group, chans, own)
+    swap_back = make(GroupSwap, "back", r.gmix, r.gmix_in, r.local.at[9])
+    swap_back.start()
+    r.n2[pc.me, 0:1, :] = jnp.sum(grad_xn * hat2, axis=0, keepdims=True)
+    r.n2[pc.me, 1:2, :] = jnp.sum(grad_xn, axis=0, keepdims=True)
+    spread2 = make(GroupSpread, "sp2", r.n2)
+    spread2.start()
+    r.o_part[...] = mm(mixed_t, grad_mix).astype(bf16).reshape(group, chans, feats)
+    red_o.give(0, 1, 2, 3)
+    red_m.far()
+    red_o.far()
+    swap_back.finish()
+    norm2 = make(DepthGather, "zn2", r.m2)
+
+    def near_sums():
+        red_m.near()
+        red_o.near()
+        spread2.finish()
+        r.m2[pc.dp] = jnp.sum(r.n2[...], axis=0)
+        norm2.start()
+
+    def own_sums():
+        red_m.pair(3)
+        red_o.pair(3)
+        red_x2.drain()
+        work.remove(red_x2)
+
+    def last_sums():
+        r.res[...] = (r.hid[...] + red_m.total().T).astype(bf16)
+        norm2.finish()
+        sums = jnp.sum(r.m2[...], axis=0)
+        r.g2[...] = sums[0:1]
+        r.b2[...] = sums[1:2]
+
+    def depth_sums():
+        r.dup[...] = sum_up.total()
+        r.ddown[...] = sum_down.total()
+
+    w_joint = joined(r.wqkvo)
+    red_x1 = make(GroupReduce, "x1", r.x_part, r.x_land, r.x_half, r.x_last)
+
+    def grads(s):
+        return r.dqkv[s].reshape(3 * chans, own)
+
+    def chunk_back(s):
+        padded = jnp.concatenate([grads(s), jnp.zeros((chans, own), bf16)], axis=0)
+        r.x_part[s] = mm(w_joint, padded).astype(bf16)
+
+    def start_back():
+        for i, s in enumerate(red_x1.theirs):
+            chunk_back(s)
+            red_x1.give(i)
+        for s in red_x1.mine:
+            chunk_back(s)
+
+    run_beside(
+        mixer_backward(
+            UNROLL, r.gmix_in, r.qkv, r.core, r.s, r.f, r.urev, r.pp, r.kern, *mixer,
+            r.dqkv, r.dsw, r.drate, r.dinb, r.doutc, r.dskip,
+            r.t0, r.t1, r.t2, r.t3, r.w0, r.w1, r.w2, r.w3, r.dur, r.w2, r.w4, r.w5, r.w6, r.gr, r.red,
+        ),
+        (near_sums, own_sums, last_sums, depth_sums, start_back),
+    )
+    red_x1.far()
+    r.params[pc.dp] = jnp.zeros(r.params.shape[1:], bf16)
+    ns = r.drate.shape[0]
+    pieces = ((0, r.drate, r.out_rate), (ns, r.dinb, r.out_inb), (2 * ns, r.doutc, r.out_outc),
+              (TAPS_AT, r.dsw, r.out_taps), (SKIP_AT, r.dskip, r.out_skip))
+    for at, ref, _ in pieces:
+        r.params[pc.dp, at : at + ref.shape[0], 0:chans] = ref[...].astype(bf16)
+    z_par = make(DepthGather, "zp", r.params)
+    z_par.start()
+    grad_w = jnp.zeros((feats, 3 * chans), f32)
+    for s in range(group):
+        grad_w = grad_w + mm(r.xn1[s], grads(s), NT)
+    split_rows(r.w_part, jnp.concatenate([grad_w, red_o.total().T], axis=1))
+    sum_w = make(DepthReduce, "gw", r.w_part, r.w_land)
+    sum_w.start()
+    red_x1.near()
+    red_x1.pair(3)
+    hat1, inv1 = row_norm(r.tok[...].astype(f32))
+    grad_xn = red_x1.total().T
+    r.n1[pc.me, 0:1, :] = jnp.sum(grad_xn * hat1, axis=0, keepdims=True)
+    r.n1[pc.me, 1:2, :] = jnp.sum(grad_xn, axis=0, keepdims=True)
+    spread1 = make(GroupSpread, "sp1", r.n1)
+    spread1.start()
+    r.gx[...] = r.ghid[...] + row_norm_back(grad_xn, gain1, hat1, inv1)
+    spread1.finish()
+    r.m1[pc.dp] = jnp.sum(r.n1[...], axis=0)
+    norm1 = make(DepthGather, "zn1", r.m1)
+    norm1.start()
+    z_par.finish()
+    sums = jnp.sum(r.params[...].astype(f32), axis=0)
+    for at, ref, out in pieces:
+        out[...] = sums[at : at + ref.shape[0], 0:chans]
+    norm1.finish()
+    sums = jnp.sum(r.m1[...], axis=0)
+    r.g1[...] = sums[0:1]
+    r.b1[...] = sums[1:2]
+    w_sum = sum_w.total()
+    for i, ref in enumerate((r.dq, r.dk, r.dv, r.do)):
+        ref[...] = w_sum[:, i * chans : (i + 1) * chans]
+    for one in work:
+        one.drain()
+
+
+def hand_over(*refs):
+    n = len(refs) // 2
+    for src, dst in zip(refs[:n], refs[n:]):
+        dst[...] = src[...].reshape(dst.shape)
+
+
+def whole_block(axes, args):
+    (tokens, seg, gain1, bias1, gain2, bias2, q, k, v, o, up, down, taps, rate, inb, outc, skip, cot) = args
+    own, feats = tokens.shape
+    rows, chans = q.shape
+    units = up.shape[1]
     f32, bf16 = jnp.float32, jnp.bfloat16
     sds = jax.ShapeDtypeStruct
     vm = pl.BlockSpec(memory_space=pltpu.VMEM)
     sm = pl.BlockSpec(memory_space=pltpu.SMEM)
-    sq = pltpu.VMEM((LANES, LANES), f32)
-    full = pltpu.VMEM((rows, LANES), f32)
-    half = pltpu.VMEM((rows, LANES), bf16)
+    hbm = pl.BlockSpec(memory_space=pl.ANY)
+    scratch = layout(axes, own, feats, rows, chans, units, rate.shape[0])
+    wide, thin = sds((rows, units), f32), sds((rows, chans), f32)
+    row = sds((1, feats), f32)
+    outs = pl.pallas_call(
+        functools.partial(block_kernel, axes, INPUTS + OUTPUTS + tuple(scratch)),
+        out_shape=(
+            sds((own, feats), bf16), sds((own, feats), f32), row, row, row, row, thin, thin, thin, thin, wide, wide,
+            *(sds(a.shape, f32) for a in (taps, rate, inb, outc)), sds((1, chans), f32),
+        ),
+        in_specs=[hbm] * 8 + [vm] * 5 + [sm] + [vm] * 3 + [sm],
+        out_specs=(vm,) * 17,
+        scratch_shapes=list(scratch.values()),
+        compiler_params=pltpu.CompilerParams(
+            collective_id=1, has_side_effects=True, vmem_limit_bytes=63 << 20
+        ),
+        name="block",
+    )(tokens, cot, q, k, v, o, up, down, seg, gain1, bias1, gain2, bias2, taps, rate, inb, outc, skip[None])
+    final = [sds(a.shape, a.dtype) for a in outs]
+    for i in (2, 3, 4, 5):
+        final[i] = sds((feats,), f32)
+    final[16] = sds((chans,), f32)
     return pl.pallas_call(
-        functools.partial(mixer_bwd_kernel, un),
-        out_shape=(
-            sds((nb // 2, 3, chans, 2 * LANES), bf16),
-            sds((SHIFT, chans), f32),
-            sds((ns, chans), f32),
-            sds((ns, chans), f32),
-            sds((ns, chans), f32),
-            sds((1, chans), f32),
-        ),
-        in_specs=[vm] * 9 + [sm, sm, vm, vm, vm],
-        out_specs=(vm,) * 6,
-        scratch_shapes=[
-            sq, sq, sq, sq, full, full, full, full, half, full, full, full, full, sq,
-            pltpu.VMEM((SHIFT + 1, LANES, LANES), f32),
-        ],
-        compiler_params=pltpu.CompilerParams(vmem_limit_bytes=56 << 20),
-        name="mixer_bwd",
-    )(gm, qkv, core, s, f, urev, pp, kern, seg, shift_w, skip, rate, in_b, out_c)
+        hand_over, out_shape=tuple(final), in_specs=[vm] * 17, out_specs=(vm,) * 17, name="hand_over",
+    )(*outs)
 
 
 from jax.sharding import PartitionSpec as P
@@ -395,99 +1094,8 @@
 GROUP = ("head", "tensor")
 
 
-def norm_stats(x):
-    centred = x - jnp.mean(x, axis=0, keepdims=True)
-    spread = jnp.mean(centred * centred, axis=0, keepdims=True)
-    inv = lax.rsqrt(spread + 1e-05)
-    return centred * inv, inv
-
-
-def norm_back(grad, gain, hat, inv):
-    scaled = grad * gain
-    return inv * (
-        scaled
-        - jnp.mean(scaled, axis=0, keepdims=True)
-        - hat * jnp.mean(scaled * hat, axis=0, keepdims=True)
-    )
-
-
-def lanes_sum(x):
-    return jnp.sum(x, axis=1)
-
-
-def gelu_pair(pre):
-    cdf = 0.5 * (1.0 + lax.erf(pre * 0.7071067811865476))
-    return pre * cdf, cdf + pre * (0.3989422804014327 * jnp.exp(-0.5 * pre * pre))
-
-
-def on_device(
-    tokens, seg_ids, norm1_gain, norm1_bias, norm2_gain, norm2_bias, q_weight, k_weight, v_weight,
-    out_weight, up_weight, down_weight, shift_weight, decay_rate, in_coef, out_coef, skip_coef, cotangent,
-):
-    bf16, f32 = jnp.bfloat16, jnp.float32
-    chans = q_weight.shape[1]
-    own = tokens.shape[0]
-    feats = tokens.shape[1]
-    gather = lambda w: lax.all_gather(w, "dp", axis=0, tiled=True)
-    w_joint = gather(jnp.concatenate([q_weight, k_weight, v_weight], axis=1))
-    w_out = lax.all_gather(gather(out_weight), GROUP, axis=1, tiled=True)
-    w_up, w_down = gather(up_weight), gather(down_weight)
-    group_gather = lambda x: lax.all_gather(x, GROUP, axis=0, tiled=False)
-    scatter = lambda x: lax.psum_scatter(x, GROUP, scatter_dimension=0, tiled=False).astype(f32)
-    swap = lambda x: lax.all_to_all(x, GROUP, split_axis=0, concat_axis=0, tiled=True)
-    x = tokens.T.astype(f32)
-    g = cotangent.T
-    column = lambda v: v[:, None]
-    hat1, inv1 = norm_stats(x)
-    xn1 = group_gather((hat1 * column(norm1_gain) + column(norm1_bias)).astype(bf16))
-    cot = group_gather(g)
-    group = xn1.shape[0]
-    qkv = jnp.einsum("gdt,dc->cgt", xn1, w_joint, preferred_element_type=f32)
-    qkv = qkv.reshape(3, chans * group * own // LANES, LANES)
-    mixed, *saved = mixer_fwd(
-        qkv, seg_ids, shift_weight, skip_coef[None], decay_rate, in_coef, out_coef, un=16
-    )
-    mixed = swap(mixed).reshape(group * chans, own)
-    hidden = x + jnp.dot(w_out, mixed, preferred_element_type=f32)
-    hat2, inv2 = norm_stats(hidden)
-    xn2 = group_gather((hat2 * column(norm2_gain) + column(norm2_bias)).astype(bf16))
-    pre = jnp.einsum("gdt,df->gft", xn2, w_up, preferred_element_type=f32)
-    act, slope = gelu_pair(pre)
-    act = act.astype(bf16)
-    grad_act = jnp.einsum("gdt,df->gft", cot, w_down, preferred_element_type=f32)
-    grad_pre = (grad_act * slope).astype(bf16)
-    mlp = scatter(jnp.einsum("gft,df->gdt", act, w_down, preferred_element_type=f32).astype(bf16))
-    grad_xn2 = scatter(
-        jnp.einsum("gft,df->gdt", grad_pre, w_up, preferred_element_type=f32).astype(bf16)
-    )
-    grad_down = jnp.einsum("gdt,gft->df", cot, act, preferred_element_type=f32)
-    grad_up = jnp.einsum("gdt,gft->df", xn2, grad_pre, preferred_element_type=f32)
-    result = (hidden + mlp).astype(bf16).T
-    grad_hidden = g.astype(f32) + norm_back(grad_xn2, column(norm2_gain), hat2, inv2)
-    gain2, bias2 = lanes_sum(grad_xn2 * hat2), lanes_sum(grad_xn2)
-    grad_mix = grad_hidden.astype(bf16)
-    grad_mixed = lax.dot_general(w_out, grad_mix, TN, preferred_element_type=f32).astype(bf16)
-    grad_out = lax.dot_general(grad_mix, mixed, NT, preferred_element_type=f32)
-    grad_out = lax.psum_scatter(grad_out.astype(bf16), GROUP, scatter_dimension=1, tiled=True)
-    grad_mixed = swap(grad_mixed.reshape(group, chans, own))
-    dqkv, dshift, drate, dinb, doutc, dskip = mixer_bwd(
-        grad_mixed, qkv, *saved, seg_ids, shift_weight, skip_coef[None], decay_rate, in_coef, out_coef, un=16
-    )
-    dqkv = dqkv.reshape(group, 3 * chans, own)
-    grad_w = jnp.einsum("gdt,gct->dc", xn1, dqkv, preferred_element_type=f32)
-    grad_xn1 = scatter(
-        jnp.einsum("gct,dc->gdt", dqkv, w_joint, preferred_element_type=f32).astype(bf16)
-    )
-    grad_x = (grad_hidden + norm_back(grad_xn1, column(norm1_gain), hat1, inv1)).T
-    gain1, bias1 = lanes_sum(grad_xn1 * hat1), lanes_sum(grad_xn1)
-    reduce = lambda v: lax.psum_scatter(v, "dp", scatter_dimension=0, tiled=True)
-    grad_w = reduce(grad_w)
-    sums = lax.psum((dshift, drate, dinb, doutc, dskip[0]), "dp")
-    norms = lax.psum((gain1, bias1, gain2, bias2), ("dp", "head", "tensor"))
-    return (
-        result, grad_x, *norms, grad_w[:, :chans], grad_w[:, chans : 2 * chans], grad_w[:, 2 * chans :],
-        reduce(grad_out.astype(f32)), reduce(grad_up), reduce(grad_down), *sums,
-    )
+def on_device(*args):
+    return whole_block((lax.axis_size("dp"), lax.axis_size("head"), lax.axis_size("tensor")), args)
 
 
 def solution(mesh):

time: 512 us -> 148 us (0.29)
  waiting for transfers between devices: 252 us -> 0 us
  blocking collectives: 119 us -> 0 us
  Pallas kernels: 32.3 us -> 147 us
  matrix products: 37.1 us -> 0 us
  local copies, waits for them, and re-layouts: 35.7 us -> 0 us
  other arithmetic: 16 us -> 0 us
  between operations: 14.4 us -> 0.85 us
    reduce_scatter x6 -> x0, waiting for transfers between devices: 151 us -> none  [the longest x3 136 us: on_device(): lax.psum_scatter(x, GROUP, scatter_dimension=0, tiled=False).astype(f32)]
    pallas_call x2, Pallas kernels: 32.3 us -> 147 us  [the longest x1 144 us: whole_block(): pl.pallas_call(functools.partial(block_kernel, axes, INPUTS + OUTPUTS + t...]
    all_gather x4 -> x0, blocking collectives: 66.6 us -> none  [on_device(): gather = lambda w: lax.all_gather(w, 'dp', axis=0, tiled=True)]
    unnamed x15 -> x0, waiting for transfers between devices: 42.5 us -> none
    psum x1 -> x0, blocking collectives: 41.6 us -> none  [on_device(): norms = lax.psum((gain1, bias1, gain2, bias2), ('dp', 'head', 'tensor'))]
    dot_general x12 -> x0, matrix products: 37.1 us -> none  [the longest x1 5.21 us: on_device(): pre = jnp.einsum('gdt,df->gft', xn2, w_up, preferred_element_type=f32)]
    psum x1 -> x0, waiting for transfers between devices: 37 us -> none  [on_device(): sums = lax.psum((dshift, drate, dinb, doutc, dskip[0]), 'dp')]
    unnamed x72 -> x0, local copies, waits for them, and re-layouts: 19.8 us -> none
  transfers between devices with their start and end apart: 14 -> 0, of which waited for: 10 -> 0; matrix products, arithmetic and copies ran while one was open for 11% -> 0% of each run, Pallas kernels for 6% -> 0%
where the time goes in v4:
time: 148 us
  Pallas kernels  147 us (99%)
    pallas_call x1, Pallas kernels, whole_block(): pl.pallas_call(functools.partial(block_kernel, axes, INPUTS + OUTPUTS + t...  144 us
    pallas_call x1, Pallas kernels, whole_block(): pl.pallas_call(hand_over, out_shape=tuple(final), in_specs=[vm] * 17, out...  3.06 us

profile of v4, /device:TPU:0, one launch (start us, length us, event | category | flops | bytes accessed | tf_op | source)
XLA Modules:
  0.0 147.7 jit_solution(954960304569771135)
XLA Ops:
  0.7 143.7 %block.1 = (bf16[256,768]{1,0:T(8,128)(2,1)}, f32[256,768]{1,0:T(8,128)}, f32[1,768]{1,0:T(1,128)}, f32[1,768]{1,0:T(1,128)}, f32[1,768]{1,0:T(1,128)}, /*index=...) custom-call(bf16[256,768]{1,0:T(8,128)(2,1)} %refs_0_.1, ...), custom_call_target="tpu_custom_call" | custom-call | tf_op jit(solution)/shard_map/block/pallas_call | solution.py:1069
  144.4 3.1 %hand_over.1 = (bf16[256,768]{1,0:T(8,128)(2,1)}, f32[256,768]{1,0:T(8,128)}, f32[768]{0:T(1024)}, f32[768]{0:T(1024)}, f32[768]{0:T(1024)}, /*index=5*/f32[768]...) custom-call(bf16[256,768]{1,0:T(8,128)(2,1)} %get-tuple-element.34.r, ...), custom_call_target="tpu_custom_call" | custom-call | tf_op jit(solution)/shard_map/hand_over/pallas_call | solution.py:1087

commit v5 on v4

--- a/solution.py
+++ b/solution.py
@@ -7,6 +7,7 @@
 LANES = 128
 SHIFT = 4
 SEQS = 3
+PARTS = 2
 NT = (((1,), (1,)), ((), ()))
 TN = (((0,), (0,)), ((), ()))
 NN = (((1,), (0,)), ((), ()))
@@ -147,8 +148,9 @@
             f_ref[rows, :] = mm(urk, pp)
         return 0
 
-    lax.fori_loop(0, chans // un, fresh_step, 0)
-    yield
+    for part in range(PARTS):
+        lax.fori_loop(part * chans // PARTS // un, (part + 1) * chans // PARTS // un, fresh_step, 0)
+        yield
     across = e_scr[0:chans, :]
     b_ext = b_scr[0:chans, :]
     state = jnp.zeros((chans, LANES), jnp.float32)
@@ -173,13 +175,15 @@
             u_scr[rows, :] = qkv_ref[0, rows] * core
         return 0
 
-    lax.fori_loop(0, chans // un, out_step, 0)
-    yield
-    for b in range(nb):
-        half = b % 2
-        mixed_ref[b // 2, :, half * LANES : (half + 1) * LANES] = u_scr[
-            pl.ds(b, chans, stride=nb), :
-        ].astype(jnp.bfloat16)
+    count = chans // PARTS
+    for part in range(PARTS):
+        lax.fori_loop(part * count // un, (part + 1) * count // un, out_step, 0)
+        for b in range(nb):
+            half = b % 2
+            mixed_ref[b // 2, part * count : (part + 1) * count, half * LANES : (half + 1) * LANES] = u_scr[
+                pl.ds(part * count * nb + b, count, stride=nb), :
+            ].astype(jnp.bfloat16)
+        yield
 
 
 def mixer_backward(
@@ -202,11 +206,6 @@
     red_scr[...] = jnp.zeros_like(red_scr)
     gr_scr[...] = jnp.zeros_like(gr_scr)
 
-    for b in range(nb):
-        half = b % 2
-        x_scr[pl.ds(b, chans, stride=nb), :] = gm_ref[
-            b // 2, :, half * LANES : (half + 1) * LANES
-        ].astype(jnp.float32)
     corner = iota((LANES, LANES), 0) + iota((LANES, LANES), 1) >= LANES - 1
 
     def grad_step(i, _):
@@ -233,8 +232,20 @@
             h_scr[rows, :] = mm((g * live).astype(jnp.bfloat16), pp)
         return 0
 
-    lax.fori_loop(0, chans // un, grad_step, 0)
-    yield
+    count = chans // PARTS
+    for part in range(PARTS):
+        for b in range(nb):
+            half = b % 2
+            x_scr[pl.ds(part * count * nb + b, count, stride=nb), :] = gm_ref[
+                b // 2, part * count : (part + 1) * count, half * LANES : (half + 1) * LANES
+            ].astype(jnp.float32)
+        lax.fori_loop(part * count // un, (part + 1) * count // un, grad_step, 0)
+        yield
+    for b in range(nb):
+        half = b % 2
+        dqkv_ref[b // 2, 0, :, half * LANES : (half + 1) * LANES] = dq_scr[
+            pl.ds(b, chans, stride=nb), :
+        ].astype(jnp.bfloat16)
     across = e_scr[0:chans, :]
     b_ext = b_scr[0:chans, :]
     c_ext = c_scr[0:chans, :]
@@ -250,6 +261,39 @@
         x_scr[here, :] = b_ext * adj
         adj = c_ext * h + across * carry[b : b + 1, :] * adj
 
+    dskip_ref[...] = jnp.sum(red_scr[SHIFT].T, axis=0, keepdims=True)[:, 0:chans]
+    tscr[...] = gr_scr[...].T
+
+    def kern_back(i, carried):
+        e, zeroth, first = carried
+        block = tscr[pl.ds(pl.multiple_of(i * 8, 8), 8), 0:chans]
+        for j in range(8):
+            term = e * block[j : j + 1, :]
+            zeroth = zeroth + term
+            first = first + term * (i * 8 + j).astype(jnp.float32)
+            e = e * decay
+        return e, zeroth, first
+
+    blank = jnp.zeros((ns, chans), jnp.float32)
+    _, zeroth, first = lax.fori_loop(0, LANES // 8, kern_back, (blank + 1.0, blank, blank))
+
+    def back(x):
+        tscr[...] = jnp.zeros_like(tscr)
+        tscr[0:chans, :] = x
+        y = tscr[...].T
+        return y[0:ns, 0:chans], y[ns : 2 * ns, 0:chans]
+
+    d_out, s_h1 = back(acc_out)
+    d_inp, ds_f1 = back(acc_in)
+    d_carry, _ = back(acc_carry)
+    dinb_ref[...] = decay * d_inp + out_c * zeroth
+    doutc_ref[...] = d_out + in_b * zeroth
+    drate_ref[...] = -(
+        out_c * s_h1
+        + in_b * decay * (ds_f1 + d_inp)
+        + LANES * jnp.exp(-rate * LANES) * d_carry
+        + in_b * out_c * first
+    )
     yield
 
     def back_step(i, _):
@@ -299,46 +343,13 @@
     yield
     for b in range(nb):
         half = b % 2
-        for i, scr in enumerate((dq_scr, dk_scr, dv_scr)):
+        for i, scr in ((1, dk_scr), (2, dv_scr)):
             dqkv_ref[b // 2, i, :, half * LANES : (half + 1) * LANES] = scr[
                 pl.ds(b, chans, stride=nb), :
             ].astype(jnp.bfloat16)
     yield
     for j in range(SHIFT):
         dsw_ref[j : j + 1, :] = jnp.sum(red_scr[j].T, axis=0, keepdims=True)[:, 0:chans]
-    dskip_ref[...] = jnp.sum(red_scr[SHIFT].T, axis=0, keepdims=True)[:, 0:chans]
-    tscr[...] = gr_scr[...].T
-
-    def kern_back(i, carried):
-        e, zeroth, first = carried
-        block = tscr[pl.ds(pl.multiple_of(i * 8, 8), 8), 0:chans]
-        for j in range(8):
-            term = e * block[j : j + 1, :]
-            zeroth = zeroth + term
-            first = first + term * (i * 8 + j).astype(jnp.float32)
-            e = e * decay
-        return e, zeroth, first
-
-    blank = jnp.zeros((ns, chans), jnp.float32)
-    _, zeroth, first = lax.fori_loop(0, LANES // 8, kern_back, (blank + 1.0, blank, blank))
-
-    def back(x):
-        tscr[...] = jnp.zeros_like(tscr)
-        tscr[0:chans, :] = x
-        y = tscr[...].T
-        return y[0:ns, 0:chans], y[ns : 2 * ns, 0:chans]
-
-    d_out, s_h1 = back(acc_out)
-    d_inp, ds_f1 = back(acc_in)
-    d_carry, _ = back(acc_carry)
-    dinb_ref[...] = decay * d_inp + out_c * zeroth
-    doutc_ref[...] = d_out + in_b * zeroth
-    drate_ref[...] = -(
-        out_c * s_h1
-        + in_b * decay * (ds_f1 + d_inp)
-        + LANES * jnp.exp(-rate * LANES) * d_carry
-        + in_b * out_c * first
-    )
 
 
 MESH = pl.DeviceIdType.MESH
@@ -362,7 +373,7 @@
     def dp_peer(self, step):
         return (self.dp + step) % self.n_dp
 
-    def barrier(self, whole_group, over_dp):
+    def greet_all(self, whole_group, over_dp):
         sem = pltpu.get_barrier_semaphore()
 
         def greet(where):
@@ -384,7 +395,7 @@
 
             lax.fori_loop(1, self.n_dp, step, 0)
             count += self.n_dp - 1
-        pl.semaphore_wait(sem, count)
+        return lambda: pl.semaphore_wait(sem, count)
 
 
 def remote(src, dst, ssem, rsem, where):
@@ -486,6 +497,71 @@
         self._loop(lambda i: self._copy(i, pc.dp, pc.dp_peer(i)).wait_send())
 
 
+class LineGather:
+    def __init__(self, place, ref, ssem, rsem):
+        self.pc, self.ref, self.ssem, self.rsem = place, ref, ssem, rsem
+        self.n, self.at = place.n_dp, place.dp
+        self.steps = self.n - 1
+
+    def _copy(self, slot, way):
+        return remote(
+            self.ref.at[slot], self.ref.at[slot], self.ssem.at[way * self.n + slot], self.rsem.at[slot],
+            {"dp": self.at + 1 - 2 * way},
+        )
+
+    def _pass(self, slot):
+        @pl.when((slot <= self.at) & (self.at < self.n - 1))
+        def _():
+            self._copy(slot, 0).start()
+
+        @pl.when((slot >= self.at) & (self.at > 0))
+        def _():
+            self._copy(slot, 1).start()
+
+    def start(self):
+        self._pass(self.at)
+
+    def step(self, s):
+        below, above = self.at - 1 - s, self.at + 1 + s
+
+        @pl.when(below >= 0)
+        def _():
+            self._copy(below, 0).wait_recv()
+
+            @pl.when(self.at < self.n - 1)
+            def _():
+                self._copy(below, 0).start()
+
+        @pl.when(above < self.n)
+        def _():
+            self._copy(above, 1).wait_recv()
+
+            @pl.when(self.at > 0)
+            def _():
+                self._copy(above, 1).start()
+
+    def rest(self, first):
+        def body(s, _):
+            self.step(s)
+            return 0
+
+        lax.fori_loop(first, self.steps, body, 0)
+
+    def drain(self):
+        def body(slot, _):
+            @pl.when((slot <= self.at) & (self.at < self.n - 1))
+            def _():
+                self._copy(slot, 0).wait_send()
+
+            @pl.when((slot >= self.at) & (self.at > 0))
+            def _():
+                self._copy(slot, 1).wait_send()
+
+            return 0
+
+        lax.fori_loop(0, self.n, body, 0)
+
+
 def joined(ref):
     n, rows, columns = ref.shape
     if rows % 16 == 0:
@@ -537,13 +613,15 @@
             self.part.dtype
         )
 
-    def far(self):
-        self.pair(0)
-        self.give(4, 5)
+    def side(self):
         self.pair(1)
         self.give(6)
         self.pair(2)
         self.give(7)
+
+    def far(self):
+        self.pair(0)
+        self.give(4, 5)
 
     def near(self):
         for i, s, rows in ((4, self.pc.y, self.top), (5, self.pc.x, self.low)):
@@ -578,8 +656,9 @@
 
 
 class GroupSwap:
-    def __init__(self, place, src, dst, lsem, ssem, rsem):
+    def __init__(self, place, src, dst, lsem, rows, ssem, rsem):
         self.pc, self.src, self.dst, self.ssem, self.rsem, self.lsem = place, src, dst, ssem, rsem, lsem
+        self.rows = rows
 
     def _peer(self, i):
         return (self.pc.me + i) % self.pc.size
@@ -587,10 +666,13 @@
     def _copy(self, i, slot):
         peer = self._peer(i)
         where = {"head": peer // self.pc.n_tensor, "tensor": peer % self.pc.n_tensor}
-        return remote(self.src.at[peer], self.dst.at[slot], self.ssem.at[i], self.rsem.at[i], where)
+        return remote(
+            self.src.at[peer, self.rows], self.dst.at[slot, self.rows], self.ssem.at[i], self.rsem.at[i], where
+        )
 
     def _own(self):
-        return pltpu.make_async_copy(self.src.at[self.pc.me], self.dst.at[self.pc.me], self.lsem)
+        me = self.pc.me
+        return pltpu.make_async_copy(self.src.at[me, self.rows], self.dst.at[me, self.rows], self.lsem)
 
     def start(self):
         for i in range(1, self.pc.size):
@@ -693,7 +775,7 @@
             self._copy(i, self.pc.me).wait_send()
 
 
-TAPS_AT, SKIP_AT, PARAM_ROWS = 192, 208, 224
+SKIP_AT, PARAM_ROWS = 192, 208
 UNROLL = 16
 
 
@@ -733,7 +815,10 @@
         hat=v((own, feats), f32), hid=v((own, feats), f32), ghid=v((own, feats), f32),
         up_part=v((n_dp, rows, units), bf16), up_land=v((n_dp, rows, units), bf16),
         dn_part=v((n_dp, rows, units), bf16), dn_land=v((n_dp, rows, units), bf16),
-        w_part=v((n_dp, rows, 4 * chans), bf16), w_land=v((n_dp, rows, 4 * chans), bf16),
+        q_part=v((n_dp, rows, chans), bf16), q_land=v((n_dp, rows, chans), bf16),
+        o_out=v((n_dp, rows, chans), bf16), o_in=v((n_dp, rows, chans), bf16),
+        kv_part=v((n_dp, rows, 2 * chans), bf16), kv_land=v((n_dp, rows, 2 * chans), bf16),
+        taps_all=v((n_dp, 8, LANES), f32),
         params=v((n_dp, PARAM_ROWS, LANES), bf16),
         n1=v((group, 2, feats), f32), n2=v((group, 2, feats), f32), m1=v((n_dp, 2, feats), f32), m2=v((n_dp, 2, feats), f32),
     )
@@ -742,8 +827,8 @@
             out[f"{name}_{part}"] = alloc
     for name, count in (
         ("xn1", 11), ("cots", 11), ("wout", 11), ("xn2", 11), ("x2", 10), ("m", 10), ("o", 10), ("x1", 10),
-        ("in", group), ("back", group), ("sp1", group), ("sp2", group),
-        ("zq", n_dp), ("zu", n_dp), ("zd", n_dp), ("gu", n_dp), ("gd", n_dp), ("gw", n_dp), ("zp", n_dp),
+        ("in0", group), ("in1", group), ("back0", group), ("back1", group), ("sp1", group), ("sp2", group),
+        ("zq", n_dp), ("zu", n_dp), ("zd", n_dp), ("gu", n_dp), ("gd", n_dp), ("gq", n_dp), ("go", n_dp), ("gkv", n_dp), ("zt", n_dp), ("zp", n_dp),
         ("zn1", n_dp), ("zn2", n_dp),
     ):
         out[f"send_{name}"] = dma(count)
@@ -798,10 +883,7 @@
     load_cot = local(5, r.cot_hbm, r.cot)
     load_up = local(6, r.up_hbm, r.wup.at[pc.dp])
     load_down = local(7, r.down_hbm, r.wdown.at[pc.dp])
-    pc.barrier(True, True)
-    for copy in four:
-        copy.wait()
-    r.wqkvo[pc.dp] = jnp.concatenate([r.four[i] for i in range(4)], axis=1)
+    meet = pc.greet_all(True, True)
     z_qkvo = make(DepthGather, "zq", r.wqkvo)
     z_up = make(DepthGather, "zu", r.wup)
     z_down = make(DepthGather, "zd", r.wdown)
@@ -809,27 +891,31 @@
     cot_g = make(GroupGather, "cots", r.cots)
     out_g = make(GroupGather, "wout", r.wout)
     xn2_g = make(GroupGather, "xn2", r.xn2)
-    z_qkvo.start()
-    load_tok.wait()
-    x = r.tok[...].astype(f32)
+    halves = [pl.ds(i * (chans // PARTS), chans // PARTS) for i in range(PARTS)]
+    swap_in = [make(GroupSwap, f"in{i}", r.mixed, r.mixed_in, r.local.at[8 + i], rows) for i, rows in enumerate(halves)]
+    swap_back = [make(GroupSwap, f"back{i}", r.gmix, r.gmix_in, r.local.at[10 + i], rows) for i, rows in enumerate(halves)]
     gain1, gain2 = r.gain1[...].reshape(1, feats), r.gain2[...].reshape(1, feats)
     bias1, bias2 = r.bias1[...].reshape(1, feats), r.bias2[...].reshape(1, feats)
-    hat1, _ = row_norm(x)
+    load_tok.wait()
+    hat1, _ = row_norm(r.tok[...].astype(f32))
     r.xn1[pc.me] = (hat1 * gain1 + bias1).astype(bf16).T
+    for copy in four:
+        copy.wait()
+    r.wqkvo[pc.dp] = jnp.concatenate([r.four[i] for i in range(4)], axis=1)
+    meet()
     xn1_g.start()
-    load_up.wait()
-    z_up.start()
-    load_down.wait()
-    z_down.start()
+    z_qkvo.start()
     load_cot.wait()
     r.cots[pc.me] = r.cot[...].T
     xn1_g.first()
-    cot_g.start()
     xn1_g.second()
     z_qkvo.finish()
+    load_up.wait()
+    z_up.start()
     r.wt[...] = joined(r.wqkvo).T
     r.wout[pc.me] = r.wt[3 * chans :, :]
     out_g.start()
+    load_down.wait()
 
     def project(s):
         y = mm(r.wt[0 : 3 * chans, :], r.xn1[s])
@@ -844,21 +930,18 @@
     for s in range(group):
         project(s)
 
-    def cot_first():
-        cot_g.first()
-
-    def cot_second():
-        cot_g.second()
+    def after_drive():
         out_g.first()
-
-    def late_weights():
+        out_g.second()
+        cot_g.start()
+
+    def after_scan():
+        out_g.third()
+
+    def half_out():
+        swap_in[0].start()
         z_up.finish()
-        r.wupt[...] = joined(r.wup).T
-        out_g.second()
-
-    def cot_third():
-        cot_g.third()
-        out_g.third()
+        z_down.start()
 
     mixer = (r.seg, r.taps, r.skip, r.rate, r.inb, r.outc)
     run_beside(
@@ -866,25 +949,28 @@
             UNROLL, r.qkv, *mixer, r.mixed, r.core, r.s, r.f, r.urev, r.pp, r.kern,
             r.t0, r.t1, r.t2, r.t3, r.t4, r.w0, r.t5,
         ),
-        (cot_first, cot_second, late_weights, cot_third),
+        (after_drive, lambda: None, lambda: None, after_scan, half_out, swap_in[1].start),
     )
-    swap_in = make(GroupSwap, "in", r.mixed, r.mixed_in, r.local.at[8])
-    swap_in.start()
+    cot_g.first()
     out_g.finish()
-    cot_g.finish()
+    cot_g.second()
+    w_up = joined(r.wup)
+    r.wupt[...] = w_up.T
+    wout_t = r.wout[...].reshape(feats, feats)
+    swap_in[0].finish()
+    swap_in[1].finish()
+    mixed_t = r.mixed_in[...].reshape(feats, own)
+    hidden = r.tok[...].astype(f32) + mm(mixed_t, wout_t, TN)
+    hat2, inv2 = row_norm(hidden)
+    r.xn2[pc.me] = (hat2 * gain2 + bias2).astype(bf16).T
+    xn2_g.start()
+    r.hid[...] = hidden
+    r.hat[...] = hat2
+    cot_g.third()
     z_down.finish()
     w_down = joined(r.wdown)
     r.wdownt[...] = w_down.T
-    w_up = joined(r.wup)
-    swap_in.finish()
-    mixed_t = r.mixed_in[...].reshape(feats, own)
-    wout_t = r.wout[...].reshape(feats, feats)
-    hidden = r.tok[...].astype(f32) + mm(mixed_t, wout_t, TN)
-    r.hid[...] = hidden
-    hat2, inv2 = row_norm(hidden)
-    r.xn2[pc.me] = (hat2 * gain2 + bias2).astype(bf16).T
-    xn2_g.start()
-    r.hat[...] = hat2
+    cot_g.finish()
     red_x2 = make(GroupReduce, "x2", r.x_part, r.x_land, r.x_half, r.x_last)
     red_m = make(GroupReduce, "m", r.m_part, r.m_land, r.m_half, r.m_last)
     red_o = make(GroupReduce, "o", r.o_part, r.o_land, r.o_half, r.o_last)
@@ -911,10 +997,12 @@
     chunk(pc.py)
     red_x2.give(2)
     xn2_g.third()
+    red_x2.side()
     chunk(pc.d)
     xn2_g.arrive(9, 10)
     chunk(pc.pd)
     red_x2.give(0)
+    red_x2.pair(3)
     red_x2.far()
     units = r.act.shape[1]
     grad_up = jnp.zeros((feats, units), f32)
@@ -924,7 +1012,6 @@
     sum_up = make(DepthReduce, "gu", r.up_part, r.up_land)
     sum_up.start()
     red_x2.near()
-    red_x2.pair(3)
     for i, s in enumerate(red_m.theirs):
         r.m_part[s] = mm(w_down, r.act[s]).astype(bf16)
         red_m.give(i)
@@ -942,42 +1029,53 @@
     r.ghid[...] = grad_hidden
     grad_mix = grad_hidden.astype(bf16)
     r.gmix[...] = mm(wout_t, grad_mix, NT).astype(bf16).reshape(group, chans, own)
-    swap_back = make(GroupSwap, "back", r.gmix, r.gmix_in, r.local.at[9])
-    swap_back.start()
+    swap_back[0].start()
+    swap_back[1].start()
     r.n2[pc.me, 0:1, :] = jnp.sum(grad_xn * hat2, axis=0, keepdims=True)
     r.n2[pc.me, 1:2, :] = jnp.sum(grad_xn, axis=0, keepdims=True)
     spread2 = make(GroupSpread, "sp2", r.n2)
     spread2.start()
     r.o_part[...] = mm(mixed_t, grad_mix).astype(bf16).reshape(group, chans, feats)
     red_o.give(0, 1, 2, 3)
-    red_m.far()
-    red_o.far()
-    swap_back.finish()
+    swap_back[0].finish()
     norm2 = make(DepthGather, "zn2", r.m2)
 
-    def near_sums():
+    ns = r.drate.shape[0]
+    pieces = ((0, r.drate, r.out_rate), (ns, r.dinb, r.out_inb), (2 * ns, r.doutc, r.out_outc),
+              (SKIP_AT, r.dskip, r.out_skip))
+    z_par = make(DepthGather, "zp", r.params)
+    sum_q = make(DepthReduce, "gq", r.q_part, r.q_land)
+    sum_o = make(DepthReduce, "go", r.o_out, r.o_in)
+    sum_kv = make(DepthReduce, "gkv", r.kv_part, r.kv_land)
+
+    def second_half():
+        swap_back[1].finish()
+        red_o.far()
+        red_o.side()
+        red_m.far()
+
+    def early_sums():
+        red_o.near()
+        r.params[pc.dp] = jnp.zeros(r.params.shape[1:], bf16)
+        for at, ref, _ in pieces:
+            r.params[pc.dp, at : at + ref.shape[0], 0:chans] = ref[...].astype(bf16)
+        z_par.start()
+        grad_q = jnp.zeros((feats, chans), f32)
+        for s in range(group):
+            grad_q = grad_q + mm(r.xn1[s], r.dqkv[s, 0], NT)
+        split_rows(r.q_part, grad_q)
+        sum_q.start()
+
+    def mlp_sums():
+        red_m.side()
         red_m.near()
-        red_o.near()
-        spread2.finish()
-        r.m2[pc.dp] = jnp.sum(r.n2[...], axis=0)
-        norm2.start()
-
-    def own_sums():
-        red_m.pair(3)
-        red_o.pair(3)
         red_x2.drain()
         work.remove(red_x2)
 
-    def last_sums():
-        r.res[...] = (r.hid[...] + red_m.total().T).astype(bf16)
-        norm2.finish()
-        sums = jnp.sum(r.m2[...], axis=0)
-        r.g2[...] = sums[0:1]
-        r.b2[...] = sums[1:2]
-
-    def depth_sums():
-        r.dup[...] = sum_up.total()
-        r.ddown[...] = sum_down.total()
+    def out_sums():
+        red_o.pair(3)
+        split_rows(r.o_out, red_o.total().T)
+        sum_o.start()
 
     w_joint = joined(r.wqkvo)
     red_x1 = make(GroupReduce, "x1", r.x_part, r.x_land, r.x_half, r.x_last)
@@ -990,11 +1088,26 @@
         r.x_part[s] = mm(w_joint, padded).astype(bf16)
 
     def start_back():
-        for i, s in enumerate(red_x1.theirs):
-            chunk_back(s)
-            red_x1.give(i)
-        for s in red_x1.mine:
-            chunk_back(s)
+        theirs, mine = red_x1.theirs, red_x1.mine
+        chunk_back(theirs[0])
+        red_x1.give(0)
+        chunk_back(mine[0])
+        chunk_back(theirs[1])
+        red_x1.give(1)
+        chunk_back(mine[1])
+        grad_kv = jnp.zeros((feats, 2 * chans), f32)
+        for s in range(group):
+            grad_kv = grad_kv + mm(r.xn1[s], grads(s)[chans:], NT)
+        split_rows(r.kv_part, grad_kv)
+        sum_kv.start()
+        red_x1.far()
+        chunk_back(theirs[2])
+        red_x1.give(2)
+        chunk_back(mine[2])
+        chunk_back(theirs[3])
+        red_x1.give(3)
+        red_x1.side()
+        chunk_back(mine[3])
 
     run_beside(
         mixer_backward(
@@ -1002,25 +1115,21 @@
             r.dqkv, r.dsw, r.drate, r.dinb, r.doutc, r.dskip,
             r.t0, r.t1, r.t2, r.t3, r.w0, r.w1, r.w2, r.w3, r.dur, r.w2, r.w4, r.w5, r.w6, r.gr, r.red,
         ),
-        (near_sums, own_sums, last_sums, depth_sums, start_back),
+        (second_half, lambda: None, early_sums, mlp_sums, out_sums, start_back),
     )
-    red_x1.far()
-    r.params[pc.dp] = jnp.zeros(r.params.shape[1:], bf16)
-    ns = r.drate.shape[0]
-    pieces = ((0, r.drate, r.out_rate), (ns, r.dinb, r.out_inb), (2 * ns, r.doutc, r.out_outc),
-              (TAPS_AT, r.dsw, r.out_taps), (SKIP_AT, r.dskip, r.out_skip))
-    for at, ref, _ in pieces:
-        r.params[pc.dp, at : at + ref.shape[0], 0:chans] = ref[...].astype(bf16)
-    z_par = make(DepthGather, "zp", r.params)
-    z_par.start()
-    grad_w = jnp.zeros((feats, 3 * chans), f32)
-    for s in range(group):
-        grad_w = grad_w + mm(r.xn1[s], grads(s), NT)
-    split_rows(r.w_part, jnp.concatenate([grad_w, red_o.total().T], axis=1))
-    sum_w = make(DepthReduce, "gw", r.w_part, r.w_land)
-    sum_w.start()
+    r.taps_all[pc.dp] = jnp.zeros(r.taps_all.shape[1:], f32)
+    r.taps_all[pc.dp, 0:SHIFT, 0:chans] = r.dsw[...]
+    z_taps = make(DepthGather, "zt", r.taps_all)
+    z_taps.start()
+    spread2.finish()
+    r.m2[pc.dp] = jnp.sum(r.n2[...], axis=0)
+    norm2.start()
     red_x1.near()
     red_x1.pair(3)
+    red_m.pair(3)
+    r.res[...] = (r.hid[...] + red_m.total().T).astype(bf16)
+    r.dup[...] = sum_up.total()
+    r.ddown[...] = sum_down.total()
     hat1, inv1 = row_norm(r.tok[...].astype(f32))
     grad_xn = red_x1.total().T
     r.n1[pc.me, 0:1, :] = jnp.sum(grad_xn * hat1, axis=0, keepdims=True)
@@ -1036,13 +1145,21 @@
     sums = jnp.sum(r.params[...].astype(f32), axis=0)
     for at, ref, out in pieces:
         out[...] = sums[at : at + ref.shape[0], 0:chans]
+    z_taps.finish()
+    r.out_taps[...] = jnp.sum(r.taps_all[...], axis=0)[0:SHIFT, 0:chans]
+    norm2.finish()
+    sums = jnp.sum(r.m2[...], axis=0)
+    r.g2[...] = sums[0:1]
+    r.b2[...] = sums[1:2]
     norm1.finish()
     sums = jnp.sum(r.m1[...], axis=0)
     r.g1[...] = sums[0:1]
     r.b1[...] = sums[1:2]
-    w_sum = sum_w.total()
-    for i, ref in enumerate((r.dq, r.dk, r.dv, r.do)):
-        ref[...] = w_sum[:, i * chans : (i + 1) * chans]
+    r.do[...] = sum_o.total()
+    r.dq[...] = sum_q.total()
+    kv_sum = sum_kv.total()
+    r.dk[...] = kv_sum[:, 0:chans]
+    r.dv[...] = kv_sum[:, chans:]
     for one in work:
         one.drain()
 
@@ -1085,7 +1202,11 @@
         final[i] = sds((feats,), f32)
     final[16] = sds((chans,), f32)
     return pl.pallas_call(
-        hand_over, out_shape=tuple(final), in_specs=[vm] * 17, out_specs=(vm,) * 17, name="hand_over",
+        hand_over,
+        out_shape=tuple(final),
+        in_specs=[vm] * 17,
+        out_specs=(vm,) * 17,
+        name="hand_over",
     )(*outs)
 
 

time: 148 us -> 136 us (0.919)
  Pallas kernels: 147 us -> 135 us
    pallas_call x1, Pallas kernels: 144 us -> 132 us  [whole_block(): pl.pallas_call(functools.partial(block_kernel, axes, INPUTS + OUTPUTS + t...]
where the time goes in v5:
time: 136 us
  Pallas kernels  135 us (99%)
    pallas_call x1, Pallas kernels, whole_block(): pl.pallas_call(functools.partial(block_kernel, axes, INPUTS + OUTPUTS + t...  132 us
    pallas_call x1, Pallas kernels, whole_block(): pl.pallas_call(hand_over, out_shape=tuple(final), in_specs=[vm] * 17, out...  3.06 us

profile of v5, /device:TPU:0, one launch (start us, length us, event | category | flops | bytes accessed | tf_op | source)
XLA Modules:
  0.0 136.1 jit_solution(9564267779093626932)
XLA Ops:
  0.7 132.2 %block.1 = (bf16[256,768]{1,0:T(8,128)(2,1)}, f32[256,768]{1,0:T(8,128)}, f32[1,768]{1,0:T(1,128)}, f32[1,768]{1,0:T(1,128)}, f32[1,768]{1,0:T(1,128)}, /*index=...) custom-call(bf16[256,768]{1,0:T(8,128)(2,1)} %refs_0_.1, ...), custom_call_target="tpu_custom_call" | custom-call | tf_op jit(solution)/shard_map/block/pallas_call | solution.py:1186
  132.9 3.1 %hand_over.1 = (bf16[256,768]{1,0:T(8,128)(2,1)}, f32[256,768]{1,0:T(8,128)}, f32[768]{0:T(1024)}, f32[768]{0:T(1024)}, f32[768]{0:T(1024)}, /*index=5*/f32[768]...) custom-call(bf16[256,768]{1,0:T(8,128)(2,1)} %get-tuple-element.34.r, ...), custom_call_target="tpu_custom_call" | custom-call | tf_op jit(solution)/shard_map/hand_over/pallas_call | solution.py:1204

commit v6 on v5

--- a/solution.py
+++ b/solution.py
@@ -776,7 +776,7 @@
 
 
 SKIP_AT, PARAM_ROWS = 192, 208
-UNROLL = 16
+UNROLL = 24
 
 
 class Names:
@@ -786,7 +786,7 @@
             setattr(self, name, ref)
 
 
-def layout(axes, own, feats, rows, chans, units, ns):
+def layout(axes, own, feats, rows, chans, units, ns, results):
     n_dp, n_head, n_tensor = axes
     group = n_head * n_tensor
     f32, bf16 = jnp.float32, jnp.bfloat16
@@ -822,6 +822,11 @@
         params=v((n_dp, PARAM_ROWS, LANES), bf16),
         n1=v((group, 2, feats), f32), n2=v((group, 2, feats), f32), m1=v((n_dp, 2, feats), f32), m2=v((n_dp, 2, feats), f32),
     )
+    out.update(
+        seg=v((1, group * own), jnp.int32), rate=v((ns, chans), f32), inb=v((ns, chans), f32), outc=v((ns, chans), f32),
+        gain1=v((feats,), f32), bias1=v((feats,), f32), gain2=v((feats,), f32), bias2=v((feats,), f32),
+    )
+    out.update((name, v(a.shape, a.dtype)) for name, a in zip(RESULTS, results))
     for name, height, width in (("x", feats, own), ("m", feats, own), ("o", chans, feats)):
         for part, alloc in zip(("part", "land", "half", "last"), GroupReduce.scratch(group, height, width)):
             out[f"{name}_{part}"] = alloc
@@ -834,17 +839,21 @@
         out[f"send_{name}"] = dma(count)
         out[f"recv_{name}"] = dma(count)
     out["local"] = dma(12)
+    out["small"] = dma(len(SMALL))
+    out["given"] = dma(len(RESULTS))
     return out
 
 
 INPUTS = (
     "tok_hbm", "cot_hbm", "q_hbm", "k_hbm", "v_hbm", "o_hbm", "up_hbm", "down_hbm",
-    "seg", "gain1", "bias1", "gain2", "bias2", "taps", "rate", "inb", "outc", "skip",
+    "seg_hbm", "gain1_hbm", "bias1_hbm", "gain2_hbm", "bias2_hbm", "taps", "rate_hbm", "inb_hbm", "outc_hbm", "skip",
 )
-OUTPUTS = (
+RESULTS = (
     "res", "gx", "g1", "b1", "g2", "b2", "dq", "dk", "dv", "do", "dup", "ddown",
     "out_taps", "out_rate", "out_inb", "out_outc", "out_skip",
 )
+OUTPUTS = tuple(name + "_hbm" for name in RESULTS)
+SMALL = ("seg", "gain1", "bias1", "gain2", "bias2", "rate", "inb", "outc")
 
 
 def run_beside(body, tasks):
@@ -878,8 +887,20 @@
         copy.start()
         return copy
 
+    load_tok = local(4, r.tok_hbm, r.tok)
+    small = []
+    for i, name in enumerate(SMALL):
+        small.append(pltpu.make_async_copy(getattr(r, name + "_hbm"), getattr(r, name), r.small.at[i]))
+        small[-1].start()
+    given = []
+
+    def give(*which):
+        for name in which:
+            i = RESULTS.index(name)
+            given.append(pltpu.make_async_copy(getattr(r, name), getattr(r, name + "_hbm"), r.given.at[i]))
+            given[-1].start()
+
     four = [local(i, src, r.four.at[i]) for i, src in enumerate((r.q_hbm, r.k_hbm, r.v_hbm, r.o_hbm))]
-    load_tok = local(4, r.tok_hbm, r.tok)
     load_cot = local(5, r.cot_hbm, r.cot)
     load_up = local(6, r.up_hbm, r.wup.at[pc.dp])
     load_down = local(7, r.down_hbm, r.wdown.at[pc.dp])
@@ -894,6 +915,8 @@
     halves = [pl.ds(i * (chans // PARTS), chans // PARTS) for i in range(PARTS)]
     swap_in = [make(GroupSwap, f"in{i}", r.mixed, r.mixed_in, r.local.at[8 + i], rows) for i, rows in enumerate(halves)]
     swap_back = [make(GroupSwap, f"back{i}", r.gmix, r.gmix_in, r.local.at[10 + i], rows) for i, rows in enumerate(halves)]
+    for copy in small:
+        copy.wait()
     gain1, gain2 = r.gain1[...].reshape(1, feats), r.gain2[...].reshape(1, feats)
     bias1, bias2 = r.bias1[...].reshape(1, feats), r.bias2[...].reshape(1, feats)
     load_tok.wait()
@@ -1054,7 +1077,11 @@
         red_o.side()
         red_m.far()
 
+    def row_of(x):
+        return jnp.broadcast_to(jnp.sum(x, axis=1, keepdims=True), (x.shape[0], LANES)).T[0:1]
+
     def early_sums():
+        w_wide = joined(r.wqkvo).astype(f32)
         red_o.near()
         r.params[pc.dp] = jnp.zeros(r.params.shape[1:], bf16)
         for at, ref, _ in pieces:
@@ -1065,6 +1092,7 @@
             grad_q = grad_q + mm(r.xn1[s], r.dqkv[s, 0], NT)
         split_rows(r.q_part, grad_q)
         sum_q.start()
+        r.n1[pc.me, 0:1, :] = row_of(grad_q * w_wide[:, 0:chans])
 
     def mlp_sums():
         red_m.side()
@@ -1086,6 +1114,9 @@
     def chunk_back(s):
         padded = jnp.concatenate([grads(s), jnp.zeros((chans, own), bf16)], axis=0)
         r.x_part[s] = mm(w_joint, padded).astype(bf16)
+
+    spread1 = make(GroupSpread, "sp1", r.n1)
+    norm1 = make(DepthGather, "zn1", r.m1)
 
     def start_back():
         theirs, mine = red_x1.theirs, red_x1.mine
@@ -1100,6 +1131,13 @@
             grad_kv = grad_kv + mm(r.xn1[s], grads(s)[chans:], NT)
         split_rows(r.kv_part, grad_kv)
         sum_kv.start()
+        w_wide = w_joint.astype(f32)
+        token_sums = jnp.zeros((8, 3 * chans), f32)
+        for s in range(group):
+            token_sums = token_sums + mm(jnp.ones((8, own), bf16), grads(s), NT)
+        r.n1[pc.me, 0:1, :] += row_of(grad_kv * w_wide[:, chans : 3 * chans])
+        r.n1[pc.me, 1:2, :] = row_of(w_wide[:, 0 : 3 * chans] * token_sums[0:1])
+        spread1.start()
         red_x1.far()
         chunk_back(theirs[2])
         red_x1.give(2)
@@ -1126,48 +1164,67 @@
     norm2.start()
     red_x1.near()
     red_x1.pair(3)
+    spread1.finish()
+    r.m1[pc.dp] = jnp.sum(r.n1[...], axis=0)
+    norm1.start()
     red_m.pair(3)
     r.res[...] = (r.hid[...] + red_m.total().T).astype(bf16)
+    give("res")
     r.dup[...] = sum_up.total()
     r.ddown[...] = sum_down.total()
-    hat1, inv1 = row_norm(r.tok[...].astype(f32))
-    grad_xn = red_x1.total().T
-    r.n1[pc.me, 0:1, :] = jnp.sum(grad_xn * hat1, axis=0, keepdims=True)
-    r.n1[pc.me, 1:2, :] = jnp.sum(grad_xn, axis=0, keepdims=True)
-    spread1 = make(GroupSpread, "sp1", r.n1)
-    spread1.start()
-    r.gx[...] = r.ghid[...] + row_norm_back(grad_xn, gain1, hat1, inv1)
-    spread1.finish()
-    r.m1[pc.dp] = jnp.sum(r.n1[...], axis=0)
-    norm1 = make(DepthGather, "zn1", r.m1)
-    norm1.start()
+    give("dup", "ddown")
     z_par.finish()
     sums = jnp.sum(r.params[...].astype(f32), axis=0)
     for at, ref, out in pieces:
         out[...] = sums[at : at + ref.shape[0], 0:chans]
+    give("out_rate", "out_inb", "out_outc", "out_skip")
     z_taps.finish()
     r.out_taps[...] = jnp.sum(r.taps_all[...], axis=0)[0:SHIFT, 0:chans]
+    give("out_taps")
     norm2.finish()
     sums = jnp.sum(r.m2[...], axis=0)
     r.g2[...] = sums[0:1]
     r.b2[...] = sums[1:2]
-    norm1.finish()
-    sums = jnp.sum(r.m1[...], axis=0)
-    r.g1[...] = sums[0:1]
-    r.b1[...] = sums[1:2]
+    give("g2", "b2")
     r.do[...] = sum_o.total()
     r.dq[...] = sum_q.total()
     kv_sum = sum_kv.total()
     r.dk[...] = kv_sum[:, 0:chans]
     r.dv[...] = kv_sum[:, chans:]
+    give("dq", "dk", "dv", "do")
+    norm1.finish()
+    sums = jnp.sum(r.m1[...], axis=0)
+    r.g1[...] = (sums[0:1] - bias1 * sums[1:2]) / gain1
+    r.b1[...] = sums[1:2]
+    give("g1", "b1")
+    hat1, inv1 = row_norm(r.tok[...].astype(f32))
+    grad_xn = red_x1.total().T
+    r.gx[...] = r.ghid[...] + row_norm_back(grad_xn, gain1, hat1, inv1)
+    give("gx")
     for one in work:
         one.drain()
-
-
-def hand_over(*refs):
-    n = len(refs) // 2
-    for src, dst in zip(refs[:n], refs[n:]):
-        dst[...] = src[...].reshape(dst.shape)
+    for copy in given:
+        copy.wait()
+
+
+def hand_over(count, *refs):
+    src, dst, mid, flat = refs[:count], refs[count : 2 * count], refs[2 * count : 3 * count], refs[3 * count : -2]
+    sem_in, sem_out = refs[-2:]
+    loads = [pltpu.make_async_copy(a, b, sem_in.at[i]) for i, (a, b) in enumerate(zip(src, mid))]
+    for load in loads:
+        load.start()
+    flat = iter(flat)
+    stores = []
+    for i, load in enumerate(loads):
+        load.wait()
+        held = mid[i]
+        if src[i].shape != dst[i].shape:
+            held = next(flat)
+            held[...] = mid[i][...].reshape(held.shape)
+        stores.append(pltpu.make_async_copy(held, dst[i], sem_out.at[i]))
+        stores[-1].start()
+    for store in stores:
+        store.wait()
 
 
 def whole_block(axes, args):
@@ -1180,20 +1237,21 @@
     vm = pl.BlockSpec(memory_space=pltpu.VMEM)
     sm = pl.BlockSpec(memory_space=pltpu.SMEM)
     hbm = pl.BlockSpec(memory_space=pl.ANY)
-    scratch = layout(axes, own, feats, rows, chans, units, rate.shape[0])
     wide, thin = sds((rows, units), f32), sds((rows, chans), f32)
     row = sds((1, feats), f32)
+    results = (
+        sds((own, feats), bf16), sds((own, feats), f32), row, row, row, row, thin, thin, thin, thin, wide, wide,
+        *(sds(a.shape, f32) for a in (taps, rate, inb, outc)), sds((1, chans), f32),
+    )
+    scratch = layout(axes, own, feats, rows, chans, units, rate.shape[0], results)
     outs = pl.pallas_call(
         functools.partial(block_kernel, axes, INPUTS + OUTPUTS + tuple(scratch)),
-        out_shape=(
-            sds((own, feats), bf16), sds((own, feats), f32), row, row, row, row, thin, thin, thin, thin, wide, wide,
-            *(sds(a.shape, f32) for a in (taps, rate, inb, outc)), sds((1, chans), f32),
-        ),
-        in_specs=[hbm] * 8 + [vm] * 5 + [sm] + [vm] * 3 + [sm],
-        out_specs=(vm,) * 17,
+        out_shape=results,
+        in_specs=[hbm] * 13 + [sm] + [hbm] * 3 + [sm],
+        out_specs=(hbm,) * 17,
         scratch_shapes=list(scratch.values()),
         compiler_params=pltpu.CompilerParams(
-            collective_id=1, has_side_effects=True, vmem_limit_bytes=63 << 20
+            collective_id=1, has_side_effects=True, vmem_limit_bytes=67043328
         ),
         name="block",
     )(tokens, cot, q, k, v, o, up, down, seg, gain1, bias1, gain2, bias2, taps, rate, inb, outc, skip[None])
@@ -1201,11 +1259,15 @@
     for i in (2, 3, 4, 5):
         final[i] = sds((feats,), f32)
     final[16] = sds((chans,), f32)
+    held = [pltpu.VMEM(a.shape, a.dtype) for a in outs]
+    flat = [pltpu.VMEM(b.shape, b.dtype) for a, b in zip(outs, final) if a.shape != b.shape]
+    count = len(outs)
     return pl.pallas_call(
-        hand_over,
+        functools.partial(hand_over, count),
         out_shape=tuple(final),
-        in_specs=[vm] * 17,
-        out_specs=(vm,) * 17,
+        in_specs=[hbm] * count,
+        out_specs=(hbm,) * count,
+        scratch_shapes=held + flat + [pltpu.SemaphoreType.DMA((count,))] * 2,
         name="hand_over",
     )(*outs)
 

time: 136 us -> 129 us (0.949)
  Pallas kernels: 135 us -> 128 us
    pallas_call x1, Pallas kernels: 132 us -> 125 us  [whole_block(): pl.pallas_call(functools.partial(block_kernel, axes, INPUTS + OUTPUTS + t...]
where the time goes in v6:
time: 129 us
  Pallas kernels  128 us (99%)
    pallas_call x1, Pallas kernels, whole_block(): pl.pallas_call(functools.partial(block_kernel, axes, INPUTS + OUTPUTS + t...  125 us
    pallas_call x1, Pallas kernels, whole_block(): pl.pallas_call(functools.partial(hand_over, count), out_shape=tuple(final...  2.83 us

profile of v6, /device:TPU:0, one launch (start us, length us, event | category | flops | bytes accessed | tf_op | source)
XLA Modules:
  0.0 128.5 jit_solution(14095385802988314935)
XLA Ops:
  0.7 124.9 %block.1 = (bf16[256,768]{1,0:T(8,128)(2,1)}, f32[256,768]{1,0:T(8,128)}, f32[1,768]{1,0:T(1,128)}, f32[1,768]{1,0:T(1,128)}, f32[1,768]{1,0:T(1,128)}, /*index=...) custom-call(bf16[256,768]{1,0:T(8,128)(2,1)} %refs_0_.1, ...), custom_call_target="tpu_custom_call" | custom-call | tf_op jit(solution)/shard_map/block/pallas_call | solution.py:1247
  125.5 2.8 %hand_over.1 = (bf16[256,768]{1,0:T(8,128)(2,1)}, f32[256,768]{1,0:T(8,128)}, f32[768]{0:T(1024)}, f32[768]{0:T(1024)}, f32[768]{0:T(1024)}, /*index=5*/f32[768]...) custom-call(bf16[256,768]{1,0:T(8,128)(2,1)} %get-tuple-element.34.r, ...), custom_call_target="tpu_custom_call" | custom-call | tf_op jit(solution)/shard_map/hand_over/pallas_call | solution.py:1265

commit v7 on v6

--- a/solution.py
+++ b/solution.py
@@ -776,7 +776,7 @@
 
 
 SKIP_AT, PARAM_ROWS = 192, 208
-UNROLL = 24
+UNROLL, UNROLL_BACK = 24, 48
 
 
 class Names:
@@ -922,11 +922,11 @@
     load_tok.wait()
     hat1, _ = row_norm(r.tok[...].astype(f32))
     r.xn1[pc.me] = (hat1 * gain1 + bias1).astype(bf16).T
+    meet()
+    xn1_g.start()
     for copy in four:
         copy.wait()
     r.wqkvo[pc.dp] = jnp.concatenate([r.four[i] for i in range(4)], axis=1)
-    meet()
-    xn1_g.start()
     z_qkvo.start()
     load_cot.wait()
     r.cots[pc.me] = r.cot[...].T
@@ -1025,8 +1025,8 @@
     xn2_g.arrive(9, 10)
     chunk(pc.pd)
     red_x2.give(0)
+    red_x2.far()
     red_x2.pair(3)
-    red_x2.far()
     units = r.act.shape[1]
     grad_up = jnp.zeros((feats, units), f32)
     for s in range(group):
@@ -1120,12 +1120,15 @@
 
     def start_back():
         theirs, mine = red_x1.theirs, red_x1.mine
-        chunk_back(theirs[0])
-        red_x1.give(0)
-        chunk_back(mine[0])
-        chunk_back(theirs[1])
-        red_x1.give(1)
-        chunk_back(mine[1])
+        for k in range(3):
+            chunk_back(theirs[k])
+            red_x1.give(k)
+            chunk_back(mine[k])
+        red_x1.far()
+        chunk_back(theirs[3])
+        red_x1.give(3)
+        red_x1.side()
+        chunk_back(mine[3])
         grad_kv = jnp.zeros((feats, 2 * chans), f32)
         for s in range(group):
             grad_kv = grad_kv + mm(r.xn1[s], grads(s)[chans:], NT)
@@ -1138,18 +1141,10 @@
         r.n1[pc.me, 0:1, :] += row_of(grad_kv * w_wide[:, chans : 3 * chans])
         r.n1[pc.me, 1:2, :] = row_of(w_wide[:, 0 : 3 * chans] * token_sums[0:1])
         spread1.start()
-        red_x1.far()
-        chunk_back(theirs[2])
-        red_x1.give(2)
-        chunk_back(mine[2])
-        chunk_back(theirs[3])
-        red_x1.give(3)
-        red_x1.side()
-        chunk_back(mine[3])
 
     run_beside(
         mixer_backward(
-            UNROLL, r.gmix_in, r.qkv, r.core, r.s, r.f, r.urev, r.pp, r.kern, *mixer,
+            UNROLL_BACK, r.gmix_in, r.qkv, r.core, r.s, r.f, r.urev, r.pp, r.kern, *mixer,
             r.dqkv, r.dsw, r.drate, r.dinb, r.doutc, r.dskip,
             r.t0, r.t1, r.t2, r.t3, r.w0, r.w1, r.w2, r.w3, r.dur, r.w2, r.w4, r.w5, r.w6, r.gr, r.red,
         ),

time: 129 us -> 129 us (level)
  no operation moved by 1% of the time
where the time goes in v7:
time: 129 us
  Pallas kernels  128 us (99%)
    pallas_call x1, Pallas kernels, whole_block(): pl.pallas_call(functools.partial(block_kernel, axes, INPUTS + OUTPUTS + t...  125 us
    pallas_call x1, Pallas kernels, whole_block(): pl.pallas_call(functools.partial(hand_over, count), out_shape=tuple(final...  2.83 us

profile of v7, /device:TPU:0, one launch (start us, length us, event | category | flops | bytes accessed | tf_op | source)
XLA Modules:
  0.0 128.8 jit_solution(13504523038700044154)
XLA Ops:
  0.7 125.1 %block.1 = (bf16[256,768]{1,0:T(8,128)(2,1)}, f32[256,768]{1,0:T(8,128)}, f32[1,768]{1,0:T(1,128)}, f32[1,768]{1,0:T(1,128)}, f32[1,768]{1,0:T(1,128)}, /*index=...) custom-call(bf16[256,768]{1,0:T(8,128)(2,1)} %refs_0_.1, ...), custom_call_target="tpu_custom_call" | custom-call | tf_op jit(solution)/shard_map/block/pallas_call | solution.py:1242
  125.8 2.8 %hand_over.1 = (bf16[256,768]{1,0:T(8,128)(2,1)}, f32[256,768]{1,0:T(8,128)}, f32[768]{0:T(1024)}, f32[768]{0:T(1024)}, f32[768]{0:T(1024)}, /*index=5*/f32[768]...) custom-call(bf16[256,768]{1,0:T(8,128)(2,1)} %get-tuple-element.34.r, ...), custom_call_target="tpu_custom_call" | custom-call | tf_op jit(solution)/shard_map/hand_over/pallas_call | solution.py:1260
